TPU v7x, 512 devices: a whole 4x8x8 slice. The times are simulated.
512 devices in a mesh: gx: 64 (over y, z), gy: 2 (over core), ma: 4 (over x).
Axes of the slice: x: 4, y: 8, z: 8, core: 2. Of those that a mesh axis runs over, the one named last changes fastest.
Arguments:
- ensemble: float32 [80, 2, 256, 256], P('ma', None, 'gx', 'gy'), may hold values from -6 to 6
- wind_field: float32 [2, 2, 256, 256], P(None, None, 'gx', 'gy'), may hold values from -0.45 to 0.45
- obs_value: float32 [4, 1024], replicated, may hold values from -6 to 6
- obs_var: float32 [4, 1024], replicated, may hold values from 2 to 20
- obs_region: int32 [4, 1024], replicated, may hold values from 0 to 127, as said below
- obs_cell: int32 [4, 1024], replicated, may hold values from 0 to 1023
- block_order: int32 [4], replicated, may hold values from 0 to 3, each once
- localization: float32 [64, 2, 4, 1024], P('gx', 'gy'), may hold values from 0 to 1
Outputs:
- analysis: float32 [80, 2, 256, 256], P('ma', None, 'gx', 'gy')
Inputs may be any that keep to these rules, and one draw needn't show every extreme that they name: `obs_region`: region index = first-dimension region * 2 + second-dimension region.
All inputs are finite; a program needn't handle non-finite values.
Results may differ from a plain program's by a relative error of at most 0.0001.
Values sent between devices are 32-bit elements; how exact they have to be, the bound alone decides.
No kernel may reach another device: no remote copies, remote signals or barrier semaphores. Data moves between devices by JAX's collectives and lax.ppermute only.
A program may use at most 64 MiB of HBM per device.

v0:
```python
import jax
import jax.numpy as jnp
from jax import lax
from jax.sharding import PartitionSpec as P

STEPS = 2
BLOCKS = 4


KAPPA = 0.025


def extended(block, sides, width):
    for axis, dim in sides:
        count = lax.axis_size(axis)
        forward = [(i, i + 1) for i in range(count - 1)]
        forward.append((count - 1, 0))
        backward = [(target, source) for source, target in forward]
        low = lax.ppermute(
            lax.slice_in_dim(block, block.shape[dim] - width, None, axis=dim), axis, forward
        )
        high = lax.ppermute(lax.slice_in_dim(block, 0, width, axis=dim), axis, backward)
        block = jnp.concatenate([low, block, high], axis=dim)
    return block


def advect(tracer, wind_field):
    padded = extended(tracer, (("gx", 2), ("gy", 3)), 1)
    east_wind = wind_field[0][None]
    north_wind = wind_field[1][None]
    middle = padded[:, :, 1:-1, 1:-1]
    west_side = padded[:, :, :-2, 1:-1]
    east_side = padded[:, :, 2:, 1:-1]
    south_side = padded[:, :, 1:-1, :-2]
    north_side = padded[:, :, 1:-1, 2:]
    return (
        middle
        - jnp.maximum(east_wind, 0.0) * (middle - west_side)
        - jnp.minimum(east_wind, 0.0) * (east_side - middle)
        - jnp.maximum(north_wind, 0.0) * (middle - south_side)
        - jnp.minimum(north_wind, 0.0) * (north_side - middle)
        + KAPPA * (east_side + west_side + north_side + south_side - 4.0 * middle)
    )


def mixing_matrix(prior_obs, observed, error_var, taper, ensemble_size):
    denom = ensemble_size - 1.0
    obs_mean = jnp.mean(prior_obs, axis=0)
    anomaly = prior_obs - obs_mean
    variance = jnp.sum(anomaly * anomaly, axis=0) / denom
    total_var = variance + error_var
    innovation = observed - obs_mean
    shrink = 1.0 / (1.0 + jnp.sqrt(error_var / total_var))
    gain_mean = taper * innovation / (denom * total_var)
    gain_spread = taper * shrink / (denom * total_var)
    shift_terms = jnp.dot(anomaly, gain_mean, precision=lax.Precision.HIGHEST)
    weighted = anomaly * gain_spread
    return shift_terms[:, None] - jnp.dot(weighted, anomaly.T, precision=lax.Precision.HIGHEST)


def local(
    ensemble, wind_field, obs_value, obs_var, obs_region, obs_cell, block_order, localization
):
    state = ensemble
    for step_index in range(STEPS):
        state = advect(state, wind_field)
    members_dev, levels, cells_x, cells_y = state.shape
    ensemble_size = members_dev * lax.axis_size("ma")
    own_region = lax.axis_index("gx") * lax.axis_size("gy") + lax.axis_index("gy")
    member_part = lax.axis_index("ma")
    stacked = state.reshape(members_dev, -1)
    for position in range(BLOCKS):
        block_id = block_order[position]
        gathered = lax.all_gather(stacked, "ma", axis=0, tiled=True)
        picked = jnp.take(gathered, obs_cell[block_id], axis=1)
        is_held = obs_region[block_id] == own_region
        prior_obs = lax.psum(jnp.where(is_held[None], picked, 0.0), ("gx", "gy"))
        mixing = mixing_matrix(
            prior_obs,
            obs_value[block_id],
            obs_var[block_id],
            localization[0, 0, block_id],
            ensemble_size,
        )
        center = jnp.mean(gathered, axis=0)
        own_columns = lax.dynamic_slice_in_dim(mixing, member_part * members_dev, members_dev, 1)
        stacked = stacked + jnp.dot(
            own_columns.T, gathered - center, precision=lax.Precision.HIGHEST
        )
    return stacked.reshape(state.shape)


def solution(mesh):
    in_specs = (
        P("ma", None, "gx", "gy"),
        P(None, None, "gx", "gy"),
        P(),
        P(),
        P(),
        P(),
        P(),
        P("gx", "gy", None, None),
    )
    out_specs = P("ma", None, "gx", "gy")
    return jax.shard_map(local, mesh=mesh, in_specs=in_specs, out_specs=out_specs, check_vma=False)
```

profile of v0, /device:TPU:1, one launch (start us, length us, event | category | flops | bytes accessed | tf_op | source)
XLA Modules:
  0.0 904.6 jit_solution(8745651643520247778)
XLA Ops:
  7.6 14.4 %collective-permute-start.1 = (f32[20,2,1,128]{3,2,1,0:T(1,128)S(1)}, f32[20,2,1,128]{3,2,1,0:T(1,128)S(1)}, u32[]{:S(2)}, u32[]{:S(2)}) collective-permute-start(f32[20,2,1,128]{3,2,1,0:T(1,128)S(1)} %get-tuple-element.29), channel_id=1, source_target_pairs={{8,0},{16,8},{24,16},{32,24},{40,32},{48,40},{56,48},{64,56},{72,6... | collective-permute-start | bytes 61448 | tf_op jit(solution)/shard_map/ppermute | solution.py:22
  22.0 2.1 collective-permute-start
  33.3 2.9 collective-permute-start.3
  36.2 1.9 collective-permute-start.2
  39.9 7.0 collective-permute-start.5
  46.9 1.9 collective-permute-start.4
  48.9 5.9 collective-permute-done.4
  54.9 3.5 collective-permute-start.7
  58.4 1.9 collective-permute-start.6
  62.2 10.5 %all-gather = f32[4,20,1024]{2,1,0:T(8,128)S(1)} all-gather(f32[1,20,1024]{2,1,0:T(8,128)S(1)} %reshape.117), channel_id=1, replica_groups=mesh['gx'=64,'gy'=2,'ma'=4] {'ma'}, dimensions={0}, use_global_device_ids=true | all-gather | bytes 409600 | tf_op jit(solution)/shard_map/all_gather | solution.py:74
  73.0 2.8 gather_fusion
  77.0 185.7 %all-reduce.5.cloned.1.call-done = f32[80,1024]{0,1:T(8,128)} async-done(((f32[80,1024]{0,1:T(8,128)}), f32[80,1024]{0,1:T(8,128)}) %all-reduce.5.cloned.1.call-update) | async-done | bytes 327696 | tf_op jit(solution)/shard_map/psum | solution.py:77
  267.1 10.4 %all-gather.1 = f32[4,20,1024]{2,1,0:T(8,128)S(1)} all-gather(f32[1,20,1024]{2,1,0:T(8,128)S(1)} %bitcast.72), channel_id=1, replica_groups=mesh['gx'=64,'gy'=2,'ma'=4] {'ma'}, dimensions={0}, use_global_device_ids=true | all-gather | bytes 409600 | tf_op jit(solution)/shard_map/all_gather | solution.py:74
  277.8 2.8 gather_fusion.1
  281.9 191.6 %all-reduce.7.cloned.1.call-done = f32[80,1024]{0,1:T(8,128)} async-done(((f32[80,1024]{0,1:T(8,128)}), f32[80,1024]{0,1:T(8,128)}) %all-reduce.7.cloned.1.call-update) | async-done | bytes 327696 | tf_op jit(solution)/shard_map/psum | solution.py:77
  475.3 1.5 fusion.4
  477.6 10.4 %all-gather.2 = f32[4,20,1024]{2,1,0:T(8,128)S(1)} all-gather(f32[1,20,1024]{2,1,0:T(8,128)S(1)} %bitcast.73), channel_id=1, replica_groups=mesh['gx'=64,'gy'=2,'ma'=4] {'ma'}, dimensions={0}, use_global_device_ids=true | all-gather | bytes 409600 | tf_op jit(solution)/shard_map/all_gather | solution.py:74
  488.3 2.8 gather_fusion.2
  492.5 190.9 %all-reduce.9.cloned.1.call-done = f32[80,1024]{0,1:T(8,128)} async-done(((f32[80,1024]{0,1:T(8,128)}), f32[80,1024]{0,1:T(8,128)}) %all-reduce.9.cloned.1.call-update) | async-done | bytes 327696 | tf_op jit(solution)/shard_map/psum | solution.py:77
  685.2 1.5 fusion.2
  687.5 10.4 %all-gather.3 = f32[4,20,1024]{2,1,0:T(8,128)S(1)} all-gather(f32[1,20,1024]{2,1,0:T(8,128)S(1)} %bitcast.71), channel_id=1, replica_groups=mesh['gx'=64,'gy'=2,'ma'=4] {'ma'}, dimensions={0}, use_global_device_ids=true | all-gather | bytes 409600 | tf_op jit(solution)/shard_map/all_gather | solution.py:74
  698.2 2.8 gather_fusion.3
  702.2 191.1 %all-reduce.11.cloned.1.call-done = f32[80,1024]{0,1:T(8,128)} async-done(((f32[80,1024]{0,1:T(8,128)}), f32[80,1024]{0,1:T(8,128)}) %all-reduce.11.cloned.1.call-update) | async-done | bytes 327696 | tf_op jit(solution)/shard_map/psum | solution.py:77
  895.1 1.5 fusion
  (114 shorter events, 25.0 us)
Async XLA Ops:
  6.5 256.2 %all-reduce.5.cloned.1.call-start = ((), (), s32[]{:S(2)}) async-start(), calls=%async_computation | async-start | bytes 1048576 | tf_op jit(solution)/shard_map/psum | solution.py:77
  7.5 16.5 %copy-start.11 = (s32[4]{0:T(128)S(1)}, s32[4]{0:T(128)}, u32[]{:S(2)}) copy-start(s32[4]{0:T(128)} %param.16) | copy-start | bytes 52
  7.6 25.6 %collective-permute-start.1 = (f32[20,2,1,128]{3,2,1,0:T(1,128)S(1)}, f32[20,2,1,128]{3,2,1,0:T(1,128)S(1)}, u32[]{:S(2)}, u32[]{:S(2)}) collective-permute-start(f32[20,2,1,128]{3,2,1,0:T(1,128)S(1)} %get-tuple-element.29), channel_id=1, source_target_pairs={{8,0},{16,8},{24,16},{32,24},{40,32},{48,40},{56,48},{64,56},{72,6... | collective-permute-start | bytes 61448 | tf_op jit(solution)/shard_map/ppermute | solution.py:22
  22.0 10.4 %copy-start.7 = (s32[4,1024]{1,0:T(4,128)S(1)}, s32[4,1024]{1,0:T(4,128)}, u32[]{:S(2)}) copy-start(s32[4,1024]{1,0:T(4,128)} %param.15) | copy-start | bytes 49156
  22.0 11.1 %copy-start.4 = (f32[20,2,4,128]{3,2,1,0:T(4,128)S(1)}, f32[20,2,4,128]{3,2,1,0:T(4,128)}, u32[]{:S(2)}) copy-start(f32[20,2,4,128]{3,2,1,0:T(4,128)} %param.10) | copy-start | bytes 245764
  22.0 11.1 %collective-permute-start = (f32[20,2,1,128]{3,2,1,0:T(1,128)S(1)}, f32[20,2,1,128]{3,2,1,0:T(1,128)S(1)}, u32[]{:S(2)}, u32[]{:S(2)}) collective-permute-start(f32[20,2,1,128]{3,2,1,0:T(1,128)S(1)} %get-tuple-element.28), channel_id=1, source_target_pairs={{0,8},{8,16},{16,24},{24,32},{32,40},{40,48},{48,56},{56,64},{64,7... | collective-permute-start | bytes 61448 | tf_op jit(solution)/shard_map/ppermute | solution.py:19
  32.4 0.7 copy-start.10
  33.3 4.8 collective-permute-start.3
  36.2 3.3 collective-permute-start.2
  39.8 9.0 copy-start.8
  39.9 8.9 collective-permute-start.5
  46.9 7.8 collective-permute-start.4
  54.8 5.6 copy-start.9
  54.9 5.5 collective-permute-start.7
  58.4 3.3 collective-permute-start.6
  77.0 396.5 %all-reduce.7.cloned.1.call-start = ((), (), s32[]{:S(2)}) async-start(), calls=%async_computation.1 | async-start | bytes 1048576 | tf_op jit(solution)/shard_map/psum | solution.py:77
  262.7 1.3 copy-start
  264.0 0.7 copy-start.5
  264.1 0.7 copy-start.6
  281.8 401.6 %all-reduce.9.cloned.1.call-start = ((), (), s32[]{:S(2)}) async-start(), calls=%async_computation.2 | async-start | bytes 1048576 | tf_op jit(solution)/shard_map/psum | solution.py:77
  473.5 1.3 copy-start.1
  492.3 401.1 %all-reduce.11.cloned.1.call-start = ((), (), s32[]{:S(2)}) async-start(), calls=%async_computation.3 | async-start | bytes 1048576 | tf_op jit(solution)/shard_map/psum | solution.py:77
  683.4 1.3 copy-start.2
  893.4 1.3 copy-start.3
Sparse Core Ops, SparseCore 0:
  77.1 185.5 all-reduce.4
  282.0 191.4 all-reduce.6
  492.4 190.9 all-reduce.8
  702.3 190.9 all-reduce.10
where the time goes:
time: 906 us; the launch traced here: 905 us
  waiting for transfers between devices  768 us (85%)
  blocking collectives  41.8 us (5%)
  starting transfers between devices  35.8 us (4%)
  between operations  21.4 us (2%)
  local copies, waits for them, and re-layouts  15.9 us (2%)
  other arithmetic  12.7 us (1%)
    psum x4, waiting for transfers between devices, local(): prior_obs = lax.psum(jnp.where(is_held[None], picked, 0.0), ('gx', 'gy'))  759 us
    all_gather x4, blocking collectives, local(): gathered = lax.all_gather(stacked, 'ma', axis=0, tiled=True)  41.8 us
    ppermute x4, starting transfers between devices, extended(): lax.ppermute(lax.slice_in_dim(block, 0, width, axis=dim), axis, backward)  27.7 us
  transfers between devices with their start and end apart: 12, of which 7 were waited for; matrix products, arithmetic and copies ran while one was open for 0% of the time, Pallas kernels for 0%

commit v1 on v0

v1 whole, which is shorter than its diff:
```python
import jax
import jax.numpy as jnp
from jax import lax
from jax.experimental import pallas as pl
from jax.experimental.pallas import tpu as pltpu
from jax.sharding import PartitionSpec as P

MEMBERS = 80
OWN = 20
BLOCKS = 4
OBS = 1024
CELLS = 1024
GX = 64
MA = 4
LANES = 128
GROUPS = OBS // LANES
KAPPA = 0.025
CHUNK = 5
HALF = OWN * 2 * GROUPS
ROWS_O = 256
F32 = jnp.float32
BF16 = jnp.bfloat16
VMEM = pl.BlockSpec(memory_space=pltpu.VMEM)
SMEM = pl.BlockSpec(memory_space=pltpu.SMEM)


def split(value):
    high = value.astype(BF16)
    return high, (value - high.astype(F32)).astype(BF16)


def dot_nn(a, b):
    return lax.dot_general(a, b, (((1,), (0,)), ((), ())), preferred_element_type=F32)


def dot_nt(a, b):
    return lax.dot_general(a, b, (((1,), (1,)), ((), ())), preferred_element_type=F32)


def block_row(ref, b, columns):
    row = ref[pl.ds(0, 1), columns]
    for i in range(1, BLOCKS):
        row = jnp.where(b == i, ref[pl.ds(i, 1), columns], row)
    return row


def advect_kernel(order, own_ref, other_ref, cell_ref, region_ref, state_ref, picked_ref, work):
    lane = lax.broadcasted_iota(jnp.int32, (8, LANES), 1)
    first, last = lane == 0, lane == LANES - 1

    def step(q, beside, u, v):
        west, east = pltpu.roll(q, 1, 0), pltpu.roll(q, 7, 0)
        south = jnp.where(first, pltpu.roll(beside, 1, 1), pltpu.roll(q, 1, 1))
        north = jnp.where(last, pltpu.roll(beside, LANES - 1, 1), pltpu.roll(q, LANES - 1, 1))
        return (
            q
            - jnp.maximum(u, 0.0) * (q - west)
            - jnp.minimum(u, 0.0) * (east - q)
            - jnp.maximum(v, 0.0) * (q - south)
            - jnp.minimum(v, 0.0) * (north - q)
            + KAPPA * (east + west + north + south - 4.0 * q)
        )

    work[pl.ds(160, 32), :] = jnp.zeros((32, LANES), F32)
    for level in range(2):
        row = (OWN * 2 + level) * 8
        u, v = own_ref[pl.ds(row, 8), :], own_ref[pl.ds(row + 32 - 16, 8), :]
        u_o, v_o = other_ref[pl.ds(row, 8), :], other_ref[pl.ds(row + 32 - 16, 8), :]
        for m in range(OWN):
            at = (m * 2 + level) * 8
            q, q_o = own_ref[pl.ds(at, 8), :], other_ref[pl.ds(at, 8), :]
            once, once_o = step(q, q_o, u, v), step(q_o, q, u_o, v_o)
            twice = step(once, once_o, u, v)
            work[pl.ds(m * 8 + level * 4, 4), :] = twice[2:6]
            state_ref[pl.ds(m * 8 + level * 4, 4), :] = twice[2:6]

    own_region = lax.axis_index("gx") * 2 + lax.axis_index("gy")
    for k in range(BLOCKS):
        b = order[k]
        for g in range(GROUPS):
            columns = pl.ds(g * LANES, LANES)
            cell, region = block_row(cell_ref, b, columns), block_row(region_ref, b, columns)
            y = jnp.broadcast_to(jnp.bitwise_and(cell, LANES - 1), (24, LANES))
            part = jnp.where(region == own_region, jnp.right_shift(cell, 7), -1)
            part = jnp.broadcast_to(part, (24, LANES))
            total = jnp.zeros((24, LANES), F32)
            for c in range(8):
                source = work[pl.ds(c, 24, stride=8), :]
                found = jnp.take_along_axis(source, y, axis=1)
                total = jnp.where(part == c, found, total)
            at = (k // 2) * HALF + (k % 2) * GROUPS + g
            picked_ref[pl.ds(at, OWN, stride=16), :] = total[:OWN]


def owner_kernel(parts_ref, out_ref):
    total = parts_ref[pl.ds(0, 40), :]
    for i in range(1, 16):
        total = total + parts_ref[pl.ds(i * 40, 40), :]
    part = total[0:CHUNK]
    for i in range(1, 8):
        part = part + total[i * CHUNK : (i + 1) * CHUNK]
    eight = jnp.concatenate([part] * 8, axis=0)
    for i in range(GX * MA // 8):
        out_ref[pl.ds(i * 40, 40), :] = eight


def filter_kernel(
    order,
    prior_ref,
    prior_o_ref,
    taper_ref,
    taper_o_ref,
    taper_own_ref,
    value_ref,
    var_ref,
    region_ref,
    gathered_ref,
    state_ref,
    out_ref,
    xt,
    tapers,
    onehots,
    b_high,
    b_both,
    increments,
):
    gy = lax.axis_index("gy")
    denom = MEMBERS - 1.0

    def load_half(ref, half):
        for g in range(16):
            block = ref[pl.ds(g, MEMBERS, stride=16), :]
            mean = jnp.mean(block, axis=0, keepdims=True)
            full = jnp.concatenate(
                [block - mean, mean, jnp.zeros((LANES - MEMBERS - 1, LANES), F32)], axis=0
            )
            xt[pl.ds((half * 16 + g) * LANES, LANES), :] = full.T

    @pl.when(gy == 0)
    def _():
        load_half(prior_ref, 0)
        load_half(prior_o_ref, 1)

    @pl.when(gy == 1)
    def _():
        load_half(prior_o_ref, 0)
        load_half(prior_ref, 1)

    for k in range(BLOCKS - 1):
        b = order[k]
        for g in range(GROUPS):
            for i, ref in enumerate((taper_ref, taper_o_ref)):
                high, low = split(ref.at[pl.ds(pl.multiple_of(b * (GX * 8), GX * 8), GX * 8), :][pl.ds(g, GX, stride=8), :])
                tapers[k, pl.ds(i * GX, GX), pl.ds(g * LANES, LANES)] = high
                tapers[k, pl.ds(LANES + i * GX, GX), pl.ds(g * LANES, LANES)] = low

    rows = lax.broadcasted_iota(jnp.int32, (LANES, LANES), 0)
    for k in range(1, BLOCKS):
        b = order[k]
        for g in range(GROUPS):
            region = block_row(region_ref, b, pl.ds(g * LANES, LANES))
            place = jnp.where(
                jnp.bitwise_and(region, 1) == gy, 0, GX
            ) + jnp.right_shift(region, 1)
            hot = (rows == jnp.broadcast_to(place, (LANES, LANES))).astype(F32).T.astype(BF16)
            at = pl.ds(((k - 1) * GROUPS + g) * LANES, LANES)
            onehots[at, pl.ds(0, LANES)] = hot
            onehots[at, pl.ds(LANES, LANES)] = hot

    lane = lax.broadcasted_iota(jnp.int32, (ROWS_O, LANES), 1)
    member_row = lax.broadcasted_iota(jnp.int32, (LANES, OBS), 0)
    increments[...] = jnp.zeros((LANES, LANES), F32)
    for k in range(BLOCKS):
        b = order[k]
        now = jnp.concatenate(
            [xt[pl.ds((k * GROUPS + g) * LANES, LANES), :].T for g in range(GROUPS)], axis=1
        )
        anomaly = jnp.where(member_row < MEMBERS, now, 0.0)
        mean = now[MEMBERS : MEMBERS + 1]
        variance = jnp.sum(anomaly * anomaly, axis=0, keepdims=True) / denom
        error_var = block_row(var_ref, b, pl.ds(0, OBS))
        total_var = variance + error_var
        shrink = 1.0 / (1.0 + jnp.sqrt(error_var / total_var))
        scale = 1.0 / (denom * total_var)
        gain_mean = (block_row(value_ref, b, pl.ds(0, OBS)) - mean) * scale
        gain = jnp.where(member_row == MEMBERS, gain_mean, -(shrink * scale) * anomaly)
        gain_high, gain_low = split(gain)

        tapered_high, tapered_low = split(anomaly * block_row(taper_own_ref, b, pl.ds(0, OBS)))
        mixing = (
            dot_nt(gain_high, tapered_high)
            + dot_nt(gain_low, tapered_high)
            + dot_nt(gain_high, tapered_low)
        )
        e = increments[...]
        increments[...] = e + mixing + jnp.dot(
            mixing, e, precision=lax.Precision.HIGHEST, preferred_element_type=F32
        )

        if k == BLOCKS - 1:
            continue
        a_high, a_low = split(anomaly)
        left = jnp.concatenate([a_high[:MEMBERS], a_high[:MEMBERS], a_low[:MEMBERS], jnp.zeros((16, OBS), BF16)], axis=0)
        b_high[...] = gain_high.astype(F32).T.astype(BF16)
        b_both[:, pl.ds(0, LANES)] = b_high[...]
        b_both[:, pl.ds(LANES, LANES)] = gain_low.astype(F32).T.astype(BF16)

        def chunk(i, carry, k=k, left=left):
            at = pl.multiple_of((k + 1) * OBS + i * ROWS_O, ROWS_O)
            x = xt[pl.ds(at, ROWS_O), :]
            clean = jnp.where(lane < MEMBERS, x, 0.0)
            high = clean.astype(BF16).astype(F32)
            low = (clean - high)
            low_rolled = pltpu.roll(low, MEMBERS, 1)
            first = jnp.where(lane < MEMBERS, high, low_rolled)
            second = jnp.where(lane < 2 * MEMBERS - LANES, low_rolled, pltpu.roll(high, 2 * MEMBERS - LANES, 1))
            second = jnp.where(lane < 3 * MEMBERS - LANES, second, 0.0)
            query = jnp.concatenate([first, second], axis=1).astype(BF16)
            hot = onehots[pl.ds(pl.multiple_of(at - OBS, ROWS_O), ROWS_O), :]
            weight = dot_nn(query, left) * dot_nn(hot, tapers[k])
            w_high, w_low = split(weight)
            both = dot_nn(w_high, b_both[...])
            xt[pl.ds(at, ROWS_O), :] = (
                x + both[:, :LANES] + both[:, LANES:] + dot_nn(w_low, b_high[...])
            )
            return carry

        lax.fori_loop(0, (BLOCKS - 1 - k) * OBS // ROWS_O, chunk, 0)

    q = lax.axis_index("ma")
    e = increments[...]
    total = e + e[MEMBERS : MEMBERS + 1]
    pick_row = lax.broadcasted_iota(jnp.int32, (24, LANES), 0)
    pick_lane = lax.broadcasted_iota(jnp.int32, (24, LANES), 1)
    chosen = jnp.where((pick_lane == pick_row + q * OWN) & (pick_row < OWN), 1.0, 0.0)
    transform = jnp.dot(chosen, total, precision=lax.Precision.HIGHEST, preferred_element_type=F32)
    tiles = []
    for c in range(8):
        tile = gathered_ref[pl.ds(c, MEMBERS, stride=8), :]
        tiles.append(tile - jnp.mean(tile, axis=0, keepdims=True))
    centered = jnp.concatenate(
        [jnp.concatenate(tiles, axis=1), jnp.zeros((LANES - MEMBERS, CELLS), F32)], axis=0
    )
    update = jnp.dot(transform, centered, precision=lax.Precision.HIGHEST, preferred_element_type=F32)
    for c in range(8):
        at = pl.ds(c, OWN, stride=8)
        out_ref[at, :] = state_ref[at, :] + update[:OWN, c * LANES : (c + 1) * LANES]


def other_core(x):
    return lax.ppermute(x, "gy", [(0, 1), (1, 0)])


def local(
    ensemble, wind_field, obs_value, obs_var, obs_region, obs_cell, block_order, localization
):
    q = lax.axis_index("ma")
    both = jnp.concatenate([ensemble, wind_field], axis=0)
    forward = [(i, (i + 1) % GX) for i in range(GX)]
    backward = [(i, (i - 1) % GX) for i in range(GX)]
    low = lax.ppermute(both[:, :, 2:], "gx", forward)
    high = lax.ppermute(both[:, :, :2], "gx", backward)
    own = jnp.concatenate([low, both, high], axis=2).reshape(-1, LANES)
    beside = other_core(own)

    taper_own = localization.reshape(BLOCKS, OBS)
    taper_send = lax.dynamic_slice_in_dim(taper_own, q, 1, 0)
    taper_send = jnp.broadcast_to(taper_send[None], (MA * GX, 1, OBS))
    tapers = lax.all_to_all(taper_send, ("ma", "gx"), 0, 0, tiled=True).reshape(-1, LANES)
    tapers_beside = other_core(tapers)

    state, picked = pl.pallas_call(
        advect_kernel,
        out_shape=(
            jax.ShapeDtypeStruct((OWN * 8, LANES), F32),
            jax.ShapeDtypeStruct((2 * HALF, LANES), F32),
        ),
        in_specs=[SMEM, VMEM, VMEM, VMEM, VMEM],
        out_specs=(VMEM, VMEM),
        scratch_shapes=[pltpu.VMEM((24 * 8, LANES), F32)],
        cost_estimate=pl.CostEstimate(flops=10_000_000, bytes_accessed=1_000_000, transcendentals=0),
        name="advect",
    )(block_order, own, beside, obs_cell, obs_region)

    parts = lax.all_to_all(picked.reshape(2 * GX, 1, CHUNK * LANES), ("gy", "gx"), 0, 0, tiled=True)
    gathered = lax.all_to_all(
        jnp.broadcast_to(state[None], (MA, OWN * 8, LANES)), "ma", 0, 0, tiled=True
    ).reshape(-1, LANES)
    owned = pl.pallas_call(
        owner_kernel,
        out_shape=jax.ShapeDtypeStruct((MA * GX * CHUNK, LANES), F32),
        in_specs=[VMEM],
        out_specs=VMEM,
        name="owner",
    )(parts.reshape(-1, LANES))
    priors = lax.all_to_all(
        owned.reshape(MA * GX, 1, CHUNK * LANES), ("ma", "gx"), 0, 0, tiled=True
    ).reshape(-1, LANES)
    priors_beside = other_core(priors)

    out = pl.pallas_call(
        filter_kernel,
        out_shape=jax.ShapeDtypeStruct((OWN * 8, LANES), F32),
        in_specs=[SMEM] + [VMEM] * 10,
        out_specs=VMEM,
        scratch_shapes=[
            pltpu.VMEM((BLOCKS * OBS, LANES), F32),
            pltpu.VMEM((BLOCKS - 1, 2 * LANES, OBS), BF16),
            pltpu.VMEM(((BLOCKS - 1) * OBS, 2 * LANES), BF16),
            pltpu.VMEM((OBS, LANES), BF16),
            pltpu.VMEM((OBS, 2 * LANES), BF16),
            pltpu.VMEM((LANES, LANES), F32),
        ],
        cost_estimate=pl.CostEstimate(flops=3_000_000_000, bytes_accessed=4_000_000, transcendentals=0),
        name="filter",
    )(
        block_order,
        priors,
        priors_beside,
        tapers,
        tapers_beside,
        taper_own,
        obs_value,
        obs_var,
        obs_region,
        gathered,
        state,
    )
    return out.reshape(ensemble.shape)


def solution(mesh):
    in_specs = (
        P("ma", None, "gx", "gy"),
        P(None, None, "gx", "gy"),
        P(),
        P(),
        P(),
        P(),
        P(),
        P("gx", "gy", None, None),
    )
    out_specs = P("ma", None, "gx", "gy")
    return jax.shard_map(local, mesh=mesh, in_specs=in_specs, out_specs=out_specs, check_vma=False)
```

time: 906 us -> 172 us (0.19)
  waiting for transfers between devices: 768 us -> 61.5 us
  Pallas kernels: 0 us -> 33.9 us
  blocking collectives: 41.8 us -> 10.6 us
  starting transfers between devices: 35.8 us -> 60 us
  between operations: 21.4 us -> 0.15 us
  other arithmetic: 12.7 us -> 0.06 us
  local copies, waits for them, and re-layouts: 15.9 us -> 5.1 us
    psum x4 -> x0, waiting for transfers between devices: 759 us -> none  [local(): prior_obs = lax.psum(jnp.where(is_held[None], picked, 0.0), ('gx', 'gy'))]
    all_to_all x0 -> x3, waiting for transfers between devices: none -> 59.4 us  [the longest x1 27.4 us: local(): lax.all_to_all(taper_send, ('ma', 'gx'), 0, 0, tiled=True)]
    all_gather x4 -> x0, blocking collectives: 41.8 us -> none  [local(): gathered = lax.all_gather(stacked, 'ma', axis=0, tiled=True)]
    pallas_call x0 -> x3, Pallas kernels: none -> 33.9 us  [the longest x1 26.6 us: local(): pl.pallas_call(filter_kernel, out_shape=jax.ShapeDtypeStruct((OWN * 8, LA...]
    all_to_all x0 -> x3, starting transfers between devices: none -> 30.2 us  [the longest x1 10.5 us: local(): lax.all_to_all(owned.reshape(MA * GX, 1, CHUNK * LANES), ('ma', 'gx'), 0,...]
    gather x4 -> x0, local copies, waits for them, and re-layouts: 11.2 us -> none  [local(): picked = jnp.take(gathered, obs_cell[block_id], axis=1)]
    all_to_all x0 -> x1, blocking collectives: none -> 10.6 us  [local(): lax.all_to_all(jnp.broadcast_to(state[None], (MA, OWN * 8, LANES)), 'ma',...]
    ppermute x8 -> x5, starting transfers between devices: 35.5 us -> 29.8 us  [the longest x3 13.5 us: other_core(): return lax.ppermute(x, 'gy', [(0, 1), (1, 0)])]
  transfers between devices with their start and end apart: 12 -> 8, of which waited for: 7 -> 5; matrix products, arithmetic and copies ran while one was open for 0% -> 0% of each run, Pallas kernels for 0% -> 1%
where the time goes in v1:
time: 172 us; the launch traced here: 171 us
  waiting for transfers between devices  61.5 us (36%)
  starting transfers between devices  60 us (35%)
  Pallas kernels  33.9 us (20%)
  blocking collectives  10.6 us (6%)
  local copies, waits for them, and re-layouts  5.1 us (3%)
    all_to_all x1, waiting for transfers between devices, local(): lax.all_to_all(taper_send, ('ma', 'gx'), 0, 0, tiled=True)  27.4 us
    pallas_call x1, Pallas kernels, local(): pl.pallas_call(filter_kernel, out_shape=jax.ShapeDtypeStruct((OWN * 8, LA...  26.6 us
    all_to_all x1, waiting for transfers between devices, local(): lax.all_to_all(picked.reshape(2 * GX, 1, CHUNK * LANES), ('gy', 'gx'), 0,...  16.4 us
    all_to_all x1, waiting for transfers between devices, local(): lax.all_to_all(owned.reshape(MA * GX, 1, CHUNK * LANES), ('ma', 'gx'), 0,...  15.5 us
    ppermute x3, starting transfers between devices, other_core(): return lax.ppermute(x, 'gy', [(0, 1), (1, 0)])  13.5 us
    ppermute x1, starting transfers between devices, local(): high = lax.ppermute(both[:, :, :2], 'gx', backward)  11.5 us
    all_to_all x1, blocking collectives, local(): lax.all_to_all(jnp.broadcast_to(state[None], (MA, OWN * 8, LANES)), 'ma',...  10.6 us
    all_to_all x1, starting transfers between devices, local(): lax.all_to_all(owned.reshape(MA * GX, 1, CHUNK * LANES), ('ma', 'gx'), 0,...  10.5 us
  transfers between devices with their start and end apart: 8, of which 5 were waited for; matrix products, arithmetic and copies ran while one was open for 0% of the time, Pallas kernels for 1%

profile of v1, /device:TPU:1, one launch (start us, length us, event | category | flops | bytes accessed | tf_op | source)
XLA Modules:
  0.0 171.3 jit_solution(517362162701175879)
XLA Ops:
  0.0 0.9 constant_dynamic-update-slice_fusion.1
  1.0 4.8 %collective-permute-start = (f32[22,2,2,128]{3,2,1,0:T(2,128)S(1)}, f32[22,2,2,128]{3,2,1,0:T(2,128)S(1)}, u32[]{:S(2)}, u32[]{:S(2)}) collective-permute-start(f32[22,2,2,128]{3,2,1,0:T(2,128)S(1)} %get-tuple-element.9), channel_id=1, source_target_pairs={{0,8},{8,16},{16,24},{24,32},{32,40},{40,48},{48,56},{56,64},{64,7... | collective-permute-start | bytes 135176 | tf_op jit(solution)/shard_map/ppermute | solution.py:261
  5.8 11.5 %collective-permute-start.1 = (f32[22,2,2,128]{3,2,1,0:T(2,128)S(1)}, f32[22,2,2,128]{3,2,1,0:T(2,128)S(1)}, u32[]{:S(2)}, u32[]{:S(2)}) collective-permute-start(f32[22,2,2,128]{3,2,1,0:T(2,128)S(1)} %get-tuple-element.10), channel_id=1, source_target_pairs={{0,504},{8,0},{16,8},{24,16},{32,24},{40,32},{48,40},{56,48},{64,5... | collective-permute-start | bytes 135176 | tf_op jit(solution)/shard_map/ppermute | solution.py:262
  17.3 1.1 collective-permute-done.1
  18.4 0.1 pad_maximum_fusion
  18.5 3.4 %collective-permute-start.2 = (f32[352,128]{1,0:T(8,128)S(1)}, f32[352,128]{1,0:T(8,128)S(1)}, u32[]{:S(2)}, u32[]{:S(2)}) collective-permute-start(f32[352,128]{1,0:T(8,128)S(1)} %bitcast.14), channel_id=1, source_target_pairs={{0,4},{4,0},{1,5},{5,1},{2,6},{6,2},{3,7},{7,3},{8,12},{12,8},{9,1... | collective-permute-start | bytes 540680 | tf_op jit(solution)/shard_map/ppermute | solution.py:251
  21.9 1.0 collective-permute-done.2.other_ref
  23.0 0.7 copy-done.4
  23.6 5.4 %advect.1 = (f32[160,128]{1,0:T(8,128)}, f32[640,128]{1,0:T(8,128)}) custom-call(s32[4]{0:T(128)} %order.3, f32[352,128]{1,0:T(8,128)} %bitcast.15, f32[352,128]{1,0:T(8,128)} %copy-done.4, s32[4,1024]{1,0:T(4,128)} %cell_ref.1, s32[4,1024]{1,0:T(4,128)} %region_ref.3), custom_call_target="tpu_custom_call" | custom-call | flops 10000000 | bytes 1000000 | tf_op jit(solution)/shard_map/advect/pallas_call | solution.py:272
  29.0 10.1 %all-to-all-start = ((f32[128,1,640]{2,1,0:T(1,128)}), f32[128,1,640]{2,1,0:T(1,128)S(1)}, u32[]{:S(2)}, u32[]{:S(2)}) async-start(f32[128,1,640]{2,1,0:T(1,128)} %bitcast.18), calls=%async_computation | async-start | bytes 655360 | tf_op jit(solution)/shard_map/all_to_all | solution.py:285
  39.2 0.7 constant_dynamic-slice_fusion
  39.9 16.4 %all-to-all-done = f32[128,1,640]{2,1,0:T(1,128)S(1)} async-done(((f32[128,1,640]{2,1,0:T(1,128)}), f32[128,1,640]{2,1,0:T(1,128)S(1)}, u32[]{:S(2)}, u32[]{:S(2)}) %all-to-all-start) | async-done | bytes 327712 | tf_op jit(solution)/shard_map/all_to_all | solution.py:285
  56.3 1.5 broadcast_in_dim.7
  57.9 9.5 %all-to-all-start.2 = ((f32[256,1,1024]{2,1,0:T(1,128)}), f32[256,1,1024]{2,1,0:T(1,128)S(1)}, u32[]{:S(2)}, u32[]{:S(2)}) async-start(f32[256,1,1024]{2,1,0:T(1,128)} %broadcast_in_dim.7), calls=%async_computation.2 | async-start | bytes 2097152 | tf_op jit(solution)/shard_map/all_to_all | solution.py:269
  67.4 1.9 %owner.1 = f32[1280,128]{1,0:T(8,128)} custom-call(f32[640,128]{1,0:T(8,128)} %bitcast.11), custom_call_target="tpu_custom_call" | custom-call | tf_op jit(solution)/shard_map/owner/pallas_call | solution.py:289
  69.3 27.4 %all-to-all-done.2 = f32[256,1,1024]{2,1,0:T(1,128)S(1)} async-done(((f32[256,1,1024]{2,1,0:T(1,128)}), f32[256,1,1024]{2,1,0:T(1,128)S(1)}, u32[]{:S(2)}, u32[]{:S(2)}) %all-to-all-start.2) | async-done | bytes 1048608 | tf_op jit(solution)/shard_map/all_to_all | solution.py:269
  96.7 10.5 %all-to-all-start.1 = ((f32[256,1,640]{2,1,0:T(1,128)}), f32[256,1,640]{2,1,0:T(1,128)S(1)}, u32[]{:S(2)}, u32[]{:S(2)}) async-start(f32[256,1,640]{2,1,0:T(1,128)} %bitcast.10), calls=%async_computation.1 | async-start | bytes 1310720 | tf_op jit(solution)/shard_map/all_to_all | solution.py:296
  107.3 3.9 %collective-permute-start.4 = (f32[2048,128]{1,0:T(8,128)S(1)}, f32[2048,128]{1,0:T(8,128)S(1)}, u32[]{:S(2)}, u32[]{:S(2)}) collective-permute-start(f32[2048,128]{1,0:T(8,128)S(1)} %bitcast.12), channel_id=1, source_target_pairs={{0,4},{4,0},{1,5},{5,1},{2,6},{6,2},{3,7},{7,3},{8,12},{12,8},{9,1... | collective-permute-start | bytes 3145736 | tf_op jit(solution)/shard_map/ppermute | solution.py:251
  111.2 15.5 %all-to-all-done.1 = f32[256,1,640]{2,1,0:T(1,128)S(1)} async-done(((f32[256,1,640]{2,1,0:T(1,128)}), f32[256,1,640]{2,1,0:T(1,128)S(1)}, u32[]{:S(2)}, u32[]{:S(2)}) %all-to-all-start.1) | async-done | bytes 655392 | tf_op jit(solution)/shard_map/all_to_all | solution.py:296
  126.8 6.1 %collective-permute-start.3 = (f32[1280,128]{1,0:T(8,128)S(1)}, f32[1280,128]{1,0:T(8,128)S(1)}, u32[]{:S(2)}, u32[]{:S(2)}) collective-permute-start(f32[1280,128]{1,0:T(8,128)S(1)} %bitcast.16), channel_id=1, source_target_pairs={{0,4},{4,0},{1,5},{5,1},{2,6},{6,2},{3,7},{7,3},{8,12},{12,8},{9,1... | collective-permute-start | bytes 1966088 | tf_op jit(solution)/shard_map/ppermute | solution.py:251
  132.9 10.6 %all_to_all.20 = f32[4,160,128]{2,1,0:T(8,128)} all-to-all(f32[4,160,128]{2,1,0:T(8,128)S(1)} %broadcast_in_dim.16), channel_id=1, replica_groups=mesh['gx'=64,'gy'=2,'ma'=4] {'ma'}, dimensions={0} | all-to-all | bytes 655360 | tf_op jit(solution)/shard_map/all_to_all | solution.py:286
  143.5 0.8 copy-done.8
  144.3 0.4 copy-done.7
  144.7 26.6 %filter.1 = f32[160,128]{1,0:T(8,128)} custom-call(s32[4]{0:T(128)} %order.3, f32[1280,128]{1,0:T(8,128)} %bitcast.17, f32[1280,128]{1,0:T(8,128)} %copy-done.8, f32[2048,128]{1,0:T(8,128)} %bitcast.13, f32[2048,128]{1,0:T(8,128)} %copy-done.7, f32[4,1024]{1,0:T(4,128)} %bitcast.21, f32[4,1024]{1,0:T(4,128)} %value_ref.1, f32[4,1024]{1,0:T(4,128)} %var_ref.1, ...), custom_call_target="tpu_custom_call" | custom-call | flops 3000000000 | bytes 4000000 | tf_op jit(solution)/shard_map/filter/pallas_call | solution.py:301
  (21 shorter events, 0.1 us)
Async XLA Ops:
  0.0 0.9 copy-start.6
  1.0 16.3 %collective-permute-start = (f32[22,2,2,128]{3,2,1,0:T(2,128)S(1)}, f32[22,2,2,128]{3,2,1,0:T(2,128)S(1)}, u32[]{:S(2)}, u32[]{:S(2)}) collective-permute-start(f32[22,2,2,128]{3,2,1,0:T(2,128)S(1)} %get-tuple-element.9), channel_id=1, source_target_pairs={{0,8},{8,16},{16,24},{24,32},{32,40},{40,48},{48,56},{56,64},{64,7... | collective-permute-start | bytes 135176 | tf_op jit(solution)/shard_map/ppermute | solution.py:261
  5.8 12.6 %collective-permute-start.1 = (f32[22,2,2,128]{3,2,1,0:T(2,128)S(1)}, f32[22,2,2,128]{3,2,1,0:T(2,128)S(1)}, u32[]{:S(2)}, u32[]{:S(2)}) collective-permute-start(f32[22,2,2,128]{3,2,1,0:T(2,128)S(1)} %get-tuple-element.10), channel_id=1, source_target_pairs={{0,504},{8,0},{16,8},{24,16},{32,24},{40,32},{48,40},{56,48},{64,5... | collective-permute-start | bytes 135176 | tf_op jit(solution)/shard_map/ppermute | solution.py:262
  18.5 4.5 %copy-start.2 = (f32[22,2,8,128]{3,2,1,0:T(8,128)}, f32[22,2,8,128]{3,2,1,0:T(8,128)S(1)}, u32[]{:S(2)}) copy-start(f32[22,2,8,128]{3,2,1,0:T(8,128)S(1)} %pad_maximum_fusion) | copy-start | bytes 540676
  18.5 4.5 %collective-permute-start.2 = (f32[352,128]{1,0:T(8,128)S(1)}, f32[352,128]{1,0:T(8,128)S(1)}, u32[]{:S(2)}, u32[]{:S(2)}) collective-permute-start(f32[352,128]{1,0:T(8,128)S(1)} %bitcast.14), channel_id=1, source_target_pairs={{0,4},{4,0},{1,5},{5,1},{2,6},{6,2},{3,7},{7,3},{8,12},{12,8},{9,1... | collective-permute-start | bytes 540680 | tf_op jit(solution)/shard_map/ppermute | solution.py:251
  23.0 0.7 copy-start.4
  29.0 27.3 %all-to-all-start = ((f32[128,1,640]{2,1,0:T(1,128)}), f32[128,1,640]{2,1,0:T(1,128)S(1)}, u32[]{:S(2)}, u32[]{:S(2)}) async-start(f32[128,1,640]{2,1,0:T(1,128)} %bitcast.18), calls=%async_computation | async-start | bytes 655360 | tf_op jit(solution)/shard_map/all_to_all | solution.py:285
  56.3 1.5 copy-start
  57.9 38.9 %all-to-all-start.2 = ((f32[256,1,1024]{2,1,0:T(1,128)}), f32[256,1,1024]{2,1,0:T(1,128)S(1)}, u32[]{:S(2)}, u32[]{:S(2)}) async-start(f32[256,1,1024]{2,1,0:T(1,128)} %broadcast_in_dim.7), calls=%async_computation.2 | async-start | bytes 2097152 | tf_op jit(solution)/shard_map/all_to_all | solution.py:269
  96.7 46.8 %copy-start.1 = (f32[256,1,1024]{2,1,0:T(1,128)}, f32[256,1,1024]{2,1,0:T(1,128)S(1)}, u32[]{:S(2)}) copy-start(f32[256,1,1024]{2,1,0:T(1,128)S(1)} %all-to-all-done.2) | copy-start | bytes 3145732
  96.7 36.1 %copy-start.5 = (f32[160,128]{1,0:T(8,128)S(1)}, f32[160,128]{1,0:T(8,128)}, u32[]{:S(2)}) copy-start(f32[160,128]{1,0:T(8,128)} %get-tuple-element.8.state_ref) | copy-start | bytes 245764
  96.7 30.0 %all-to-all-start.1 = ((f32[256,1,640]{2,1,0:T(1,128)}), f32[256,1,640]{2,1,0:T(1,128)S(1)}, u32[]{:S(2)}, u32[]{:S(2)}) async-start(f32[256,1,640]{2,1,0:T(1,128)} %bitcast.10), calls=%async_computation.1 | async-start | bytes 1310720 | tf_op jit(solution)/shard_map/all_to_all | solution.py:296
  107.3 36.2 %collective-permute-start.4 = (f32[2048,128]{1,0:T(8,128)S(1)}, f32[2048,128]{1,0:T(8,128)S(1)}, u32[]{:S(2)}, u32[]{:S(2)}) collective-permute-start(f32[2048,128]{1,0:T(8,128)S(1)} %bitcast.12), channel_id=1, source_target_pairs={{0,4},{4,0},{1,5},{5,1},{2,6},{6,2},{3,7},{7,3},{8,12},{12,8},{9,1... | collective-permute-start | bytes 3145736 | tf_op jit(solution)/shard_map/ppermute | solution.py:251
  126.7 16.8 %copy-start.3 = (f32[256,1,640]{2,1,0:T(1,128)}, f32[256,1,640]{2,1,0:T(1,128)S(1)}, u32[]{:S(2)}) copy-start(f32[256,1,640]{2,1,0:T(1,128)S(1)} %all-to-all-done.1) | copy-start | bytes 1966084
  126.8 16.8 %collective-permute-start.3 = (f32[1280,128]{1,0:T(8,128)S(1)}, f32[1280,128]{1,0:T(8,128)S(1)}, u32[]{:S(2)}, u32[]{:S(2)}) collective-permute-start(f32[1280,128]{1,0:T(8,128)S(1)} %bitcast.16), channel_id=1, source_target_pairs={{0,4},{4,0},{1,5},{5,1},{2,6},{6,2},{3,7},{7,3},{8,12},{12,8},{9,1... | collective-permute-start | bytes 1966088 | tf_op jit(solution)/shard_map/ppermute | solution.py:251
  143.5 0.8 copy-start.8
  143.5 1.2 copy-start.7

commit v2 on v1

--- a/solution.py
+++ b/solution.py
@@ -17,6 +17,7 @@
 KAPPA = 0.025
 CHUNK = 5
 HALF = OWN * 2 * GROUPS
+QUARTER = (BLOCKS - 1) * GROUPS // MA
 ROWS_O = 256
 F32 = jnp.float32
 BF16 = jnp.bfloat16
@@ -45,56 +46,78 @@
 
 
 def advect_kernel(order, own_ref, other_ref, cell_ref, region_ref, state_ref, picked_ref, work):
+    gx, gy = lax.axis_index("gx"), lax.axis_index("gy")
     lane = lax.broadcasted_iota(jnp.int32, (8, LANES), 1)
     first, last = lane == 0, lane == LANES - 1
 
-    def step(q, beside, u, v):
+    def step(q, beside, wind):
+        u_up, u_down, v_up, v_down = wind
         west, east = pltpu.roll(q, 1, 0), pltpu.roll(q, 7, 0)
         south = jnp.where(first, pltpu.roll(beside, 1, 1), pltpu.roll(q, 1, 1))
         north = jnp.where(last, pltpu.roll(beside, LANES - 1, 1), pltpu.roll(q, LANES - 1, 1))
         return (
             q
-            - jnp.maximum(u, 0.0) * (q - west)
-            - jnp.minimum(u, 0.0) * (east - q)
-            - jnp.maximum(v, 0.0) * (q - south)
-            - jnp.minimum(v, 0.0) * (north - q)
+            - u_up * (q - west)
+            - u_down * (east - q)
+            - v_up * (q - south)
+            - v_down * (north - q)
             + KAPPA * (east + west + north + south - 4.0 * q)
         )
 
-    work[pl.ds(160, 32), :] = jnp.zeros((32, LANES), F32)
+    def winds(ref, level):
+        u = ref[pl.ds((OWN * 2 + level) * 8, 8), :]
+        v = ref[pl.ds((OWN * 2 + 2 + level) * 8, 8), :]
+        return jnp.maximum(u, 0.0), jnp.minimum(u, 0.0), jnp.maximum(v, 0.0), jnp.minimum(v, 0.0)
+
+    for side in range(2):
+        work[side, pl.ds(OWN * 8, 32), :] = jnp.zeros((32, LANES), F32)
     for level in range(2):
-        row = (OWN * 2 + level) * 8
-        u, v = own_ref[pl.ds(row, 8), :], own_ref[pl.ds(row + 32 - 16, 8), :]
-        u_o, v_o = other_ref[pl.ds(row, 8), :], other_ref[pl.ds(row + 32 - 16, 8), :]
+        wind, wind_o = winds(own_ref, level), winds(other_ref, level)
         for m in range(OWN):
             at = (m * 2 + level) * 8
             q, q_o = own_ref[pl.ds(at, 8), :], other_ref[pl.ds(at, 8), :]
-            once, once_o = step(q, q_o, u, v), step(q_o, q, u_o, v_o)
-            twice = step(once, once_o, u, v)
-            work[pl.ds(m * 8 + level * 4, 4), :] = twice[2:6]
-            state_ref[pl.ds(m * 8 + level * 4, 4), :] = twice[2:6]
-
-    own_region = lax.axis_index("gx") * 2 + lax.axis_index("gy")
-    for k in range(BLOCKS):
-        b = order[k]
+            once, once_o = step(q, q_o, wind), step(q_o, q, wind_o)
+            twice, twice_o = step(once, once_o, wind), step(once_o, once, wind_o)
+            at = pl.ds(m * 8 + level * 4, 4)
+            state_ref[at, :] = twice[2:6]
+            work[0, at, :] = twice[2:6]
+            work[1, at, :] = twice_o[2:6]
+
+    for k in range(2):
+        b = order[gy * 2 + k]
         for g in range(GROUPS):
             columns = pl.ds(g * LANES, LANES)
             cell, region = block_row(cell_ref, b, columns), block_row(region_ref, b, columns)
             y = jnp.broadcast_to(jnp.bitwise_and(cell, LANES - 1), (24, LANES))
-            part = jnp.where(region == own_region, jnp.right_shift(cell, 7), -1)
+            part = jnp.right_shift(cell, 7) + jnp.where(jnp.bitwise_and(region, 1) == gy, 0, 8)
+            part = jnp.where(jnp.right_shift(region, 1) == gx, part, -1)
             part = jnp.broadcast_to(part, (24, LANES))
             total = jnp.zeros((24, LANES), F32)
-            for c in range(8):
-                source = work[pl.ds(c, 24, stride=8), :]
+            for c in range(16):
+                source = work[c // 8, pl.ds(c % 8, 24, stride=8), :]
                 found = jnp.take_along_axis(source, y, axis=1)
                 total = jnp.where(part == c, found, total)
-            at = (k // 2) * HALF + (k % 2) * GROUPS + g
-            picked_ref[pl.ds(at, OWN, stride=16), :] = total[:OWN]
+            picked_ref[pl.ds(k * GROUPS + g, OWN, stride=16), :] = total[:OWN]
+
+
+def send_kernel(order, taper_ref, out_ref):
+    q = lax.axis_index("ma")
+    pieces = []
+    for i in range(QUARTER):
+        tile = q * QUARTER + i
+        b, g = order[tile // GROUPS], tile % GROUPS
+        row = block_row(taper_ref, b, pl.ds(0, LANES))
+        for j in range(1, GROUPS):
+            row = jnp.where(g == j, block_row(taper_ref, b, pl.ds(j * LANES, LANES)), row)
+        pieces.append(row)
+    four = jnp.concatenate(pieces * 4, axis=0)
+    for i in range(GX // 4):
+        out_ref[pl.ds(i * 4 * QUARTER, 4 * QUARTER), :] = four
 
 
 def owner_kernel(parts_ref, out_ref):
     total = parts_ref[pl.ds(0, 40), :]
-    for i in range(1, 16):
+    for i in range(1, GX // 8):
         total = total + parts_ref[pl.ds(i * 40, 40), :]
     part = total[0:CHUNK]
     for i in range(1, 8):
@@ -104,22 +127,43 @@
         out_ref[pl.ds(i * 40, 40), :] = eight
 
 
+def prepare_kernel(order, taper_ref, taper_o_ref, region_ref, tapers, onehots):
+    q, gy = lax.axis_index("ma"), lax.axis_index("gy")
+    for shift in range(MA):
+        for i in range(QUARTER):
+            tile = lax.rem(q - shift + MA, MA) * QUARTER + i
+            for side, ref in enumerate((taper_ref, taper_o_ref)):
+                high, low = split(ref[pl.ds(shift * GX * QUARTER + i, GX, stride=QUARTER), :])
+                tapers[tile, pl.ds(side * GX, GX), :] = high
+                tapers[tile, pl.ds(LANES + side * GX, GX), :] = low
+
+    rows = lax.broadcasted_iota(jnp.int32, (LANES, LANES), 0)
+    for k in range(1, BLOCKS):
+        b = order[k]
+        for g in range(GROUPS):
+            region = block_row(region_ref, b, pl.ds(g * LANES, LANES))
+            place = jnp.where(jnp.bitwise_and(region, 1) == gy, 0, GX) + jnp.right_shift(region, 1)
+            hot = (rows == jnp.broadcast_to(place, (LANES, LANES))).astype(F32).T.astype(BF16)
+            at = pl.ds(((k - 1) * GROUPS + g) * LANES, LANES)
+            onehots[at, pl.ds(0, LANES)] = hot
+            onehots[at, pl.ds(LANES, LANES)] = hot
+
+
 def filter_kernel(
     order,
     prior_ref,
     prior_o_ref,
-    taper_ref,
-    taper_o_ref,
+    tapers,
+    onehots,
     taper_own_ref,
     value_ref,
     var_ref,
-    region_ref,
-    gathered_ref,
+    gathered_1,
+    gathered_2,
+    gathered_3,
     state_ref,
     out_ref,
     xt,
-    tapers,
-    onehots,
     b_high,
     b_both,
     increments,
@@ -145,27 +189,6 @@
     def _():
         load_half(prior_o_ref, 0)
         load_half(prior_ref, 1)
-
-    for k in range(BLOCKS - 1):
-        b = order[k]
-        for g in range(GROUPS):
-            for i, ref in enumerate((taper_ref, taper_o_ref)):
-                high, low = split(ref.at[pl.ds(pl.multiple_of(b * (GX * 8), GX * 8), GX * 8), :][pl.ds(g, GX, stride=8), :])
-                tapers[k, pl.ds(i * GX, GX), pl.ds(g * LANES, LANES)] = high
-                tapers[k, pl.ds(LANES + i * GX, GX), pl.ds(g * LANES, LANES)] = low
-
-    rows = lax.broadcasted_iota(jnp.int32, (LANES, LANES), 0)
-    for k in range(1, BLOCKS):
-        b = order[k]
-        for g in range(GROUPS):
-            region = block_row(region_ref, b, pl.ds(g * LANES, LANES))
-            place = jnp.where(
-                jnp.bitwise_and(region, 1) == gy, 0, GX
-            ) + jnp.right_shift(region, 1)
-            hot = (rows == jnp.broadcast_to(place, (LANES, LANES))).astype(F32).T.astype(BF16)
-            at = pl.ds(((k - 1) * GROUPS + g) * LANES, LANES)
-            onehots[at, pl.ds(0, LANES)] = hot
-            onehots[at, pl.ds(LANES, LANES)] = hot
 
     lane = lax.broadcasted_iota(jnp.int32, (ROWS_O, LANES), 1)
     member_row = lax.broadcasted_iota(jnp.int32, (LANES, OBS), 0)
@@ -206,6 +229,7 @@
         b_both[:, pl.ds(LANES, LANES)] = gain_low.astype(F32).T.astype(BF16)
 
         def chunk(i, carry, k=k, left=left):
+            taper = jnp.concatenate([tapers[k * GROUPS + g] for g in range(GROUPS)], axis=1)
             at = pl.multiple_of((k + 1) * OBS + i * ROWS_O, ROWS_O)
             x = xt[pl.ds(at, ROWS_O), :]
             clean = jnp.where(lane < MEMBERS, x, 0.0)
@@ -217,7 +241,7 @@
             second = jnp.where(lane < 3 * MEMBERS - LANES, second, 0.0)
             query = jnp.concatenate([first, second], axis=1).astype(BF16)
             hot = onehots[pl.ds(pl.multiple_of(at - OBS, ROWS_O), ROWS_O), :]
-            weight = dot_nn(query, left) * dot_nn(hot, tapers[k])
+            weight = dot_nn(query, left) * dot_nn(hot, taper)
             w_high, w_low = split(weight)
             both = dot_nn(w_high, b_both[...])
             xt[pl.ds(at, ROWS_O), :] = (
@@ -230,13 +254,22 @@
     q = lax.axis_index("ma")
     e = increments[...]
     total = e + e[MEMBERS : MEMBERS + 1]
-    pick_row = lax.broadcasted_iota(jnp.int32, (24, LANES), 0)
-    pick_lane = lax.broadcasted_iota(jnp.int32, (24, LANES), 1)
-    chosen = jnp.where((pick_lane == pick_row + q * OWN) & (pick_row < OWN), 1.0, 0.0)
+    row = lax.broadcasted_iota(jnp.int32, (24, LANES), 0)
+    col = lax.broadcasted_iota(jnp.int32, (24, LANES), 1)
+    chosen = jnp.where((col == row + q * OWN) & (row < OWN), 1.0, 0.0)
     transform = jnp.dot(chosen, total, precision=lax.Precision.HIGHEST, preferred_element_type=F32)
+    row = lax.broadcasted_iota(jnp.int32, (LANES, LANES), 0)
+    col = lax.broadcasted_iota(jnp.int32, (LANES, LANES), 1)
+    back = sum(jnp.where(col >= i * OWN, 1, 0) for i in range(1, MA))
+    member = jnp.bitwise_and(q - back, MA - 1) * OWN + col - back * OWN
+    shuffle = jnp.where((row == member) & (col < MEMBERS), 1.0, 0.0)
+    transform = jnp.dot(transform, shuffle, precision=lax.Precision.HIGHEST, preferred_element_type=F32)
     tiles = []
     for c in range(8):
-        tile = gathered_ref[pl.ds(c, MEMBERS, stride=8), :]
+        at = pl.ds(c, OWN, stride=8)
+        tile = jnp.concatenate(
+            [ref[at, :] for ref in (state_ref, gathered_1, gathered_2, gathered_3)], axis=0
+        )
         tiles.append(tile - jnp.mean(tile, axis=0, keepdims=True))
     centered = jnp.concatenate(
         [jnp.concatenate(tiles, axis=1), jnp.zeros((LANES - MEMBERS, CELLS), F32)], axis=0
@@ -251,10 +284,30 @@
     return lax.ppermute(x, "gy", [(0, 1), (1, 0)])
 
 
+def params(mebibytes):
+    return pltpu.CompilerParams(vmem_limit_bytes=mebibytes * 1024 * 1024)
+
+
+def over_members(x):
+    return [lax.ppermute(x, "ma", [(i, (i + s) % MA) for i in range(MA)]) for s in range(1, MA)]
+
+
 def local(
     ensemble, wind_field, obs_value, obs_var, obs_region, obs_cell, block_order, localization
 ):
-    q = lax.axis_index("ma")
+    taper_own = localization.reshape(BLOCKS, OBS)
+    taper_send = pl.pallas_call(
+        send_kernel,
+        out_shape=jax.ShapeDtypeStruct((GX * QUARTER, LANES), F32),
+        in_specs=[SMEM, VMEM],
+        out_specs=VMEM,
+        compiler_params=params(2),
+        name="send",
+    )(block_order, taper_own)
+    tapers = lax.all_to_all(
+        taper_send.reshape(GX, 1, QUARTER * LANES), "gx", 0, 0, tiled=True
+    ).reshape(-1, LANES)
+
     both = jnp.concatenate([ensemble, wind_field], axis=0)
     forward = [(i, (i + 1) % GX) for i in range(GX)]
     backward = [(i, (i - 1) % GX) for i in range(GX)]
@@ -263,67 +316,75 @@
     own = jnp.concatenate([low, both, high], axis=2).reshape(-1, LANES)
     beside = other_core(own)
 
-    taper_own = localization.reshape(BLOCKS, OBS)
-    taper_send = lax.dynamic_slice_in_dim(taper_own, q, 1, 0)
-    taper_send = jnp.broadcast_to(taper_send[None], (MA * GX, 1, OBS))
-    tapers = lax.all_to_all(taper_send, ("ma", "gx"), 0, 0, tiled=True).reshape(-1, LANES)
-    tapers_beside = other_core(tapers)
-
     state, picked = pl.pallas_call(
         advect_kernel,
         out_shape=(
             jax.ShapeDtypeStruct((OWN * 8, LANES), F32),
-            jax.ShapeDtypeStruct((2 * HALF, LANES), F32),
+            jax.ShapeDtypeStruct((HALF, LANES), F32),
         ),
         in_specs=[SMEM, VMEM, VMEM, VMEM, VMEM],
         out_specs=(VMEM, VMEM),
-        scratch_shapes=[pltpu.VMEM((24 * 8, LANES), F32)],
+        scratch_shapes=[pltpu.VMEM((2, 24 * 8, LANES), F32)],
+        compiler_params=params(4),
         cost_estimate=pl.CostEstimate(flops=10_000_000, bytes_accessed=1_000_000, transcendentals=0),
         name="advect",
     )(block_order, own, beside, obs_cell, obs_region)
 
-    parts = lax.all_to_all(picked.reshape(2 * GX, 1, CHUNK * LANES), ("gy", "gx"), 0, 0, tiled=True)
-    gathered = lax.all_to_all(
-        jnp.broadcast_to(state[None], (MA, OWN * 8, LANES)), "ma", 0, 0, tiled=True
-    ).reshape(-1, LANES)
+    picked, tapers = lax.optimization_barrier((picked, tapers))
+    parts = lax.all_to_all(picked.reshape(GX, 1, CHUNK * LANES), "gx", 0, 0, tiled=True)
+    parts, tapers = lax.optimization_barrier((parts, [tapers] + over_members(tapers)))
+    tapers = jnp.concatenate(tapers, axis=0)
+    tapers_beside = other_core(tapers)
+    gathered = over_members(state)
+    prepared = pl.pallas_call(
+        prepare_kernel,
+        out_shape=(
+            jax.ShapeDtypeStruct(((BLOCKS - 1) * GROUPS, 2 * LANES, LANES), BF16),
+            jax.ShapeDtypeStruct(((BLOCKS - 1) * OBS, 2 * LANES), BF16),
+        ),
+        in_specs=[SMEM, VMEM, VMEM, VMEM],
+        out_specs=(VMEM, VMEM),
+        compiler_params=params(8),
+        cost_estimate=pl.CostEstimate(flops=10_000_000, bytes_accessed=5_000_000, transcendentals=0),
+        name="prepare",
+    )(block_order, tapers, tapers_beside, obs_region)
     owned = pl.pallas_call(
         owner_kernel,
         out_shape=jax.ShapeDtypeStruct((MA * GX * CHUNK, LANES), F32),
         in_specs=[VMEM],
         out_specs=VMEM,
+        compiler_params=params(4),
         name="owner",
     )(parts.reshape(-1, LANES))
     priors = lax.all_to_all(
         owned.reshape(MA * GX, 1, CHUNK * LANES), ("ma", "gx"), 0, 0, tiled=True
     ).reshape(-1, LANES)
+    priors, prepared, gathered = lax.optimization_barrier((priors, prepared, gathered))
     priors_beside = other_core(priors)
 
     out = pl.pallas_call(
         filter_kernel,
         out_shape=jax.ShapeDtypeStruct((OWN * 8, LANES), F32),
-        in_specs=[SMEM] + [VMEM] * 10,
+        in_specs=[SMEM] + [VMEM] * 11,
         out_specs=VMEM,
         scratch_shapes=[
             pltpu.VMEM((BLOCKS * OBS, LANES), F32),
-            pltpu.VMEM((BLOCKS - 1, 2 * LANES, OBS), BF16),
-            pltpu.VMEM(((BLOCKS - 1) * OBS, 2 * LANES), BF16),
             pltpu.VMEM((OBS, LANES), BF16),
             pltpu.VMEM((OBS, 2 * LANES), BF16),
             pltpu.VMEM((LANES, LANES), F32),
         ],
+        compiler_params=params(32),
         cost_estimate=pl.CostEstimate(flops=3_000_000_000, bytes_accessed=4_000_000, transcendentals=0),
         name="filter",
     )(
         block_order,
         priors,
         priors_beside,
-        tapers,
-        tapers_beside,
+        *prepared,
         taper_own,
         obs_value,
         obs_var,
-        obs_region,
-        gathered,
+        *gathered,
         state,
     )
     return out.reshape(ensemble.shape)

time: 172 us -> 144 us (0.84)
  waiting for transfers between devices: 61.5 us -> 12.5 us
  starting transfers between devices: 60 us -> 89.3 us
  blocking collectives: 10.6 us -> 0 us
  local copies, waits for them, and re-layouts: 5.1 us -> 7.78 us
    all_to_all x2, waiting for transfers between devices: 43.8 us -> 0.01 us  [the longest x1 0.01 us: local(): lax.all_to_all(taper_send.reshape(GX, 1, QUARTER * LANES), 'gx', 0, 0, ti...]
    ppermute x0 -> x6, starting transfers between devices: none -> 20.6 us  [over_members(): lax.ppermute(x, 'ma', [(i, (i + s) % MA) for i in range(MA)])]
    all_to_all x1, waiting for transfers between devices: 15.5 us -> 2.76 us  [local(): lax.all_to_all(owned.reshape(MA * GX, 1, CHUNK * LANES), ('ma', 'gx'), 0,...]
    all_to_all x1 -> x0, blocking collectives: 10.6 us -> none  [local(): lax.all_to_all(jnp.broadcast_to(state[None], (MA, OWN * 8, LANES)), 'ma',...]
    all_to_all x2, starting transfers between devices: 19.6 us -> 28.3 us  [the longest x1 17.1 us: local(): lax.all_to_all(taper_send.reshape(GX, 1, QUARTER * LANES), 'gx', 0, 0, ti...]
    all_to_all x1, starting transfers between devices: 10.5 us -> 18.6 us  [local(): lax.all_to_all(owned.reshape(MA * GX, 1, CHUNK * LANES), ('ma', 'gx'), 0,...]
    ppermute x0 -> x6, waiting for transfers between devices: none -> 5.9 us  [over_members(): lax.ppermute(x, 'ma', [(i, (i + s) % MA) for i in range(MA)])]
    ppermute x1, starting transfers between devices: 11.5 us -> 5.68 us  [local(): high = lax.ppermute(both[:, :, :2], 'gx', backward)]
  transfers between devices with their start and end apart: 8 -> 14, of which waited for: 5 -> 8; matrix products, arithmetic and copies ran while one was open for 0% -> 1% of each run, Pallas kernels for 1% -> 4%
where the time goes in v2:
time: 144 us; the launch traced here: 143 us
  starting transfers between devices  89.3 us (62%)
  Pallas kernels  32.9 us (23%)
  waiting for transfers between devices  12.5 us (9%)
  local copies, waits for them, and re-layouts  7.78 us (5%)
    pallas_call x1, Pallas kernels, local(): pl.pallas_call(filter_kernel, out_shape=jax.ShapeDtypeStruct((OWN * 8, LA...  24.8 us
    ppermute x6, starting transfers between devices, over_members(): lax.ppermute(x, 'ma', [(i, (i + s) % MA) for i in range(MA)])  20.6 us
    all_to_all x1, starting transfers between devices, local(): lax.all_to_all(owned.reshape(MA * GX, 1, CHUNK * LANES), ('ma', 'gx'), 0,...  18.6 us
    all_to_all x1, starting transfers between devices, local(): lax.all_to_all(taper_send.reshape(GX, 1, QUARTER * LANES), 'gx', 0, 0, ti...  17.1 us
    ppermute x3, starting transfers between devices, other_core(): return lax.ppermute(x, 'gy', [(0, 1), (1, 0)])  13.2 us
    all_to_all x1, starting transfers between devices, local(): lax.all_to_all(picked.reshape(GX, 1, CHUNK * LANES), 'gx', 0, 0, tiled=True)  11.2 us
    unnamed x28, local copies, waits for them, and re-layouts  7.02 us
    ppermute x6, waiting for transfers between devices, over_members(): lax.ppermute(x, 'ma', [(i, (i + s) % MA) for i in range(MA)])  5.9 us
  transfers between devices with their start and end apart: 14, of which 8 were waited for; matrix products, arithmetic and copies ran while one was open for 1% of the time, Pallas kernels for 4%

profile of v2, /device:TPU:1, one launch (start us, length us, event | category | flops | bytes accessed | tf_op | source)
XLA Modules:
  0.0 142.8 jit_solution(11187638079763639874)
XLA Ops:
  1.4 1.3 send.1
  2.7 17.1 %all-to-all-start = ((f32[64,1,768]{2,1,0:T(1,128)}), f32[64,1,768]{2,1,0:T(1,128)S(1)}, u32[]{:S(2)}, u32[]{:S(2)}) async-start(f32[64,1,768]{2,1,0:T(1,128)} %bitcast.2), calls=%async_computation | async-start | bytes 393216 | tf_op jit(solution)/shard_map/all_to_all | solution.py:307
  21.5 2.9 %collective-permute-start = (f32[22,2,2,128]{3,2,1,0:T(2,128)S(1)}, f32[22,2,2,128]{3,2,1,0:T(2,128)S(1)}, u32[]{:S(2)}, u32[]{:S(2)}) collective-permute-start(f32[22,2,2,128]{3,2,1,0:T(2,128)S(1)} %get-tuple-element.39), channel_id=1, source_target_pairs={{0,8},{8,16},{16,24},{24,32},{32,40},{40,48},{48,56},{56,64},{64,7... | collective-permute-start | bytes 135176 | tf_op jit(solution)/shard_map/ppermute | solution.py:314
  24.4 5.7 %collective-permute-start.1 = (f32[22,2,2,128]{3,2,1,0:T(2,128)S(1)}, f32[22,2,2,128]{3,2,1,0:T(2,128)S(1)}, u32[]{:S(2)}, u32[]{:S(2)}) collective-permute-start(f32[22,2,2,128]{3,2,1,0:T(2,128)S(1)} %get-tuple-element.40), channel_id=1, source_target_pairs={{0,504},{8,0},{16,8},{24,16},{32,24},{40,32},{48,40},{56,48},{64,5... | collective-permute-start | bytes 135176 | tf_op jit(solution)/shard_map/ppermute | solution.py:315
  31.3 4.0 %collective-permute-start.2 = (f32[352,128]{1,0:T(8,128)S(1)}, f32[352,128]{1,0:T(8,128)S(1)}, u32[]{:S(2)}, u32[]{:S(2)}) collective-permute-start(f32[352,128]{1,0:T(8,128)S(1)} %bitcast.9), channel_id=1, source_target_pairs={{0,4},{4,0},{1,5},{5,1},{2,6},{6,2},{3,7},{7,3},{8,12},{12,8},{9,1... | collective-permute-start | bytes 540680 | tf_op jit(solution)/shard_map/ppermute | solution.py:284
  38.4 4.8 %advect.1 = (f32[160,128]{1,0:T(8,128)S(1)}, f32[320,128]{1,0:T(8,128)}) custom-call(s32[4]{0:T(128)S(1)} %copy-done.6, f32[352,128]{1,0:T(8,128)S(1)} %bitcast.10, f32[352,128]{1,0:T(8,128)S(1)} %collective-permute-done.2.other_ref, s32[4,1024]{1,0:T(4,128)S(1)} %copy-done.2, s32[4,1024]{1,0:T(4,128)S(1)} %copy-done), custom_call_target="tpu_custom_call" | custom-call | flops 10000000 | bytes 1000000 | tf_op jit(solution)/shard_map/advect/pallas_call | solution.py:319
  43.2 11.2 %all-to-all-start.1 = ((f32[64,1,640]{2,1,0:T(1,128)}), f32[64,1,640]{2,1,0:T(1,128)S(1)}, u32[]{:S(2)}, u32[]{:S(2)}) async-start(f32[64,1,640]{2,1,0:T(1,128)} %bitcast.4), calls=%async_computation.1 | async-start | bytes 327680 | tf_op jit(solution)/shard_map/all_to_all | solution.py:334
  54.4 3.1 %collective-permute-start.3 = (f32[384,128]{1,0:T(8,128)S(1)}, f32[384,128]{1,0:T(8,128)S(1)}, u32[]{:S(2)}, u32[]{:S(2)}) collective-permute-start(f32[384,128]{1,0:T(8,128)S(1)} %bitcast.16), channel_id=1, source_target_pairs={{0,1},{1,2},{2,3},{3,0},{4,5},{5,6},{6,7},{7,4},{8,9},{9,10},{10,1... | collective-permute-start | bytes 589832 | tf_op jit(solution)/shard_map/ppermute | solution.py:292
  57.5 4.4 %collective-permute-start.4 = (f32[384,128]{1,0:T(8,128)S(1)}, f32[384,128]{1,0:T(8,128)S(1)}, u32[]{:S(2)}, u32[]{:S(2)}) collective-permute-start(f32[384,128]{1,0:T(8,128)S(1)} %bitcast.17), channel_id=1, source_target_pairs={{0,2},{1,3},{2,0},{3,1},{4,6},{5,7},{6,4},{7,5},{8,10},{9,11},{10,... | collective-permute-start | bytes 589832 | tf_op jit(solution)/shard_map/ppermute | solution.py:292
  61.9 3.1 %collective-permute-start.5 = (f32[384,128]{1,0:T(8,128)S(1)}, f32[384,128]{1,0:T(8,128)S(1)}, u32[]{:S(2)}, u32[]{:S(2)}) collective-permute-start(f32[384,128]{1,0:T(8,128)S(1)} %bitcast.18), channel_id=1, source_target_pairs={{0,3},{1,0},{2,1},{3,2},{4,7},{5,4},{6,5},{7,6},{8,11},{9,8},{10,9... | collective-permute-start | bytes 589832 | tf_op jit(solution)/shard_map/ppermute | solution.py:292
  65.0 3.5 %collective-permute-done.4 = f32[384,128]{1,0:T(8,128)S(1)} collective-permute-done((f32[384,128]{1,0:T(8,128)S(1)}, f32[384,128]{1,0:T(8,128)S(1)}, u32[]{:S(2)}, u32[]{:S(2)}) %collective-permute-start.4) | collective-permute-done | bytes 196640 | tf_op jit(solution)/shard_map/ppermute | solution.py:292
  68.5 1.3 collective-permute-done.5
  70.7 18.6 %all-to-all-start.2 = ((f32[256,1,640]{2,1,0:T(1,128)}), f32[256,1,640]{2,1,0:T(1,128)S(1)}, u32[]{:S(2)}, u32[]{:S(2)}) async-start(f32[256,1,640]{2,1,0:T(1,128)} %bitcast.6), calls=%async_computation.2 | async-start | bytes 1310720 | tf_op jit(solution)/shard_map/all_to_all | solution.py:359
  89.5 3.6 %collective-permute-start.6 = (f32[1536,128]{1,0:T(8,128)S(1)}, f32[1536,128]{1,0:T(8,128)S(1)}, u32[]{:S(2)}, u32[]{:S(2)}) collective-permute-start(f32[1536,128]{1,0:T(8,128)S(1)} %constant_dynamic-update-slice_fusion.2.taper_ref), channel_id=1, source_target_pairs={{0,4},{4,0},{1,5},{5,1},{2,6},{6,2},{3,7},{7,3},{8,12},{12,8},{9,1... | collective-permute-start | bytes 2359304 | tf_op jit(solution)/shard_map/ppermute | solution.py:284
  93.1 2.2 %collective-permute-start.7 = (f32[160,128]{1,0:T(8,128)S(1)}, f32[160,128]{1,0:T(8,128)S(1)}, u32[]{:S(2)}, u32[]{:S(2)}) collective-permute-start(f32[160,128]{1,0:T(8,128)S(1)} %get-tuple-element.32.state_ref), channel_id=1, source_target_pairs={{0,1},{1,2},{2,3},{3,0},{4,5},{5,6},{6,7},{7,4},{8,9},{9,10},{10,1... | collective-permute-start | bytes 245768 | tf_op jit(solution)/shard_map/ppermute | solution.py:292
  95.3 5.2 %collective-permute-start.8 = (f32[160,128]{1,0:T(8,128)S(1)}, f32[160,128]{1,0:T(8,128)S(1)}, u32[]{:S(2)}, u32[]{:S(2)}) collective-permute-start(f32[160,128]{1,0:T(8,128)S(1)} %get-tuple-element.32.state_ref), channel_id=1, source_target_pairs={{0,2},{1,3},{2,0},{3,1},{4,6},{5,7},{6,4},{7,5},{8,10},{9,11},{10,... | collective-permute-start | bytes 245768 | tf_op jit(solution)/shard_map/ppermute | solution.py:292
  100.5 2.7 %collective-permute-start.9 = (f32[160,128]{1,0:T(8,128)S(1)}, f32[160,128]{1,0:T(8,128)S(1)}, u32[]{:S(2)}, u32[]{:S(2)}) collective-permute-start(f32[160,128]{1,0:T(8,128)S(1)} %get-tuple-element.32.state_ref), channel_id=1, source_target_pairs={{0,3},{1,0},{2,1},{3,2},{4,7},{5,4},{6,5},{7,6},{8,11},{9,8},{10,9... | collective-permute-start | bytes 245768 | tf_op jit(solution)/shard_map/ppermute | solution.py:292
  103.2 1.1 prepare.1
  104.3 1.2 copy-done.8
  106.5 2.8 %all-to-all-done.2 = f32[256,1,640]{2,1,0:T(1,128)S(1)} async-done(((f32[256,1,640]{2,1,0:T(1,128)}), f32[256,1,640]{2,1,0:T(1,128)S(1)}, u32[]{:S(2)}, u32[]{:S(2)}) %all-to-all-start.2) | async-done | bytes 655392 | tf_op jit(solution)/shard_map/all_to_all | solution.py:359
  109.3 5.6 %collective-permute-start.10 = (f32[1280,128]{1,0:T(8,128)S(1)}, f32[1280,128]{1,0:T(8,128)S(1)}, u32[]{:S(2)}, u32[]{:S(2)}) collective-permute-start(f32[1280,128]{1,0:T(8,128)S(1)} %bitcast.11), channel_id=1, source_target_pairs={{0,4},{4,0},{1,5},{5,1},{2,6},{6,2},{3,7},{7,3},{8,12},{12,8},{9,1... | collective-permute-start | bytes 1966088 | tf_op jit(solution)/shard_map/ppermute | solution.py:284
  114.9 1.7 %collective-permute-done.10.prior_o_ref = f32[1280,128]{1,0:T(8,128)S(1)} collective-permute-done((f32[1280,128]{1,0:T(8,128)S(1)}, f32[1280,128]{1,0:T(8,128)S(1)}, u32[]{:S(2)}, u32[]{:S(2)}) %collective-permute-start.10) | collective-permute-done | bytes 655392 | tf_op jit(solution)/shard_map/ppermute | solution.py:284
  116.6 1.4 copy-done.9
  118.1 24.8 %filter.1 = f32[160,128]{1,0:T(8,128)} custom-call(s32[4]{0:T(128)S(1)} %copy-done.7, f32[1280,128]{1,0:T(8,128)S(1)} %bitcast.12, f32[1280,128]{1,0:T(8,128)S(1)} %collective-permute-done.10.prior_o_ref, bf16[24,256,128]{2,1,0:T(8,128)(2,1)S(1)} %get-tuple-element.34.tapers, bf16[3072,256]{1,0:T(8,128)(2,1)S(1)} %copy-done.9, f32[4,1024]{1,0:T(4,128)S(1)} %bitcast.15, ...), custom_call_target="tpu_custom_call" | custom-call | flops 3000000000 | bytes 4000000 | tf_op jit(solution)/shard_map/filter/pallas_call | solution.py:365
  (41 shorter events, 9.4 us)
Async XLA Ops:
  0.0 0.7 copy-start.3
  2.7 40.5 %all-to-all-start = ((f32[64,1,768]{2,1,0:T(1,128)}), f32[64,1,768]{2,1,0:T(1,128)S(1)}, u32[]{:S(2)}, u32[]{:S(2)}) async-start(f32[64,1,768]{2,1,0:T(1,128)} %bitcast.2), calls=%async_computation | async-start | bytes 393216 | tf_op jit(solution)/shard_map/all_to_all | solution.py:307
  21.5 8.6 %collective-permute-start = (f32[22,2,2,128]{3,2,1,0:T(2,128)S(1)}, f32[22,2,2,128]{3,2,1,0:T(2,128)S(1)}, u32[]{:S(2)}, u32[]{:S(2)}) collective-permute-start(f32[22,2,2,128]{3,2,1,0:T(2,128)S(1)} %get-tuple-element.39), channel_id=1, source_target_pairs={{0,8},{8,16},{16,24},{24,32},{32,40},{40,48},{48,56},{56,64},{64,7... | collective-permute-start | bytes 135176 | tf_op jit(solution)/shard_map/ppermute | solution.py:314
  24.4 6.8 %collective-permute-start.1 = (f32[22,2,2,128]{3,2,1,0:T(2,128)S(1)}, f32[22,2,2,128]{3,2,1,0:T(2,128)S(1)}, u32[]{:S(2)}, u32[]{:S(2)}) collective-permute-start(f32[22,2,2,128]{3,2,1,0:T(2,128)S(1)} %get-tuple-element.40), channel_id=1, source_target_pairs={{0,504},{8,0},{16,8},{24,16},{32,24},{40,32},{48,40},{56,48},{64,5... | collective-permute-start | bytes 135176 | tf_op jit(solution)/shard_map/ppermute | solution.py:315
  31.3 5.0 %collective-permute-start.2 = (f32[352,128]{1,0:T(8,128)S(1)}, f32[352,128]{1,0:T(8,128)S(1)}, u32[]{:S(2)}, u32[]{:S(2)}) collective-permute-start(f32[352,128]{1,0:T(8,128)S(1)} %bitcast.9), channel_id=1, source_target_pairs={{0,4},{4,0},{1,5},{5,1},{2,6},{6,2},{3,7},{7,3},{8,12},{12,8},{9,1... | collective-permute-start | bytes 540680 | tf_op jit(solution)/shard_map/ppermute | solution.py:284
  36.3 0.7 copy-start
  37.0 0.7 copy-start.2
  43.2 26.6 %all-to-all-start.1 = ((f32[64,1,640]{2,1,0:T(1,128)}), f32[64,1,640]{2,1,0:T(1,128)S(1)}, u32[]{:S(2)}, u32[]{:S(2)}) async-start(f32[64,1,640]{2,1,0:T(1,128)} %bitcast.4), calls=%async_computation.1 | async-start | bytes 327680 | tf_op jit(solution)/shard_map/all_to_all | solution.py:334
  54.4 10.6 %collective-permute-start.3 = (f32[384,128]{1,0:T(8,128)S(1)}, f32[384,128]{1,0:T(8,128)S(1)}, u32[]{:S(2)}, u32[]{:S(2)}) collective-permute-start(f32[384,128]{1,0:T(8,128)S(1)} %bitcast.16), channel_id=1, source_target_pairs={{0,1},{1,2},{2,3},{3,0},{4,5},{5,6},{6,7},{7,4},{8,9},{9,10},{10,1... | collective-permute-start | bytes 589832 | tf_op jit(solution)/shard_map/ppermute | solution.py:292
  57.5 11.0 %collective-permute-start.4 = (f32[384,128]{1,0:T(8,128)S(1)}, f32[384,128]{1,0:T(8,128)S(1)}, u32[]{:S(2)}, u32[]{:S(2)}) collective-permute-start(f32[384,128]{1,0:T(8,128)S(1)} %bitcast.17), channel_id=1, source_target_pairs={{0,2},{1,3},{2,0},{3,1},{4,6},{5,7},{6,4},{7,5},{8,10},{9,11},{10,... | collective-permute-start | bytes 589832 | tf_op jit(solution)/shard_map/ppermute | solution.py:292
  61.9 7.9 %collective-permute-start.5 = (f32[384,128]{1,0:T(8,128)S(1)}, f32[384,128]{1,0:T(8,128)S(1)}, u32[]{:S(2)}, u32[]{:S(2)}) collective-permute-start(f32[384,128]{1,0:T(8,128)S(1)} %bitcast.18), channel_id=1, source_target_pairs={{0,3},{1,0},{2,1},{3,2},{4,7},{5,4},{6,5},{7,6},{8,11},{9,8},{10,9... | collective-permute-start | bytes 589832 | tf_op jit(solution)/shard_map/ppermute | solution.py:292
  70.7 32.4 %copy-start.1 = (s32[4,1024]{1,0:T(4,128)S(1)}, s32[4,1024]{1,0:T(4,128)}, u32[]{:S(2)}) copy-start(s32[4,1024]{1,0:T(4,128)} %region_ref.3) | copy-start | bytes 49156
  70.7 32.5 %copy-start.7 = (s32[4]{0:T(128)S(1)}, s32[4]{0:T(128)}, u32[]{:S(2)}) copy-start(s32[4]{0:T(128)} %order.7) | copy-start | bytes 52
  70.7 38.6 %all-to-all-start.2 = ((f32[256,1,640]{2,1,0:T(1,128)}), f32[256,1,640]{2,1,0:T(1,128)S(1)}, u32[]{:S(2)}, u32[]{:S(2)}) async-start(f32[256,1,640]{2,1,0:T(1,128)} %bitcast.6), calls=%async_computation.2 | async-start | bytes 1310720 | tf_op jit(solution)/shard_map/all_to_all | solution.py:359
  89.3 27.3 %copy-start.4 = (f32[1,1,4,1024]{3,2,1,0:T(4,128)S(1)}, f32[1,1,4,1024]{3,2,1,0:T(4,128)}, u32[]{:S(2)}) copy-start(f32[1,1,4,1024]{3,2,1,0:T(4,128)} %param.15) | copy-start | bytes 49156
  89.4 27.3 %copy-start.10 = (f32[4,1024]{1,0:T(4,128)S(1)}, f32[4,1024]{1,0:T(4,128)}, u32[]{:S(2)}) copy-start(f32[4,1024]{1,0:T(4,128)} %value_ref.1) | copy-start | bytes 49156
  89.4 27.3 %copy-start.11 = (f32[4,1024]{1,0:T(4,128)S(1)}, f32[4,1024]{1,0:T(4,128)}, u32[]{:S(2)}) copy-start(f32[4,1024]{1,0:T(4,128)} %var_ref.1) | copy-start | bytes 49156
  89.5 13.7 %collective-permute-start.6 = (f32[1536,128]{1,0:T(8,128)S(1)}, f32[1536,128]{1,0:T(8,128)S(1)}, u32[]{:S(2)}, u32[]{:S(2)}) collective-permute-start(f32[1536,128]{1,0:T(8,128)S(1)} %constant_dynamic-update-slice_fusion.2.taper_ref), channel_id=1, source_target_pairs={{0,4},{4,0},{1,5},{5,1},{2,6},{6,2},{3,7},{7,3},{8,12},{12,8},{9,1... | collective-permute-start | bytes 2359304 | tf_op jit(solution)/shard_map/ppermute | solution.py:284
  93.1 12.4 %collective-permute-start.7 = (f32[160,128]{1,0:T(8,128)S(1)}, f32[160,128]{1,0:T(8,128)S(1)}, u32[]{:S(2)}, u32[]{:S(2)}) collective-permute-start(f32[160,128]{1,0:T(8,128)S(1)} %get-tuple-element.32.state_ref), channel_id=1, source_target_pairs={{0,1},{1,2},{2,3},{3,0},{4,5},{5,6},{6,7},{7,4},{8,9},{9,10},{10,1... | collective-permute-start | bytes 245768 | tf_op jit(solution)/shard_map/ppermute | solution.py:292
  95.3 10.3 %collective-permute-start.8 = (f32[160,128]{1,0:T(8,128)S(1)}, f32[160,128]{1,0:T(8,128)S(1)}, u32[]{:S(2)}, u32[]{:S(2)}) collective-permute-start(f32[160,128]{1,0:T(8,128)S(1)} %get-tuple-element.32.state_ref), channel_id=1, source_target_pairs={{0,2},{1,3},{2,0},{3,1},{4,6},{5,7},{6,4},{7,5},{8,10},{9,11},{10,... | collective-permute-start | bytes 245768 | tf_op jit(solution)/shard_map/ppermute | solution.py:292
  100.5 6.1 %collective-permute-start.9 = (f32[160,128]{1,0:T(8,128)S(1)}, f32[160,128]{1,0:T(8,128)S(1)}, u32[]{:S(2)}, u32[]{:S(2)}) collective-permute-start(f32[160,128]{1,0:T(8,128)S(1)} %get-tuple-element.32.state_ref), channel_id=1, source_target_pairs={{0,3},{1,0},{2,1},{3,2},{4,7},{5,4},{6,5},{7,6},{8,11},{9,8},{10,9... | collective-permute-start | bytes 245768 | tf_op jit(solution)/shard_map/ppermute | solution.py:292
  104.3 1.2 copy-start.8
  109.3 7.3 %collective-permute-start.10 = (f32[1280,128]{1,0:T(8,128)S(1)}, f32[1280,128]{1,0:T(8,128)S(1)}, u32[]{:S(2)}, u32[]{:S(2)}) collective-permute-start(f32[1280,128]{1,0:T(8,128)S(1)} %bitcast.11), channel_id=1, source_target_pairs={{0,4},{4,0},{1,5},{5,1},{2,6},{6,2},{3,7},{7,3},{8,12},{12,8},{9,1... | collective-permute-start | bytes 1966088 | tf_op jit(solution)/shard_map/ppermute | solution.py:284
  116.6 1.4 copy-start.9
  (2 other events, 1.3 us)

commit v3 on v2

--- a/solution.py
+++ b/solution.py
@@ -18,6 +18,7 @@
 CHUNK = 5
 HALF = OWN * 2 * GROUPS
 QUARTER = (BLOCKS - 1) * GROUPS // MA
+SENT = CHUNK + QUARTER
 ROWS_O = 256
 F32 = jnp.float32
 BF16 = jnp.bfloat16
@@ -45,8 +46,7 @@
     return row
 
 
-def advect_kernel(order, own_ref, other_ref, cell_ref, region_ref, state_ref, picked_ref, work):
-    gx, gy = lax.axis_index("gx"), lax.axis_index("gy")
+def advect_kernel(own_ref, other_ref, index_ref, state_ref, picked_ref, work):
     lane = lax.broadcasted_iota(jnp.int32, (8, LANES), 1)
     first, last = lane == 0, lane == LANES - 1
 
@@ -83,59 +83,55 @@
             work[0, at, :] = twice[2:6]
             work[1, at, :] = twice_o[2:6]
 
+    for g in range(2 * GROUPS):
+        y = jnp.broadcast_to(index_ref[pl.ds(g, 1), :].astype(jnp.int32), (24, LANES))
+        part = jnp.broadcast_to(index_ref[pl.ds(g + 16, 1), :].astype(jnp.int32), (24, LANES))
+        total = jnp.zeros((24, LANES), F32)
+        for c in range(16):
+            source = work[c // 8, pl.ds(c % 8, 24, stride=8), :]
+            found = jnp.take_along_axis(source, y, axis=1, mode="promise_in_bounds")
+            total = jnp.where(part == c, found, total)
+        for i in range(MA):
+            at = (i * 2 * GROUPS + g) * CHUNK
+            picked_ref[pl.ds(at, CHUNK), :] = total[i * CHUNK : (i + 1) * CHUNK]
+
+
+def prepare_kernel(*refs):
+    sources, results, copies, done = refs[:6], refs[6:9], refs[9:15], refs[15]
+    moves = [
+        pltpu.make_async_copy(source, copy, done.at[i])
+        for i, (source, copy) in enumerate(zip(sources, copies))
+    ]
+    for move in moves:
+        move.start()
+    for move in moves:
+        move.wait()
+    order, cell_ref, region_ref, value_ref, var_ref, taper_ref = copies
+    index_ref, obs_ref, onehots = results
+    gx, gy, q = lax.axis_index("gx"), lax.axis_index("gy"), lax.axis_index("ma")
     for k in range(2):
         b = order[gy * 2 + k]
         for g in range(GROUPS):
             columns = pl.ds(g * LANES, LANES)
             cell, region = block_row(cell_ref, b, columns), block_row(region_ref, b, columns)
-            y = jnp.broadcast_to(jnp.bitwise_and(cell, LANES - 1), (24, LANES))
             part = jnp.right_shift(cell, 7) + jnp.where(jnp.bitwise_and(region, 1) == gy, 0, 8)
             part = jnp.where(jnp.right_shift(region, 1) == gx, part, -1)
-            part = jnp.broadcast_to(part, (24, LANES))
-            total = jnp.zeros((24, LANES), F32)
-            for c in range(16):
-                source = work[c // 8, pl.ds(c % 8, 24, stride=8), :]
-                found = jnp.take_along_axis(source, y, axis=1)
-                total = jnp.where(part == c, found, total)
-            picked_ref[pl.ds(k * GROUPS + g, OWN, stride=16), :] = total[:OWN]
-
-
-def send_kernel(order, taper_ref, out_ref):
-    q = lax.axis_index("ma")
-    pieces = []
+            at = k * GROUPS + g
+            index_ref[pl.ds(at, 1), :] = jnp.bitwise_and(cell, LANES - 1).astype(F32)
+            index_ref[pl.ds(at + 16, 1), :] = part.astype(F32)
+
+    for k in range(BLOCKS):
+        for i, ref in enumerate((value_ref, var_ref, taper_ref)):
+            obs_ref[pl.ds(i * BLOCKS + k, 1), :] = block_row(ref, order[k], pl.ds(0, OBS))
+
+    index_ref[pl.ds(32, 8), :] = jnp.zeros((8, LANES), F32)
     for i in range(QUARTER):
         tile = q * QUARTER + i
         b, g = order[tile // GROUPS], tile % GROUPS
         row = block_row(taper_ref, b, pl.ds(0, LANES))
         for j in range(1, GROUPS):
             row = jnp.where(g == j, block_row(taper_ref, b, pl.ds(j * LANES, LANES)), row)
-        pieces.append(row)
-    four = jnp.concatenate(pieces * 4, axis=0)
-    for i in range(GX // 4):
-        out_ref[pl.ds(i * 4 * QUARTER, 4 * QUARTER), :] = four
-
-
-def owner_kernel(parts_ref, out_ref):
-    total = parts_ref[pl.ds(0, 40), :]
-    for i in range(1, GX // 8):
-        total = total + parts_ref[pl.ds(i * 40, 40), :]
-    part = total[0:CHUNK]
-    for i in range(1, 8):
-        part = part + total[i * CHUNK : (i + 1) * CHUNK]
-    eight = jnp.concatenate([part] * 8, axis=0)
-    for i in range(GX * MA // 8):
-        out_ref[pl.ds(i * 40, 40), :] = eight
-
-
-def prepare_kernel(order, taper_ref, taper_o_ref, region_ref, tapers, onehots):
-    q, gy = lax.axis_index("ma"), lax.axis_index("gy")
-    for shift in range(MA):
-        for i in range(QUARTER):
-            tile = lax.rem(q - shift + MA, MA) * QUARTER + i
-            for side, ref in enumerate((taper_ref, taper_o_ref)):
-                high, low = split(ref[pl.ds(shift * GX * QUARTER + i, GX, stride=QUARTER), :])
-                tapers[tile, pl.ds(side * GX, GX), :] = high
-                tapers[tile, pl.ds(LANES + side * GX, GX), :] = low
+        index_ref[pl.ds(32 + i, 1), :] = row
 
     rows = lax.broadcasted_iota(jnp.int32, (LANES, LANES), 0)
     for k in range(1, BLOCKS):
@@ -149,21 +145,30 @@
             onehots[at, pl.ds(LANES, LANES)] = hot
 
 
+def owner_kernel(parts_ref, index_ref, out_ref):
+    total = parts_ref[pl.ds(0, 40), :]
+    for i in range(1, GX // 8):
+        total = total + parts_ref[pl.ds(i * 40, 40), :]
+    part = total[0:CHUNK]
+    for i in range(1, 8):
+        part = part + total[i * CHUNK : (i + 1) * CHUNK]
+    eight = jnp.concatenate([part, index_ref[pl.ds(32, QUARTER), :]] * 8, axis=0)
+    for i in range(GX * MA // 8):
+        out_ref[pl.ds(i * 8 * SENT, 8 * SENT), :] = eight
+
+
 def filter_kernel(
-    order,
-    prior_ref,
-    prior_o_ref,
-    tapers,
+    came_ref,
+    came_o_ref,
     onehots,
-    taper_own_ref,
-    value_ref,
-    var_ref,
+    obs_ref,
     gathered_1,
     gathered_2,
     gathered_3,
     state_ref,
     out_ref,
     xt,
+    tapers,
     b_high,
     b_both,
     increments,
@@ -173,7 +178,9 @@
 
     def load_half(ref, half):
         for g in range(16):
-            block = ref[pl.ds(g, MEMBERS, stride=16), :]
+            block = jnp.concatenate(
+                [ref[pl.ds(g * SENT + i, 16, stride=16 * SENT), :] for i in range(CHUNK)], axis=0
+            )
             mean = jnp.mean(block, axis=0, keepdims=True)
             full = jnp.concatenate(
                 [block - mean, mean, jnp.zeros((LANES - MEMBERS - 1, LANES), F32)], axis=0
@@ -182,34 +189,40 @@
 
     @pl.when(gy == 0)
     def _():
-        load_half(prior_ref, 0)
-        load_half(prior_o_ref, 1)
+        load_half(came_ref, 0)
+        load_half(came_o_ref, 1)
 
     @pl.when(gy == 1)
     def _():
-        load_half(prior_o_ref, 0)
-        load_half(prior_ref, 1)
+        load_half(came_o_ref, 0)
+        load_half(came_ref, 1)
+
+    for tile in range((BLOCKS - 1) * GROUPS):
+        at = pl.ds(tile // QUARTER * GX * SENT + CHUNK + tile % QUARTER, GX, stride=SENT)
+        for side, ref in enumerate((came_ref, came_o_ref)):
+            high, low = split(ref[at, :])
+            tapers[tile, pl.ds(side * GX, GX), :] = high
+            tapers[tile, pl.ds(LANES + side * GX, GX), :] = low
 
     lane = lax.broadcasted_iota(jnp.int32, (ROWS_O, LANES), 1)
     member_row = lax.broadcasted_iota(jnp.int32, (LANES, OBS), 0)
     increments[...] = jnp.zeros((LANES, LANES), F32)
     for k in range(BLOCKS):
-        b = order[k]
         now = jnp.concatenate(
             [xt[pl.ds((k * GROUPS + g) * LANES, LANES), :].T for g in range(GROUPS)], axis=1
         )
         anomaly = jnp.where(member_row < MEMBERS, now, 0.0)
         mean = now[MEMBERS : MEMBERS + 1]
         variance = jnp.sum(anomaly * anomaly, axis=0, keepdims=True) / denom
-        error_var = block_row(var_ref, b, pl.ds(0, OBS))
+        error_var = obs_ref[pl.ds(BLOCKS + k, 1), :]
         total_var = variance + error_var
         shrink = 1.0 / (1.0 + jnp.sqrt(error_var / total_var))
         scale = 1.0 / (denom * total_var)
-        gain_mean = (block_row(value_ref, b, pl.ds(0, OBS)) - mean) * scale
+        gain_mean = (obs_ref[pl.ds(k, 1), :] - mean) * scale
         gain = jnp.where(member_row == MEMBERS, gain_mean, -(shrink * scale) * anomaly)
         gain_high, gain_low = split(gain)
 
-        tapered_high, tapered_low = split(anomaly * block_row(taper_own_ref, b, pl.ds(0, OBS)))
+        tapered_high, tapered_low = split(anomaly * obs_ref[pl.ds(2 * BLOCKS + k, 1), :])
         mixing = (
             dot_nt(gain_high, tapered_high)
             + dot_nt(gain_low, tapered_high)
@@ -256,12 +269,16 @@
     total = e + e[MEMBERS : MEMBERS + 1]
     row = lax.broadcasted_iota(jnp.int32, (24, LANES), 0)
     col = lax.broadcasted_iota(jnp.int32, (24, LANES), 1)
-    chosen = jnp.where((col == row + q * OWN) & (row < OWN), 1.0, 0.0)
+    fifth = sum(jnp.where(row >= i * CHUNK, 1, 0) for i in range(1, MA))
+    member = (row - fifth * CHUNK) * 16 + q * MA + fifth
+    chosen = jnp.where((col == member) & (row < OWN), 1.0, 0.0)
     transform = jnp.dot(chosen, total, precision=lax.Precision.HIGHEST, preferred_element_type=F32)
     row = lax.broadcasted_iota(jnp.int32, (LANES, LANES), 0)
     col = lax.broadcasted_iota(jnp.int32, (LANES, LANES), 1)
     back = sum(jnp.where(col >= i * OWN, 1, 0) for i in range(1, MA))
-    member = jnp.bitwise_and(q - back, MA - 1) * OWN + col - back * OWN
+    place = col - back * OWN
+    fifth = sum(jnp.where(place >= i * CHUNK, 1, 0) for i in range(1, MA))
+    member = (place - fifth * CHUNK) * 16 + jnp.bitwise_and(q - back, MA - 1) * MA + fifth
     shuffle = jnp.where((row == member) & (col < MEMBERS), 1.0, 0.0)
     transform = jnp.dot(transform, shuffle, precision=lax.Precision.HIGHEST, preferred_element_type=F32)
     tiles = []
@@ -295,24 +312,30 @@
 def local(
     ensemble, wind_field, obs_value, obs_var, obs_region, obs_cell, block_order, localization
 ):
-    taper_own = localization.reshape(BLOCKS, OBS)
-    taper_send = pl.pallas_call(
-        send_kernel,
-        out_shape=jax.ShapeDtypeStruct((GX * QUARTER, LANES), F32),
-        in_specs=[SMEM, VMEM],
-        out_specs=VMEM,
-        compiler_params=params(2),
-        name="send",
-    )(block_order, taper_own)
-    tapers = lax.all_to_all(
-        taper_send.reshape(GX, 1, QUARTER * LANES), "gx", 0, 0, tiled=True
-    ).reshape(-1, LANES)
-
     both = jnp.concatenate([ensemble, wind_field], axis=0)
     forward = [(i, (i + 1) % GX) for i in range(GX)]
     backward = [(i, (i - 1) % GX) for i in range(GX)]
     low = lax.ppermute(both[:, :, 2:], "gx", forward)
     high = lax.ppermute(both[:, :, :2], "gx", backward)
+    prepared = pl.pallas_call(
+        prepare_kernel,
+        out_shape=(
+            jax.ShapeDtypeStruct((40, LANES), F32),
+            jax.ShapeDtypeStruct((3 * BLOCKS, OBS), F32),
+            jax.ShapeDtypeStruct(((BLOCKS - 1) * OBS, 2 * LANES), BF16),
+        ),
+        in_specs=[pl.BlockSpec(memory_space=pltpu.HBM)] * 6,
+        out_specs=(VMEM,) * 3,
+        scratch_shapes=[pltpu.SMEM((BLOCKS,), jnp.int32)]
+        + [pltpu.VMEM((BLOCKS, OBS), jnp.int32)] * 2
+        + [pltpu.VMEM((BLOCKS, OBS), F32)] * 3
+        + [pltpu.SemaphoreType.DMA((6,))],
+        compiler_params=params(60),
+        cost_estimate=pl.CostEstimate(flops=10_000_000, bytes_accessed=2_000_000, transcendentals=0),
+        name="prepare",
+    )(block_order, obs_cell, obs_region, obs_value, obs_var, localization.reshape(BLOCKS, OBS))
+    low, high, prepared = lax.optimization_barrier((low, high, prepared))
+    index, observed, onehots = prepared
     own = jnp.concatenate([low, both, high], axis=2).reshape(-1, LANES)
     beside = other_core(own)
 
@@ -322,53 +345,38 @@
             jax.ShapeDtypeStruct((OWN * 8, LANES), F32),
             jax.ShapeDtypeStruct((HALF, LANES), F32),
         ),
-        in_specs=[SMEM, VMEM, VMEM, VMEM, VMEM],
+        in_specs=[VMEM] * 3,
         out_specs=(VMEM, VMEM),
         scratch_shapes=[pltpu.VMEM((2, 24 * 8, LANES), F32)],
         compiler_params=params(4),
         cost_estimate=pl.CostEstimate(flops=10_000_000, bytes_accessed=1_000_000, transcendentals=0),
         name="advect",
-    )(block_order, own, beside, obs_cell, obs_region)
-
-    picked, tapers = lax.optimization_barrier((picked, tapers))
+    )(own, beside, index)
+
     parts = lax.all_to_all(picked.reshape(GX, 1, CHUNK * LANES), "gx", 0, 0, tiled=True)
-    parts, tapers = lax.optimization_barrier((parts, [tapers] + over_members(tapers)))
-    tapers = jnp.concatenate(tapers, axis=0)
-    tapers_beside = other_core(tapers)
     gathered = over_members(state)
-    prepared = pl.pallas_call(
-        prepare_kernel,
-        out_shape=(
-            jax.ShapeDtypeStruct(((BLOCKS - 1) * GROUPS, 2 * LANES, LANES), BF16),
-            jax.ShapeDtypeStruct(((BLOCKS - 1) * OBS, 2 * LANES), BF16),
-        ),
-        in_specs=[SMEM, VMEM, VMEM, VMEM],
-        out_specs=(VMEM, VMEM),
-        compiler_params=params(8),
-        cost_estimate=pl.CostEstimate(flops=10_000_000, bytes_accessed=5_000_000, transcendentals=0),
-        name="prepare",
-    )(block_order, tapers, tapers_beside, obs_region)
     owned = pl.pallas_call(
         owner_kernel,
-        out_shape=jax.ShapeDtypeStruct((MA * GX * CHUNK, LANES), F32),
-        in_specs=[VMEM],
+        out_shape=jax.ShapeDtypeStruct((MA * GX * SENT, LANES), F32),
+        in_specs=[VMEM, VMEM],
         out_specs=VMEM,
         compiler_params=params(4),
         name="owner",
-    )(parts.reshape(-1, LANES))
-    priors = lax.all_to_all(
-        owned.reshape(MA * GX, 1, CHUNK * LANES), ("ma", "gx"), 0, 0, tiled=True
+    )(parts.reshape(-1, LANES), index)
+    came = lax.all_to_all(
+        owned.reshape(MA * GX, 1, SENT * LANES), ("ma", "gx"), 0, 0, tiled=True
     ).reshape(-1, LANES)
-    priors, prepared, gathered = lax.optimization_barrier((priors, prepared, gathered))
-    priors_beside = other_core(priors)
+    came, gathered = lax.optimization_barrier((came, gathered))
+    came_beside = other_core(came)
 
     out = pl.pallas_call(
         filter_kernel,
         out_shape=jax.ShapeDtypeStruct((OWN * 8, LANES), F32),
-        in_specs=[SMEM] + [VMEM] * 11,
+        in_specs=[VMEM] * 8,
         out_specs=VMEM,
         scratch_shapes=[
             pltpu.VMEM((BLOCKS * OBS, LANES), F32),
+            pltpu.VMEM(((BLOCKS - 1) * GROUPS, 2 * LANES, LANES), BF16),
             pltpu.VMEM((OBS, LANES), BF16),
             pltpu.VMEM((OBS, 2 * LANES), BF16),
             pltpu.VMEM((LANES, LANES), F32),
@@ -376,17 +384,7 @@
         compiler_params=params(32),
         cost_estimate=pl.CostEstimate(flops=3_000_000_000, bytes_accessed=4_000_000, transcendentals=0),
         name="filter",
-    )(
-        block_order,
-        priors,
-        priors_beside,
-        *prepared,
-        taper_own,
-        obs_value,
-        obs_var,
-        *gathered,
-        state,
-    )
+    )(came, came_beside, onehots, observed, *gathered, state)
     return out.reshape(ensemble.shape)
 
 

time: 144 us -> 132 us (0.917)
  starting transfers between devices: 89.3 us -> 44.8 us
  waiting for transfers between devices: 12.5 us -> 36.1 us
  blocking collectives: 0 us -> 16.3 us
  local copies, waits for them, and re-layouts: 7.78 us -> 2.37 us
    all_to_all x3 -> x1, starting transfers between devices: 46.9 us -> 11.1 us  [local(): lax.all_to_all(owned.reshape(MA * GX, 1, SENT * LANES), ('ma', 'gx'), 0,...]
    all_to_all x3 -> x1, waiting for transfers between devices: 2.77 us -> 21.3 us  [local(): lax.all_to_all(owned.reshape(MA * GX, 1, SENT * LANES), ('ma', 'gx'), 0,...]
    all_to_all x0 -> x1, blocking collectives: none -> 16.3 us  [local(): lax.all_to_all(picked.reshape(GX, 1, CHUNK * LANES), 'gx', 0, 0, tiled=True)]
    ppermute x6 -> x3, starting transfers between devices: 20.6 us -> 8.54 us  [over_members(): lax.ppermute(x, 'ma', [(i, (i + s) % MA) for i in range(MA)])]
    ppermute x1, starting transfers between devices: 5.68 us -> 14.4 us  [local(): high = lax.ppermute(both[:, :, :2], 'gx', backward)]
    unnamed x28 -> x7, local copies, waits for them, and re-layouts: 7.02 us -> 1.63 us
    ppermute x3 -> x2, starting transfers between devices: 13.2 us -> 8.85 us  [other_core(): return lax.ppermute(x, 'gy', [(0, 1), (1, 0)])]
    ppermute x1, waiting for transfers between devices: 0.03 us -> 3.75 us  [local(): low = lax.ppermute(both[:, :, 2:], 'gx', forward)]
  transfers between devices with their start and end apart: 14 -> 8, of which waited for: 8 -> 6; matrix products, arithmetic and copies ran while one was open for 1% -> 0% of each run, Pallas kernels for 4% -> 2%
where the time goes in v3:
time: 132 us; the launch traced here: 131 us
  starting transfers between devices  44.8 us (34%)
  waiting for transfers between devices  36.1 us (27%)
  Pallas kernels  31.5 us (24%)
  blocking collectives  16.3 us (12%)
  local copies, waits for them, and re-layouts  2.37 us (2%)
    pallas_call x1, Pallas kernels, local(): pl.pallas_call(filter_kernel, out_shape=jax.ShapeDtypeStruct((OWN * 8, LA...  24.2 us
    all_to_all x1, waiting for transfers between devices, local(): lax.all_to_all(owned.reshape(MA * GX, 1, SENT * LANES), ('ma', 'gx'), 0,...  21.3 us
    all_to_all x1, blocking collectives, local(): lax.all_to_all(picked.reshape(GX, 1, CHUNK * LANES), 'gx', 0, 0, tiled=True)  16.3 us
    ppermute x1, starting transfers between devices, local(): high = lax.ppermute(both[:, :, :2], 'gx', backward)  14.4 us
    all_to_all x1, starting transfers between devices, local(): lax.all_to_all(owned.reshape(MA * GX, 1, SENT * LANES), ('ma', 'gx'), 0,...  11.1 us
    ppermute x2, starting transfers between devices, other_core(): return lax.ppermute(x, 'gy', [(0, 1), (1, 0)])  8.85 us
    ppermute x3, starting transfers between devices, over_members(): lax.ppermute(x, 'ma', [(i, (i + s) % MA) for i in range(MA)])  8.54 us
    ppermute x3, waiting for transfers between devices, over_members(): lax.ppermute(x, 'ma', [(i, (i + s) % MA) for i in range(MA)])  7.26 us
  transfers between devices with their start and end apart: 8, of which 6 were waited for; matrix products, arithmetic and copies ran while one was open for 0% of the time, Pallas kernels for 2%

profile of v3, /device:TPU:1, one launch (start us, length us, event | category | flops | bytes accessed | tf_op | source)
XLA Modules:
  0.0 131.2 jit_solution(5313680037891361418)
XLA Ops:
  0.0 0.9 constant_dynamic-update-slice_fusion.1
  0.9 0.7 constant_dynamic-update-slice_fusion
  1.6 14.4 %collective-permute-start.1 = (f32[22,2,2,128]{3,2,1,0:T(2,128)S(1)}, f32[22,2,2,128]{3,2,1,0:T(2,128)S(1)}, u32[]{:S(2)}, u32[]{:S(2)}) collective-permute-start(f32[22,2,2,128]{3,2,1,0:T(2,128)S(1)} %get-tuple-element.33), channel_id=1, source_target_pairs={{0,504},{8,0},{16,8},{24,16},{32,24},{40,32},{48,40},{56,48},{64,5... | collective-permute-start | bytes 135176 | tf_op jit(solution)/shard_map/ppermute | solution.py:319
  16.0 1.9 %collective-permute-start = (f32[22,2,2,128]{3,2,1,0:T(2,128)S(1)}, f32[22,2,2,128]{3,2,1,0:T(2,128)S(1)}, u32[]{:S(2)}, u32[]{:S(2)}) collective-permute-start(f32[22,2,2,128]{3,2,1,0:T(2,128)S(1)} %get-tuple-element.34), channel_id=1, source_target_pairs={{0,8},{8,16},{16,24},{24,32},{32,40},{40,48},{48,56},{56,64},{64,7... | collective-permute-start | bytes 135176 | tf_op jit(solution)/shard_map/ppermute | solution.py:318
  18.0 2.4 %prepare.1 = (f32[40,128]{1,0:T(8,128)}, f32[12,1024]{1,0:T(8,128)}, bf16[3072,256]{1,0:T(8,128)(2,1)}) custom-call(s32[4]{0:T(128)} %refs_0_.1, s32[4,1024]{1,0:T(4,128)} %refs_1_.1, s32[4,1024]{1,0:T(4,128)} %refs_2_.1, f32[4,1024]{1,0:T(4,128)} %refs_3_.1, f32[4,1024]{1,0:T(4,128)} %refs_4_.1, f32[4,1024]{1,0:T(4,128)} %bitcast.13), custom_call_target="tpu_custom_call" | custom-call | flops 10000000 | bytes 2000000 | tf_op jit(solution)/shard_map/prepare/pallas_call | solution.py:320
  20.4 0.0 collective-permute-done.1
  20.4 3.8 %collective-permute-done = f32[22,2,2,128]{3,2,1,0:T(2,128)S(1)} collective-permute-done((f32[22,2,2,128]{3,2,1,0:T(2,128)S(1)}, f32[22,2,2,128]{3,2,1,0:T(2,128)S(1)}, u32[]{:S(2)}, u32[]{:S(2)}) %collective-permute-start) | collective-permute-done | bytes 45088 | tf_op jit(solution)/shard_map/ppermute | solution.py:318
  24.2 0.1 pad_maximum_fusion
  24.2 4.0 %collective-permute-start.2 = (f32[352,128]{1,0:T(8,128)S(1)}, f32[352,128]{1,0:T(8,128)S(1)}, u32[]{:S(2)}, u32[]{:S(2)}) collective-permute-start(f32[352,128]{1,0:T(8,128)S(1)} %bitcast.9), channel_id=1, source_target_pairs={{0,4},{4,0},{1,5},{5,1},{2,6},{6,2},{3,7},{7,3},{8,12},{12,8},{9,1... | collective-permute-start | bytes 540680 | tf_op jit(solution)/shard_map/ppermute | solution.py:301
  28.2 1.0 collective-permute-done.2.other_ref
  29.3 0.7 copy-done
  30.0 3.6 %advect.1 = (f32[160,128]{1,0:T(8,128)S(1)}, f32[320,128]{1,0:T(8,128)S(1)}) custom-call(f32[352,128]{1,0:T(8,128)S(1)} %bitcast.10, f32[352,128]{1,0:T(8,128)S(1)} %collective-permute-done.2.other_ref, f32[40,128]{1,0:T(8,128)S(1)} %copy-done), custom_call_target="tpu_custom_call" | custom-call | flops 10000000 | bytes 1000000 | tf_op jit(solution)/shard_map/advect/pallas_call | solution.py:342
  33.6 16.3 %all_to_all.10 = f32[64,1,640]{2,1,0:T(1,128)S(1)} all-to-all(f32[64,1,640]{2,1,0:T(1,128)S(1)} %bitcast.12), channel_id=1, replica_groups=mesh['gx'=64,'gy'=2,'ma'=4] {'gx'}, dimensions={0} | all-to-all | bytes 327680 | tf_op jit(solution)/shard_map/all_to_all | solution.py:356
  49.9 1.2 owner.1
  51.1 11.1 %all-to-all-start.1 = ((f32[256,1,1408]{2,1,0:T(1,128)}), f32[256,1,1408]{2,1,0:T(1,128)S(1)}, u32[]{:S(2)}, u32[]{:S(2)}) async-start(f32[256,1,1408]{2,1,0:T(1,128)} %bitcast.4), calls=%async_computation.1 | async-start | bytes 2883584 | tf_op jit(solution)/shard_map/all_to_all | solution.py:366
  62.2 4.0 %collective-permute-start.5 = (f32[160,128]{1,0:T(8,128)S(1)}, f32[160,128]{1,0:T(8,128)S(1)}, u32[]{:S(2)}, u32[]{:S(2)}) collective-permute-start(f32[160,128]{1,0:T(8,128)S(1)} %get-tuple-element.26.state_ref), channel_id=1, source_target_pairs={{0,3},{1,0},{2,1},{3,2},{4,7},{5,4},{6,5},{7,6},{8,11},{9,8},{10,9... | collective-permute-start | bytes 245768 | tf_op jit(solution)/shard_map/ppermute | solution.py:309
  66.2 1.9 %collective-permute-start.4 = (f32[160,128]{1,0:T(8,128)S(1)}, f32[160,128]{1,0:T(8,128)S(1)}, u32[]{:S(2)}, u32[]{:S(2)}) collective-permute-start(f32[160,128]{1,0:T(8,128)S(1)} %get-tuple-element.26.state_ref), channel_id=1, source_target_pairs={{0,2},{1,3},{2,0},{3,1},{4,6},{5,7},{6,4},{7,5},{8,10},{9,11},{10,... | collective-permute-start | bytes 245768 | tf_op jit(solution)/shard_map/ppermute | solution.py:309
  68.2 2.6 %collective-permute-start.3 = (f32[160,128]{1,0:T(8,128)S(1)}, f32[160,128]{1,0:T(8,128)S(1)}, u32[]{:S(2)}, u32[]{:S(2)}) collective-permute-start(f32[160,128]{1,0:T(8,128)S(1)} %get-tuple-element.26.state_ref), channel_id=1, source_target_pairs={{0,1},{1,2},{2,3},{3,0},{4,5},{5,6},{6,7},{7,4},{8,9},{9,10},{10,1... | collective-permute-start | bytes 245768 | tf_op jit(solution)/shard_map/ppermute | solution.py:309
  70.8 3.4 %collective-permute-done.4.gathered_2 = f32[160,128]{1,0:T(8,128)S(1)} collective-permute-done((f32[160,128]{1,0:T(8,128)S(1)}, f32[160,128]{1,0:T(8,128)S(1)}, u32[]{:S(2)}, u32[]{:S(2)}) %collective-permute-start.4) | collective-permute-done | bytes 81952 | tf_op jit(solution)/shard_map/ppermute | solution.py:309
  74.1 3.9 %collective-permute-done.3.gathered_1 = f32[160,128]{1,0:T(8,128)S(1)} collective-permute-done((f32[160,128]{1,0:T(8,128)S(1)}, f32[160,128]{1,0:T(8,128)S(1)}, u32[]{:S(2)}, u32[]{:S(2)}) %collective-permute-start.3) | collective-permute-done | bytes 81952 | tf_op jit(solution)/shard_map/ppermute | solution.py:309
  78.0 21.3 %all-to-all-done.1 = f32[256,1,1408]{2,1,0:T(1,128)S(1)} async-done(((f32[256,1,1408]{2,1,0:T(1,128)}), f32[256,1,1408]{2,1,0:T(1,128)S(1)}, u32[]{:S(2)}, u32[]{:S(2)}) %all-to-all-start.1) | async-done | bytes 1441824 | tf_op jit(solution)/shard_map/all_to_all | solution.py:366
  99.3 4.8 %collective-permute-start.6 = (f32[2816,128]{1,0:T(8,128)S(1)}, f32[2816,128]{1,0:T(8,128)S(1)}, u32[]{:S(2)}, u32[]{:S(2)}) collective-permute-start(f32[2816,128]{1,0:T(8,128)S(1)} %bitcast.7), channel_id=1, source_target_pairs={{0,4},{4,0},{1,5},{5,1},{2,6},{6,2},{3,7},{7,3},{8,12},{12,8},{9,1... | collective-permute-start | bytes 4325384 | tf_op jit(solution)/shard_map/ppermute | solution.py:301
  104.1 2.8 %collective-permute-done.6.came_o_ref = f32[2816,128]{1,0:T(8,128)S(1)} collective-permute-done((f32[2816,128]{1,0:T(8,128)S(1)}, f32[2816,128]{1,0:T(8,128)S(1)}, u32[]{:S(2)}, u32[]{:S(2)}) %collective-permute-start.6) | collective-permute-done | bytes 1441824 | tf_op jit(solution)/shard_map/ppermute | solution.py:301
  107.0 24.2 %filter.1 = f32[160,128]{1,0:T(8,128)} custom-call(f32[2816,128]{1,0:T(8,128)S(1)} %bitcast.8, f32[2816,128]{1,0:T(8,128)S(1)} %collective-permute-done.6.came_o_ref, bf16[3072,256]{1,0:T(8,128)(2,1)S(1)} %copy-done.1, f32[12,1024]{1,0:T(8,128)S(1)} %copy-done.2, f32[160,128]{1,0:T(8,128)S(1)} %collective-permute-done.3.gathered_1, ...), custom_call_target="tpu_custom_call" | custom-call | flops 3000000000 | bytes 4000000 | tf_op jit(solution)/shard_map/filter/pallas_call | solution.py:372
  (7 shorter events, 0.0 us)
Async XLA Ops:
  1.6 18.8 %collective-permute-start.1 = (f32[22,2,2,128]{3,2,1,0:T(2,128)S(1)}, f32[22,2,2,128]{3,2,1,0:T(2,128)S(1)}, u32[]{:S(2)}, u32[]{:S(2)}) collective-permute-start(f32[22,2,2,128]{3,2,1,0:T(2,128)S(1)} %get-tuple-element.33), channel_id=1, source_target_pairs={{0,504},{8,0},{16,8},{24,16},{32,24},{40,32},{48,40},{56,48},{64,5... | collective-permute-start | bytes 135176 | tf_op jit(solution)/shard_map/ppermute | solution.py:319
  16.0 8.1 %collective-permute-start = (f32[22,2,2,128]{3,2,1,0:T(2,128)S(1)}, f32[22,2,2,128]{3,2,1,0:T(2,128)S(1)}, u32[]{:S(2)}, u32[]{:S(2)}) collective-permute-start(f32[22,2,2,128]{3,2,1,0:T(2,128)S(1)} %get-tuple-element.34), channel_id=1, source_target_pairs={{0,8},{8,16},{16,24},{24,32},{32,40},{40,48},{48,56},{56,64},{64,7... | collective-permute-start | bytes 135176 | tf_op jit(solution)/shard_map/ppermute | solution.py:318
  24.2 5.0 %collective-permute-start.2 = (f32[352,128]{1,0:T(8,128)S(1)}, f32[352,128]{1,0:T(8,128)S(1)}, u32[]{:S(2)}, u32[]{:S(2)}) collective-permute-start(f32[352,128]{1,0:T(8,128)S(1)} %bitcast.9), channel_id=1, source_target_pairs={{0,4},{4,0},{1,5},{5,1},{2,6},{6,2},{3,7},{7,3},{8,12},{12,8},{9,1... | collective-permute-start | bytes 540680 | tf_op jit(solution)/shard_map/ppermute | solution.py:301
  29.3 0.7 copy-start
  51.1 55.8 %copy-start.1 = (bf16[3072,256]{1,0:T(8,128)(2,1)S(1)}, bf16[3072,256]{1,0:T(8,128)(2,1)}, u32[]{:S(2)}) copy-start(bf16[3072,256]{1,0:T(8,128)(2,1)} %get-tuple-element.28.onehots) | copy-start | bytes 4718596
  51.1 55.8 %copy-start.2 = (f32[12,1024]{1,0:T(8,128)S(1)}, f32[12,1024]{1,0:T(8,128)}, u32[]{:S(2)}) copy-start(f32[12,1024]{1,0:T(8,128)} %get-tuple-element.29.obs_ref) | copy-start | bytes 147460
  51.1 48.1 %all-to-all-start.1 = ((f32[256,1,1408]{2,1,0:T(1,128)}), f32[256,1,1408]{2,1,0:T(1,128)S(1)}, u32[]{:S(2)}, u32[]{:S(2)}) async-start(f32[256,1,1408]{2,1,0:T(1,128)} %bitcast.4), calls=%async_computation.1 | async-start | bytes 2883584 | tf_op jit(solution)/shard_map/all_to_all | solution.py:366
  62.2 8.6 %collective-permute-start.5 = (f32[160,128]{1,0:T(8,128)S(1)}, f32[160,128]{1,0:T(8,128)S(1)}, u32[]{:S(2)}, u32[]{:S(2)}) collective-permute-start(f32[160,128]{1,0:T(8,128)S(1)} %get-tuple-element.26.state_ref), channel_id=1, source_target_pairs={{0,3},{1,0},{2,1},{3,2},{4,7},{5,4},{6,5},{7,6},{8,11},{9,8},{10,9... | collective-permute-start | bytes 245768 | tf_op jit(solution)/shard_map/ppermute | solution.py:309
  66.2 7.9 %collective-permute-start.4 = (f32[160,128]{1,0:T(8,128)S(1)}, f32[160,128]{1,0:T(8,128)S(1)}, u32[]{:S(2)}, u32[]{:S(2)}) collective-permute-start(f32[160,128]{1,0:T(8,128)S(1)} %get-tuple-element.26.state_ref), channel_id=1, source_target_pairs={{0,2},{1,3},{2,0},{3,1},{4,6},{5,7},{6,4},{7,5},{8,10},{9,11},{10,... | collective-permute-start | bytes 245768 | tf_op jit(solution)/shard_map/ppermute | solution.py:309
  68.2 9.9 %collective-permute-start.3 = (f32[160,128]{1,0:T(8,128)S(1)}, f32[160,128]{1,0:T(8,128)S(1)}, u32[]{:S(2)}, u32[]{:S(2)}) collective-permute-start(f32[160,128]{1,0:T(8,128)S(1)} %get-tuple-element.26.state_ref), channel_id=1, source_target_pairs={{0,1},{1,2},{2,3},{3,0},{4,5},{5,6},{6,7},{7,4},{8,9},{9,10},{10,1... | collective-permute-start | bytes 245768 | tf_op jit(solution)/shard_map/ppermute | solution.py:309
  99.3 7.7 %collective-permute-start.6 = (f32[2816,128]{1,0:T(8,128)S(1)}, f32[2816,128]{1,0:T(8,128)S(1)}, u32[]{:S(2)}, u32[]{:S(2)}) collective-permute-start(f32[2816,128]{1,0:T(8,128)S(1)} %bitcast.7), channel_id=1, source_target_pairs={{0,4},{4,0},{1,5},{5,1},{2,6},{6,2},{3,7},{7,3},{8,12},{12,8},{9,1... | collective-permute-start | bytes 4325384 | tf_op jit(solution)/shard_map/ppermute | solution.py:301

commit v4 on v3

--- a/solution.py
+++ b/solution.py
@@ -19,6 +19,7 @@
 HALF = OWN * 2 * GROUPS
 QUARTER = (BLOCKS - 1) * GROUPS // MA
 SENT = CHUNK + QUARTER
+TAPERS = (BLOCKS - 1) * GROUPS * 2 * LANES
 ROWS_O = 256
 F32 = jnp.float32
 BF16 = jnp.bfloat16
@@ -83,6 +84,7 @@
             work[0, at, :] = twice[2:6]
             work[1, at, :] = twice_o[2:6]
 
+    send = index_ref[pl.ds(32, QUARTER), :]
     for g in range(2 * GROUPS):
         y = jnp.broadcast_to(index_ref[pl.ds(g, 1), :].astype(jnp.int32), (24, LANES))
         part = jnp.broadcast_to(index_ref[pl.ds(g + 16, 1), :].astype(jnp.int32), (24, LANES))
@@ -92,12 +94,13 @@
             found = jnp.take_along_axis(source, y, axis=1, mode="promise_in_bounds")
             total = jnp.where(part == c, found, total)
         for i in range(MA):
-            at = (i * 2 * GROUPS + g) * CHUNK
+            at = (i * 2 * GROUPS + g) * SENT
             picked_ref[pl.ds(at, CHUNK), :] = total[i * CHUNK : (i + 1) * CHUNK]
+            picked_ref[pl.ds(at + CHUNK, QUARTER), :] = send
 
 
 def prepare_kernel(*refs):
-    sources, results, copies, done = refs[:6], refs[6:9], refs[9:15], refs[15]
+    sources, results, copies, done = refs[:6], refs[6:8], refs[8:14], refs[14]
     moves = [
         pltpu.make_async_copy(source, copy, done.at[i])
         for i, (source, copy) in enumerate(zip(sources, copies))
@@ -107,7 +110,7 @@
     for move in moves:
         move.wait()
     order, cell_ref, region_ref, value_ref, var_ref, taper_ref = copies
-    index_ref, obs_ref, onehots = results
+    index_ref, obs_ref = results
     gx, gy, q = lax.axis_index("gx"), lax.axis_index("gy"), lax.axis_index("ma")
     for k in range(2):
         b = order[gy * 2 + k]
@@ -123,6 +126,9 @@
     for k in range(BLOCKS):
         for i, ref in enumerate((value_ref, var_ref, taper_ref)):
             obs_ref[pl.ds(i * BLOCKS + k, 1), :] = block_row(ref, order[k], pl.ds(0, OBS))
+        region = block_row(region_ref, order[k], pl.ds(0, OBS))
+        place = jnp.where(jnp.bitwise_and(region, 1) == gy, 0, GX) + jnp.right_shift(region, 1)
+        obs_ref[pl.ds(3 * BLOCKS + k, 1), :] = place.astype(F32)
 
     index_ref[pl.ds(32, 8), :] = jnp.zeros((8, LANES), F32)
     for i in range(QUARTER):
@@ -133,34 +139,47 @@
             row = jnp.where(g == j, block_row(taper_ref, b, pl.ds(j * LANES, LANES)), row)
         index_ref[pl.ds(32 + i, 1), :] = row
 
-    rows = lax.broadcasted_iota(jnp.int32, (LANES, LANES), 0)
-    for k in range(1, BLOCKS):
-        b = order[k]
-        for g in range(GROUPS):
-            region = block_row(region_ref, b, pl.ds(g * LANES, LANES))
-            place = jnp.where(jnp.bitwise_and(region, 1) == gy, 0, GX) + jnp.right_shift(region, 1)
-            hot = (rows == jnp.broadcast_to(place, (LANES, LANES))).astype(F32).T.astype(BF16)
-            at = pl.ds(((k - 1) * GROUPS + g) * LANES, LANES)
-            onehots[at, pl.ds(0, LANES)] = hot
-            onehots[at, pl.ds(LANES, LANES)] = hot
-
-
-def owner_kernel(parts_ref, index_ref, out_ref):
-    total = parts_ref[pl.ds(0, 40), :]
+
+def weights_kernel(parts_ref, weights_ref):
+    for i in range(QUARTER):
+        weights_ref[pl.ds(i * GX, GX), :] = parts_ref[pl.ds(CHUNK + i, GX, stride=SENT), :]
+
+
+def owner_kernel(parts_ref, out_ref):
+    total = parts_ref[pl.ds(0, 8 * SENT), :]
     for i in range(1, GX // 8):
-        total = total + parts_ref[pl.ds(i * 40, 40), :]
+        total = total + parts_ref[pl.ds(i * 8 * SENT, 8 * SENT), :]
     part = total[0:CHUNK]
     for i in range(1, 8):
-        part = part + total[i * CHUNK : (i + 1) * CHUNK]
-    eight = jnp.concatenate([part, index_ref[pl.ds(32, QUARTER), :]] * 8, axis=0)
+        part = part + total[i * SENT : i * SENT + CHUNK]
+    eight = jnp.concatenate([part] * 8, axis=0)
     for i in range(GX * MA // 8):
-        out_ref[pl.ds(i * 8 * SENT, 8 * SENT), :] = eight
+        out_ref[pl.ds(i * 8 * CHUNK, 8 * CHUNK), :] = eight
+
+
+def tapers_kernel(own_ref, other_ref, obs_ref, out_ref):
+    q = lax.axis_index("ma")
+    for shift in range(MA):
+        for i in range(QUARTER):
+            tile = jnp.bitwise_and(q - shift, MA - 1) * QUARTER + i
+            for side, ref in enumerate((own_ref, other_ref)):
+                high, low = split(ref[pl.ds((shift * QUARTER + i) * GX, GX), :])
+                at = pl.multiple_of(tile * 2 * LANES, 2 * LANES) + side * GX
+                out_ref[pl.ds(pl.multiple_of(at, GX), GX), :] = high
+                out_ref[pl.ds(pl.multiple_of(at + LANES, GX), GX), :] = low
+
+    rows = lax.broadcasted_iota(jnp.int32, (LANES, LANES), 0).astype(F32)
+    for k in range(1, BLOCKS):
+        for g in range(GROUPS):
+            place = obs_ref[pl.ds(3 * BLOCKS + k, 1), pl.ds(g * LANES, LANES)]
+            hot = (rows == jnp.broadcast_to(place, (LANES, LANES))).astype(F32).T.astype(BF16)
+            out_ref[pl.ds(TAPERS + ((k - 1) * GROUPS + g) * LANES, LANES), :] = hot
 
 
 def filter_kernel(
     came_ref,
     came_o_ref,
-    onehots,
+    tapers,
     obs_ref,
     gathered_1,
     gathered_2,
@@ -168,7 +187,6 @@
     state_ref,
     out_ref,
     xt,
-    tapers,
     b_high,
     b_both,
     increments,
@@ -179,7 +197,7 @@
     def load_half(ref, half):
         for g in range(16):
             block = jnp.concatenate(
-                [ref[pl.ds(g * SENT + i, 16, stride=16 * SENT), :] for i in range(CHUNK)], axis=0
+                [ref[pl.ds(g * CHUNK + i, 16, stride=16 * CHUNK), :] for i in range(CHUNK)], axis=0
             )
             mean = jnp.mean(block, axis=0, keepdims=True)
             full = jnp.concatenate(
@@ -196,13 +214,6 @@
     def _():
         load_half(came_o_ref, 0)
         load_half(came_ref, 1)
-
-    for tile in range((BLOCKS - 1) * GROUPS):
-        at = pl.ds(tile // QUARTER * GX * SENT + CHUNK + tile % QUARTER, GX, stride=SENT)
-        for side, ref in enumerate((came_ref, came_o_ref)):
-            high, low = split(ref[at, :])
-            tapers[tile, pl.ds(side * GX, GX), :] = high
-            tapers[tile, pl.ds(LANES + side * GX, GX), :] = low
 
     lane = lax.broadcasted_iota(jnp.int32, (ROWS_O, LANES), 1)
     member_row = lax.broadcasted_iota(jnp.int32, (LANES, OBS), 0)
@@ -242,7 +253,7 @@
         b_both[:, pl.ds(LANES, LANES)] = gain_low.astype(F32).T.astype(BF16)
 
         def chunk(i, carry, k=k, left=left):
-            taper = jnp.concatenate([tapers[k * GROUPS + g] for g in range(GROUPS)], axis=1)
+            taper = jnp.concatenate([tapers[pl.ds((k * GROUPS + g) * 2 * LANES, 2 * LANES), :] for g in range(GROUPS)], axis=1)
             at = pl.multiple_of((k + 1) * OBS + i * ROWS_O, ROWS_O)
             x = xt[pl.ds(at, ROWS_O), :]
             clean = jnp.where(lane < MEMBERS, x, 0.0)
@@ -253,7 +264,8 @@
             second = jnp.where(lane < 2 * MEMBERS - LANES, low_rolled, pltpu.roll(high, 2 * MEMBERS - LANES, 1))
             second = jnp.where(lane < 3 * MEMBERS - LANES, second, 0.0)
             query = jnp.concatenate([first, second], axis=1).astype(BF16)
-            hot = onehots[pl.ds(pl.multiple_of(at - OBS, ROWS_O), ROWS_O), :]
+            hot = tapers[pl.ds(pl.multiple_of(at + TAPERS - OBS, ROWS_O), ROWS_O), :]
+            hot = jnp.concatenate([hot, hot], axis=1)
             weight = dot_nn(query, left) * dot_nn(hot, taper)
             w_high, w_low = split(weight)
             both = dot_nn(w_high, b_both[...])
@@ -321,11 +333,10 @@
         prepare_kernel,
         out_shape=(
             jax.ShapeDtypeStruct((40, LANES), F32),
-            jax.ShapeDtypeStruct((3 * BLOCKS, OBS), F32),
-            jax.ShapeDtypeStruct(((BLOCKS - 1) * OBS, 2 * LANES), BF16),
+            jax.ShapeDtypeStruct((4 * BLOCKS, OBS), F32),
         ),
         in_specs=[pl.BlockSpec(memory_space=pltpu.HBM)] * 6,
-        out_specs=(VMEM,) * 3,
+        out_specs=(VMEM,) * 2,
         scratch_shapes=[pltpu.SMEM((BLOCKS,), jnp.int32)]
         + [pltpu.VMEM((BLOCKS, OBS), jnp.int32)] * 2
         + [pltpu.VMEM((BLOCKS, OBS), F32)] * 3
@@ -335,7 +346,7 @@
         name="prepare",
     )(block_order, obs_cell, obs_region, obs_value, obs_var, localization.reshape(BLOCKS, OBS))
     low, high, prepared = lax.optimization_barrier((low, high, prepared))
-    index, observed, onehots = prepared
+    index, observed = prepared
     own = jnp.concatenate([low, both, high], axis=2).reshape(-1, LANES)
     beside = other_core(own)
 
@@ -343,7 +354,7 @@
         advect_kernel,
         out_shape=(
             jax.ShapeDtypeStruct((OWN * 8, LANES), F32),
-            jax.ShapeDtypeStruct((HALF, LANES), F32),
+            jax.ShapeDtypeStruct((GX * SENT, LANES), F32),
         ),
         in_specs=[VMEM] * 3,
         out_specs=(VMEM, VMEM),
@@ -353,20 +364,39 @@
         name="advect",
     )(own, beside, index)
 
-    parts = lax.all_to_all(picked.reshape(GX, 1, CHUNK * LANES), "gx", 0, 0, tiled=True)
+    parts = lax.all_to_all(picked.reshape(GX, 1, SENT * LANES), "gx", 0, 0, tiled=True)
     gathered = over_members(state)
+    parts, gathered = lax.optimization_barrier((parts, gathered))
+    parts = parts.reshape(-1, LANES)
     owned = pl.pallas_call(
         owner_kernel,
-        out_shape=jax.ShapeDtypeStruct((MA * GX * SENT, LANES), F32),
-        in_specs=[VMEM, VMEM],
+        out_shape=jax.ShapeDtypeStruct((MA * GX * CHUNK, LANES), F32),
+        in_specs=[VMEM],
         out_specs=VMEM,
         compiler_params=params(4),
         name="owner",
-    )(parts.reshape(-1, LANES), index)
+    )(parts)
+    weights = pl.pallas_call(
+        weights_kernel,
+        out_shape=jax.ShapeDtypeStruct((QUARTER * GX, LANES), F32),
+        in_specs=[VMEM],
+        out_specs=VMEM,
+        compiler_params=params(4),
+        name="weights",
+    )(parts)
     came = lax.all_to_all(
-        owned.reshape(MA * GX, 1, SENT * LANES), ("ma", "gx"), 0, 0, tiled=True
+        owned.reshape(MA * GX, 1, CHUNK * LANES), ("ma", "gx"), 0, 0, tiled=True
     ).reshape(-1, LANES)
-    came, gathered = lax.optimization_barrier((came, gathered))
+    weights = jnp.concatenate([weights] + over_members(weights), axis=0)
+    tapers = pl.pallas_call(
+        tapers_kernel,
+        out_shape=jax.ShapeDtypeStruct((TAPERS + (BLOCKS - 1) * OBS, LANES), BF16),
+        in_specs=[VMEM] * 3,
+        out_specs=VMEM,
+        compiler_params=params(4),
+        name="tapers",
+    )(weights, other_core(weights), observed)
+    came, tapers = lax.optimization_barrier((came, tapers))
     came_beside = other_core(came)
 
     out = pl.pallas_call(
@@ -376,7 +406,6 @@
         out_specs=VMEM,
         scratch_shapes=[
             pltpu.VMEM((BLOCKS * OBS, LANES), F32),
-            pltpu.VMEM(((BLOCKS - 1) * GROUPS, 2 * LANES, LANES), BF16),
             pltpu.VMEM((OBS, LANES), BF16),
             pltpu.VMEM((OBS, 2 * LANES), BF16),
             pltpu.VMEM((LANES, LANES), F32),
@@ -384,7 +413,7 @@
         compiler_params=params(32),
         cost_estimate=pl.CostEstimate(flops=3_000_000_000, bytes_accessed=4_000_000, transcendentals=0),
         name="filter",
-    )(came, came_beside, onehots, observed, *gathered, state)
+    )(came, came_beside, tapers, observed, *gathered, state)
     return out.reshape(ensemble.shape)
 
 

time: 132 us -> 124 us (0.939)
  starting transfers between devices: 44.8 us -> 71.6 us
  waiting for transfers between devices: 36.1 us -> 17.3 us
  blocking collectives: 16.3 us -> 0 us
    all_to_all x1 -> x2, waiting for transfers between devices: 21.3 us -> 1.34 us  [the longest x1 1.33 us: local(): lax.all_to_all(picked.reshape(GX, 1, SENT * LANES), 'gx', 0, 0, tiled=True)]
    all_to_all x1 -> x0, blocking collectives: 16.3 us -> none  [local(): lax.all_to_all(picked.reshape(GX, 1, CHUNK * LANES), 'gx', 0, 0, tiled=True)]
    all_to_all x1 -> x2, starting transfers between devices: 11.1 us -> 25 us  [the longest x1 16.2 us: local(): lax.all_to_all(owned.reshape(MA * GX, 1, CHUNK * LANES), ('ma', 'gx'), 0,...]
    ppermute x3 -> x6, starting transfers between devices: 8.54 us -> 20.4 us  [over_members(): lax.ppermute(x, 'ma', [(i, (i + s) % MA) for i in range(MA)])]
    ppermute x3 -> x6, waiting for transfers between devices: 7.26 us -> 11.3 us  [over_members(): lax.ppermute(x, 'ma', [(i, (i + s) % MA) for i in range(MA)])]
    ppermute x1, waiting for transfers between devices: 3.75 us -> 0.01 us  [local(): low = lax.ppermute(both[:, :, 2:], 'gx', forward)]
    ppermute x1, starting transfers between devices: 1.92 us -> 4.83 us  [local(): low = lax.ppermute(both[:, :, 2:], 'gx', forward)]
    ppermute x1, starting transfers between devices: 14.4 us -> 11.5 us  [local(): high = lax.ppermute(both[:, :, :2], 'gx', backward)]
  transfers between devices with their start and end apart: 8 -> 13, of which waited for: 6 -> 7; matrix products, arithmetic and copies ran while one was open for 0% -> 0% of each run, Pallas kernels for 2% -> 2%
where the time goes in v4:
time: 124 us; the launch traced here: 123 us
  starting transfers between devices  71.6 us (58%)
  Pallas kernels  31.4 us (25%)
  waiting for transfers between devices  17.3 us (14%)
  local copies, waits for them, and re-layouts  2.36 us (2%)
    pallas_call x1, Pallas kernels, local(): pl.pallas_call(filter_kernel, out_shape=jax.ShapeDtypeStruct((OWN * 8, LA...  24.2 us
    ppermute x6, starting transfers between devices, over_members(): lax.ppermute(x, 'ma', [(i, (i + s) % MA) for i in range(MA)])  20.4 us
    all_to_all x1, starting transfers between devices, local(): lax.all_to_all(owned.reshape(MA * GX, 1, CHUNK * LANES), ('ma', 'gx'), 0,...  16.2 us
    ppermute x1, starting transfers between devices, local(): high = lax.ppermute(both[:, :, :2], 'gx', backward)  11.5 us
    ppermute x6, waiting for transfers between devices, over_members(): lax.ppermute(x, 'ma', [(i, (i + s) % MA) for i in range(MA)])  11.3 us
    ppermute x3, starting transfers between devices, other_core(): return lax.ppermute(x, 'gy', [(0, 1), (1, 0)])  9.81 us
    all_to_all x1, starting transfers between devices, local(): lax.all_to_all(picked.reshape(GX, 1, SENT * LANES), 'gx', 0, 0, tiled=True)  8.8 us
    ppermute x1, starting transfers between devices, local(): low = lax.ppermute(both[:, :, 2:], 'gx', forward)  4.83 us
  transfers between devices with their start and end apart: 13, of which 7 were waited for; matrix products, arithmetic and copies ran while one was open for 0% of the time, Pallas kernels for 2%

profile of v4, /device:TPU:1, one launch (start us, length us, event | category | flops | bytes accessed | tf_op | source)
XLA Modules:
  0.0 122.9 jit_solution(14630246320528696246)
XLA Ops:
  0.0 0.9 constant_dynamic-update-slice_fusion.1
  1.6 4.8 %collective-permute-start = (f32[22,2,2,128]{3,2,1,0:T(2,128)S(1)}, f32[22,2,2,128]{3,2,1,0:T(2,128)S(1)}, u32[]{:S(2)}, u32[]{:S(2)}) collective-permute-start(f32[22,2,2,128]{3,2,1,0:T(2,128)S(1)} %get-tuple-element.34), channel_id=1, source_target_pairs={{0,8},{8,16},{16,24},{24,32},{32,40},{40,48},{48,56},{56,64},{64,7... | collective-permute-start | bytes 135176 | tf_op jit(solution)/shard_map/ppermute | solution.py:330
  6.5 11.5 %collective-permute-start.1 = (f32[22,2,2,128]{3,2,1,0:T(2,128)S(1)}, f32[22,2,2,128]{3,2,1,0:T(2,128)S(1)}, u32[]{:S(2)}, u32[]{:S(2)}) collective-permute-start(f32[22,2,2,128]{3,2,1,0:T(2,128)S(1)} %get-tuple-element.33), channel_id=1, source_target_pairs={{0,504},{8,0},{16,8},{24,16},{32,24},{40,32},{48,40},{56,48},{64,5... | collective-permute-start | bytes 135176 | tf_op jit(solution)/shard_map/ppermute | solution.py:331
  18.0 1.6 %prepare.1 = (f32[40,128]{1,0:T(8,128)}, f32[16,1024]{1,0:T(8,128)}) custom-call(s32[4]{0:T(128)} %refs_0_.1, s32[4,1024]{1,0:T(4,128)} %refs_1_.1, s32[4,1024]{1,0:T(4,128)} %refs_2_.1, f32[4,1024]{1,0:T(4,128)} %refs_3_.1, f32[4,1024]{1,0:T(4,128)} %refs_4_.1, f32[4,1024]{1,0:T(4,128)} %bitcast.13), custom_call_target="tpu_custom_call" | custom-call | flops 10000000 | bytes 2000000 | tf_op jit(solution)/shard_map/prepare/pallas_call | solution.py:332
  19.7 2.9 %collective-permute-start.2 = (f32[352,128]{1,0:T(8,128)S(1)}, f32[352,128]{1,0:T(8,128)S(1)}, u32[]{:S(2)}, u32[]{:S(2)}) collective-permute-start(f32[352,128]{1,0:T(8,128)S(1)} %bitcast.9), channel_id=1, source_target_pairs={{0,4},{4,0},{1,5},{5,1},{2,6},{6,2},{3,7},{7,3},{8,12},{12,8},{9,1... | collective-permute-start | bytes 540680 | tf_op jit(solution)/shard_map/ppermute | solution.py:313
  22.6 1.0 collective-permute-done.2.other_ref
  24.4 4.3 %advect.1 = (f32[160,128]{1,0:T(8,128)S(1)}, f32[704,128]{1,0:T(8,128)}) custom-call(f32[352,128]{1,0:T(8,128)S(1)} %bitcast.10, f32[352,128]{1,0:T(8,128)S(1)} %collective-permute-done.2.other_ref, f32[40,128]{1,0:T(8,128)S(1)} %copy-done.1), custom_call_target="tpu_custom_call" | custom-call | flops 10000000 | bytes 1000000 | tf_op jit(solution)/shard_map/advect/pallas_call | solution.py:353
  28.7 8.8 %all-to-all-start = ((f32[64,1,1408]{2,1,0:T(1,128)}), f32[64,1,1408]{2,1,0:T(1,128)S(1)}, u32[]{:S(2)}, u32[]{:S(2)}) async-start(f32[64,1,1408]{2,1,0:T(1,128)} %bitcast.2), calls=%async_computation | async-start | bytes 720896 | tf_op jit(solution)/shard_map/all_to_all | solution.py:367
  37.5 3.3 %collective-permute-start.3 = (f32[160,128]{1,0:T(8,128)S(1)}, f32[160,128]{1,0:T(8,128)S(1)}, u32[]{:S(2)}, u32[]{:S(2)}) collective-permute-start(f32[160,128]{1,0:T(8,128)S(1)} %get-tuple-element.25.state_ref), channel_id=1, source_target_pairs={{0,1},{1,2},{2,3},{3,0},{4,5},{5,6},{6,7},{7,4},{8,9},{9,10},{10,1... | collective-permute-start | bytes 245768 | tf_op jit(solution)/shard_map/ppermute | solution.py:321
  40.8 4.4 %collective-permute-start.4 = (f32[160,128]{1,0:T(8,128)S(1)}, f32[160,128]{1,0:T(8,128)S(1)}, u32[]{:S(2)}, u32[]{:S(2)}) collective-permute-start(f32[160,128]{1,0:T(8,128)S(1)} %get-tuple-element.25.state_ref), channel_id=1, source_target_pairs={{0,2},{1,3},{2,0},{3,1},{4,6},{5,7},{6,4},{7,5},{8,10},{9,11},{10,... | collective-permute-start | bytes 245768 | tf_op jit(solution)/shard_map/ppermute | solution.py:321
  45.1 3.1 %collective-permute-start.5 = (f32[160,128]{1,0:T(8,128)S(1)}, f32[160,128]{1,0:T(8,128)S(1)}, u32[]{:S(2)}, u32[]{:S(2)}) collective-permute-start(f32[160,128]{1,0:T(8,128)S(1)} %get-tuple-element.25.state_ref), channel_id=1, source_target_pairs={{0,3},{1,0},{2,1},{3,2},{4,7},{5,4},{6,5},{7,6},{8,11},{9,8},{10,9... | collective-permute-start | bytes 245768 | tf_op jit(solution)/shard_map/ppermute | solution.py:321
  48.2 2.4 %collective-permute-done.5.gathered_3 = f32[160,128]{1,0:T(8,128)S(1)} collective-permute-done((f32[160,128]{1,0:T(8,128)S(1)}, f32[160,128]{1,0:T(8,128)S(1)}, u32[]{:S(2)}, u32[]{:S(2)}) %collective-permute-start.5) | collective-permute-done | bytes 81952 | tf_op jit(solution)/shard_map/ppermute | solution.py:321
  50.6 1.3 %all-to-all-done = f32[64,1,1408]{2,1,0:T(1,128)S(1)} async-done(((f32[64,1,1408]{2,1,0:T(1,128)}), f32[64,1,1408]{2,1,0:T(1,128)S(1)}, u32[]{:S(2)}, u32[]{:S(2)}) %all-to-all-start) | async-done | bytes 360480 | tf_op jit(solution)/shard_map/all_to_all | solution.py:367
  52.0 0.9 owner.1
  52.9 16.2 %all-to-all-start.1 = ((f32[256,1,640]{2,1,0:T(1,128)}), f32[256,1,640]{2,1,0:T(1,128)S(1)}, u32[]{:S(2)}, u32[]{:S(2)}) async-start(f32[256,1,640]{2,1,0:T(1,128)} %bitcast.4), calls=%async_computation.1 | async-start | bytes 1310720 | tf_op jit(solution)/shard_map/all_to_all | solution.py:387
  69.1 1.9 %collective-permute-start.6 = (f32[384,128]{1,0:T(8,128)S(1)}, f32[384,128]{1,0:T(8,128)S(1)}, u32[]{:S(2)}, u32[]{:S(2)}) collective-permute-start(f32[384,128]{1,0:T(8,128)S(1)} %weights.1), channel_id=1, source_target_pairs={{0,1},{1,2},{2,3},{3,0},{4,5},{5,6},{6,7},{7,4},{8,9},{9,10},{10,1... | collective-permute-start | bytes 589832 | tf_op jit(solution)/shard_map/ppermute | solution.py:321
  71.0 5.2 %collective-permute-start.7 = (f32[384,128]{1,0:T(8,128)S(1)}, f32[384,128]{1,0:T(8,128)S(1)}, u32[]{:S(2)}, u32[]{:S(2)}) collective-permute-start(f32[384,128]{1,0:T(8,128)S(1)} %weights.1), channel_id=1, source_target_pairs={{0,2},{1,3},{2,0},{3,1},{4,6},{5,7},{6,4},{7,5},{8,10},{9,11},{10,... | collective-permute-start | bytes 589832 | tf_op jit(solution)/shard_map/ppermute | solution.py:321
  76.2 2.7 %collective-permute-start.8 = (f32[384,128]{1,0:T(8,128)S(1)}, f32[384,128]{1,0:T(8,128)S(1)}, u32[]{:S(2)}, u32[]{:S(2)}) collective-permute-start(f32[384,128]{1,0:T(8,128)S(1)} %weights.1), channel_id=1, source_target_pairs={{0,3},{1,0},{2,1},{3,2},{4,7},{5,4},{6,5},{7,6},{8,11},{9,8},{10,9... | collective-permute-start | bytes 589832 | tf_op jit(solution)/shard_map/ppermute | solution.py:321
  78.9 8.1 %collective-permute-done.7 = f32[384,128]{1,0:T(8,128)S(1)} collective-permute-done((f32[384,128]{1,0:T(8,128)S(1)}, f32[384,128]{1,0:T(8,128)S(1)}, u32[]{:S(2)}, u32[]{:S(2)}) %collective-permute-start.7) | collective-permute-done | bytes 196640 | tf_op jit(solution)/shard_map/ppermute | solution.py:321
  87.8 4.6 %collective-permute-start.9 = (f32[1536,128]{1,0:T(8,128)S(1)}, f32[1536,128]{1,0:T(8,128)S(1)}, u32[]{:S(2)}, u32[]{:S(2)}) collective-permute-start(f32[1536,128]{1,0:T(8,128)S(1)} %pad_maximum_fusion.own_ref), channel_id=1, source_target_pairs={{0,4},{4,0},{1,5},{5,1},{2,6},{6,2},{3,7},{7,3},{8,12},{12,8},{9,1... | collective-permute-start | bytes 2359304 | tf_op jit(solution)/shard_map/ppermute | solution.py:313
  92.5 1.9 %collective-permute-done.9.other_ref = f32[1536,128]{1,0:T(8,128)S(1)} collective-permute-done((f32[1536,128]{1,0:T(8,128)S(1)}, f32[1536,128]{1,0:T(8,128)S(1)}, u32[]{:S(2)}, u32[]{:S(2)}) %collective-permute-start.9) | collective-permute-done | bytes 786464 | tf_op jit(solution)/shard_map/ppermute | solution.py:313
  94.8 2.3 %collective-permute-start.10 = (f32[1280,128]{1,0:T(8,128)S(1)}, f32[1280,128]{1,0:T(8,128)S(1)}, u32[]{:S(2)}, u32[]{:S(2)}) collective-permute-start(f32[1280,128]{1,0:T(8,128)S(1)} %bitcast.11), channel_id=1, source_target_pairs={{0,4},{4,0},{1,5},{5,1},{2,6},{6,2},{3,7},{7,3},{8,12},{12,8},{9,1... | collective-permute-start | bytes 1966088 | tf_op jit(solution)/shard_map/ppermute | solution.py:313
  97.1 1.7 %collective-permute-done.10.came_o_ref = f32[1280,128]{1,0:T(8,128)S(1)} collective-permute-done((f32[1280,128]{1,0:T(8,128)S(1)}, f32[1280,128]{1,0:T(8,128)S(1)}, u32[]{:S(2)}, u32[]{:S(2)}) %collective-permute-start.10) | collective-permute-done | bytes 655392 | tf_op jit(solution)/shard_map/ppermute | solution.py:313
  98.8 24.2 %filter.1 = f32[160,128]{1,0:T(8,128)} custom-call(f32[1280,128]{1,0:T(8,128)S(1)} %bitcast.12, f32[1280,128]{1,0:T(8,128)S(1)} %collective-permute-done.10.came_o_ref, bf16[9216,128]{1,0:T(8,128)(2,1)S(1)} %tapers.1, f32[16,1024]{1,0:T(8,128)S(1)} %copy-done, f32[160,128]{1,0:T(8,128)S(1)} %collective-permute-done.3.gathered_1, ...), custom_call_target="tpu_custom_call" | custom-call | flops 3000000000 | bytes 4000000 | tf_op jit(solution)/shard_map/filter/pallas_call | solution.py:402
  (17 shorter events, 2.8 us)
Async XLA Ops:
  1.6 17.9 %collective-permute-start = (f32[22,2,2,128]{3,2,1,0:T(2,128)S(1)}, f32[22,2,2,128]{3,2,1,0:T(2,128)S(1)}, u32[]{:S(2)}, u32[]{:S(2)}) collective-permute-start(f32[22,2,2,128]{3,2,1,0:T(2,128)S(1)} %get-tuple-element.34), channel_id=1, source_target_pairs={{0,8},{8,16},{16,24},{24,32},{32,40},{40,48},{48,56},{56,64},{64,7... | collective-permute-start | bytes 135176 | tf_op jit(solution)/shard_map/ppermute | solution.py:330
  6.5 13.1 %collective-permute-start.1 = (f32[22,2,2,128]{3,2,1,0:T(2,128)S(1)}, f32[22,2,2,128]{3,2,1,0:T(2,128)S(1)}, u32[]{:S(2)}, u32[]{:S(2)}) collective-permute-start(f32[22,2,2,128]{3,2,1,0:T(2,128)S(1)} %get-tuple-element.33), channel_id=1, source_target_pairs={{0,504},{8,0},{16,8},{24,16},{32,24},{40,32},{48,40},{56,48},{64,5... | collective-permute-start | bytes 135176 | tf_op jit(solution)/shard_map/ppermute | solution.py:331
  19.7 4.0 %collective-permute-start.2 = (f32[352,128]{1,0:T(8,128)S(1)}, f32[352,128]{1,0:T(8,128)S(1)}, u32[]{:S(2)}, u32[]{:S(2)}) collective-permute-start(f32[352,128]{1,0:T(8,128)S(1)} %bitcast.9), channel_id=1, source_target_pairs={{0,4},{4,0},{1,5},{5,1},{2,6},{6,2},{3,7},{7,3},{8,12},{12,8},{9,1... | collective-permute-start | bytes 540680 | tf_op jit(solution)/shard_map/ppermute | solution.py:313
  23.6 0.7 copy-start.1
  28.7 23.3 %all-to-all-start = ((f32[64,1,1408]{2,1,0:T(1,128)}), f32[64,1,1408]{2,1,0:T(1,128)S(1)}, u32[]{:S(2)}, u32[]{:S(2)}) async-start(f32[64,1,1408]{2,1,0:T(1,128)} %bitcast.2), calls=%async_computation | async-start | bytes 720896 | tf_op jit(solution)/shard_map/all_to_all | solution.py:367
  37.5 56.9 %copy-start = (f32[16,1024]{1,0:T(8,128)S(1)}, f32[16,1024]{1,0:T(8,128)}, u32[]{:S(2)}) copy-start(f32[16,1024]{1,0:T(8,128)} %get-tuple-element.27.obs_ref) | copy-start | bytes 196612
  37.5 10.7 %collective-permute-start.3 = (f32[160,128]{1,0:T(8,128)S(1)}, f32[160,128]{1,0:T(8,128)S(1)}, u32[]{:S(2)}, u32[]{:S(2)}) collective-permute-start(f32[160,128]{1,0:T(8,128)S(1)} %get-tuple-element.25.state_ref), channel_id=1, source_target_pairs={{0,1},{1,2},{2,3},{3,0},{4,5},{5,6},{6,7},{7,4},{8,9},{9,10},{10,1... | collective-permute-start | bytes 245768 | tf_op jit(solution)/shard_map/ppermute | solution.py:321
  40.8 7.4 %collective-permute-start.4 = (f32[160,128]{1,0:T(8,128)S(1)}, f32[160,128]{1,0:T(8,128)S(1)}, u32[]{:S(2)}, u32[]{:S(2)}) collective-permute-start(f32[160,128]{1,0:T(8,128)S(1)} %get-tuple-element.25.state_ref), channel_id=1, source_target_pairs={{0,2},{1,3},{2,0},{3,1},{4,6},{5,7},{6,4},{7,5},{8,10},{9,11},{10,... | collective-permute-start | bytes 245768 | tf_op jit(solution)/shard_map/ppermute | solution.py:321
  45.1 5.5 %collective-permute-start.5 = (f32[160,128]{1,0:T(8,128)S(1)}, f32[160,128]{1,0:T(8,128)S(1)}, u32[]{:S(2)}, u32[]{:S(2)}) collective-permute-start(f32[160,128]{1,0:T(8,128)S(1)} %get-tuple-element.25.state_ref), channel_id=1, source_target_pairs={{0,3},{1,0},{2,1},{3,2},{4,7},{5,4},{6,5},{7,6},{8,11},{9,8},{10,9... | collective-permute-start | bytes 245768 | tf_op jit(solution)/shard_map/ppermute | solution.py:321
  52.9 41.9 %all-to-all-start.1 = ((f32[256,1,640]{2,1,0:T(1,128)}), f32[256,1,640]{2,1,0:T(1,128)S(1)}, u32[]{:S(2)}, u32[]{:S(2)}) async-start(f32[256,1,640]{2,1,0:T(1,128)} %bitcast.4), calls=%async_computation.1 | async-start | bytes 1310720 | tf_op jit(solution)/shard_map/all_to_all | solution.py:387
  69.1 9.8 %collective-permute-start.6 = (f32[384,128]{1,0:T(8,128)S(1)}, f32[384,128]{1,0:T(8,128)S(1)}, u32[]{:S(2)}, u32[]{:S(2)}) collective-permute-start(f32[384,128]{1,0:T(8,128)S(1)} %weights.1), channel_id=1, source_target_pairs={{0,1},{1,2},{2,3},{3,0},{4,5},{5,6},{6,7},{7,4},{8,9},{9,10},{10,1... | collective-permute-start | bytes 589832 | tf_op jit(solution)/shard_map/ppermute | solution.py:321
  71.0 16.0 %collective-permute-start.7 = (f32[384,128]{1,0:T(8,128)S(1)}, f32[384,128]{1,0:T(8,128)S(1)}, u32[]{:S(2)}, u32[]{:S(2)}) collective-permute-start(f32[384,128]{1,0:T(8,128)S(1)} %weights.1), channel_id=1, source_target_pairs={{0,2},{1,3},{2,0},{3,1},{4,6},{5,7},{6,4},{7,5},{8,10},{9,11},{10,... | collective-permute-start | bytes 589832 | tf_op jit(solution)/shard_map/ppermute | solution.py:321
  76.2 11.6 %collective-permute-start.8 = (f32[384,128]{1,0:T(8,128)S(1)}, f32[384,128]{1,0:T(8,128)S(1)}, u32[]{:S(2)}, u32[]{:S(2)}) collective-permute-start(f32[384,128]{1,0:T(8,128)S(1)} %weights.1), channel_id=1, source_target_pairs={{0,3},{1,0},{2,1},{3,2},{4,7},{5,4},{6,5},{7,6},{8,11},{9,8},{10,9... | collective-permute-start | bytes 589832 | tf_op jit(solution)/shard_map/ppermute | solution.py:321
  87.8 6.5 %collective-permute-start.9 = (f32[1536,128]{1,0:T(8,128)S(1)}, f32[1536,128]{1,0:T(8,128)S(1)}, u32[]{:S(2)}, u32[]{:S(2)}) collective-permute-start(f32[1536,128]{1,0:T(8,128)S(1)} %pad_maximum_fusion.own_ref), channel_id=1, source_target_pairs={{0,4},{4,0},{1,5},{5,1},{2,6},{6,2},{3,7},{7,3},{8,12},{12,8},{9,1... | collective-permute-start | bytes 2359304 | tf_op jit(solution)/shard_map/ppermute | solution.py:313
  94.8 4.0 %collective-permute-start.10 = (f32[1280,128]{1,0:T(8,128)S(1)}, f32[1280,128]{1,0:T(8,128)S(1)}, u32[]{:S(2)}, u32[]{:S(2)}) collective-permute-start(f32[1280,128]{1,0:T(8,128)S(1)} %bitcast.11), channel_id=1, source_target_pairs={{0,4},{4,0},{1,5},{5,1},{2,6},{6,2},{3,7},{7,3},{8,12},{12,8},{9,1... | collective-permute-start | bytes 1966088 | tf_op jit(solution)/shard_map/ppermute | solution.py:313

commit v5 on v4

--- a/solution.py
+++ b/solution.py
@@ -140,9 +140,17 @@
         index_ref[pl.ds(32 + i, 1), :] = row
 
 
-def weights_kernel(parts_ref, weights_ref):
+def weights_kernel(parts_ref, state_ref, out_ref):
     for i in range(QUARTER):
-        weights_ref[pl.ds(i * GX, GX), :] = parts_ref[pl.ds(CHUNK + i, GX, stride=SENT), :]
+        out_ref[pl.ds(i * GX, GX), :] = parts_ref[pl.ds(CHUNK + i, GX, stride=SENT), :]
+    out_ref[pl.ds(QUARTER * GX, OWN * 8), :] = state_ref[...]
+
+
+def merge_kernel(*refs):
+    weights_ref, state_ref = refs[MA:]
+    for i in range(MA):
+        weights_ref[pl.ds(i * QUARTER * GX, QUARTER * GX), :] = refs[i][pl.ds(0, QUARTER * GX), :]
+        state_ref[pl.ds(i * OWN * 8, OWN * 8), :] = refs[i][pl.ds(QUARTER * GX, OWN * 8), :]
 
 
 def owner_kernel(parts_ref, out_ref):
@@ -181,9 +189,6 @@
     came_o_ref,
     tapers,
     obs_ref,
-    gathered_1,
-    gathered_2,
-    gathered_3,
     state_ref,
     out_ref,
     xt,
@@ -295,10 +300,7 @@
     transform = jnp.dot(transform, shuffle, precision=lax.Precision.HIGHEST, preferred_element_type=F32)
     tiles = []
     for c in range(8):
-        at = pl.ds(c, OWN, stride=8)
-        tile = jnp.concatenate(
-            [ref[at, :] for ref in (state_ref, gathered_1, gathered_2, gathered_3)], axis=0
-        )
+        tile = state_ref[pl.ds(c, MEMBERS, stride=8), :]
         tiles.append(tile - jnp.mean(tile, axis=0, keepdims=True))
     centered = jnp.concatenate(
         [jnp.concatenate(tiles, axis=1), jnp.zeros((LANES - MEMBERS, CELLS), F32)], axis=0
@@ -365,8 +367,6 @@
     )(own, beside, index)
 
     parts = lax.all_to_all(picked.reshape(GX, 1, SENT * LANES), "gx", 0, 0, tiled=True)
-    gathered = over_members(state)
-    parts, gathered = lax.optimization_barrier((parts, gathered))
     parts = parts.reshape(-1, LANES)
     owned = pl.pallas_call(
         owner_kernel,
@@ -376,33 +376,48 @@
         compiler_params=params(4),
         name="owner",
     )(parts)
+    parts, owned = lax.optimization_barrier((parts, owned))
     weights = pl.pallas_call(
         weights_kernel,
-        out_shape=jax.ShapeDtypeStruct((QUARTER * GX, LANES), F32),
-        in_specs=[VMEM],
+        out_shape=jax.ShapeDtypeStruct((QUARTER * GX + OWN * 8, LANES), F32),
+        in_specs=[VMEM, VMEM],
         out_specs=VMEM,
         compiler_params=params(4),
+        cost_estimate=pl.CostEstimate(flops=1000, bytes_accessed=1000, transcendentals=0),
         name="weights",
-    )(parts)
+    )(parts, state)
     came = lax.all_to_all(
         owned.reshape(MA * GX, 1, CHUNK * LANES), ("ma", "gx"), 0, 0, tiled=True
     ).reshape(-1, LANES)
-    weights = jnp.concatenate([weights] + over_members(weights), axis=0)
+    members = [weights] + over_members(weights)
+    weights, gathered = pl.pallas_call(
+        merge_kernel,
+        out_shape=(
+            jax.ShapeDtypeStruct((MA * QUARTER * GX, LANES), F32),
+            jax.ShapeDtypeStruct((MEMBERS * 8, LANES), F32),
+        ),
+        in_specs=[VMEM] * MA,
+        out_specs=(VMEM, VMEM),
+        compiler_params=params(4),
+        cost_estimate=pl.CostEstimate(flops=1000, bytes_accessed=1000, transcendentals=0),
+        name="merge",
+    )(*members)
     tapers = pl.pallas_call(
         tapers_kernel,
         out_shape=jax.ShapeDtypeStruct((TAPERS + (BLOCKS - 1) * OBS, LANES), BF16),
         in_specs=[VMEM] * 3,
         out_specs=VMEM,
         compiler_params=params(4),
+        cost_estimate=pl.CostEstimate(flops=1000, bytes_accessed=1000, transcendentals=0),
         name="tapers",
     )(weights, other_core(weights), observed)
-    came, tapers = lax.optimization_barrier((came, tapers))
+    came, tapers, gathered = lax.optimization_barrier((came, tapers, gathered))
     came_beside = other_core(came)
 
     out = pl.pallas_call(
         filter_kernel,
         out_shape=jax.ShapeDtypeStruct((OWN * 8, LANES), F32),
-        in_specs=[VMEM] * 8,
+        in_specs=[VMEM] * 5,
         out_specs=VMEM,
         scratch_shapes=[
             pltpu.VMEM((BLOCKS * OBS, LANES), F32),
@@ -410,10 +425,10 @@
             pltpu.VMEM((OBS, 2 * LANES), BF16),
             pltpu.VMEM((LANES, LANES), F32),
         ],
-        compiler_params=params(32),
+        compiler_params=params(16),
         cost_estimate=pl.CostEstimate(flops=3_000_000_000, bytes_accessed=4_000_000, transcendentals=0),
         name="filter",
-    )(came, came_beside, tapers, observed, *gathered, state)
+    )(came, came_beside, tapers, observed, gathered)
     return out.reshape(ensemble.shape)
 
 

time: 124 us -> 126 us (1.016)
  starting transfers between devices: 71.6 us -> 45.9 us
  blocking collectives: 0 us -> 19.2 us
  waiting for transfers between devices: 17.3 us -> 27.1 us
    all_to_all x0 -> x1, blocking collectives: none -> 19.2 us  [local(): lax.all_to_all(picked.reshape(GX, 1, SENT * LANES), 'gx', 0, 0, tiled=True)]
    ppermute x6 -> x3, starting transfers between devices: 20.4 us -> 8.54 us  [over_members(): lax.ppermute(x, 'ma', [(i, (i + s) % MA) for i in range(MA)])]
    all_to_all x1 -> x0, starting transfers between devices: 8.8 us -> none  [local(): lax.all_to_all(picked.reshape(GX, 1, SENT * LANES), 'gx', 0, 0, tiled=True)]
    ppermute x6 -> x3, waiting for transfers between devices: 11.3 us -> 17.9 us  [over_members(): lax.ppermute(x, 'ma', [(i, (i + s) % MA) for i in range(MA)])]
    ppermute x1, waiting for transfers between devices: 0.01 us -> 4.57 us  [local(): low = lax.ppermute(both[:, :, 2:], 'gx', forward)]
    all_to_all x1, starting transfers between devices: 16.2 us -> 12.4 us  [local(): lax.all_to_all(owned.reshape(MA * GX, 1, CHUNK * LANES), ('ma', 'gx'), 0,...]
    ppermute x1, starting transfers between devices: 4.83 us -> 1.92 us  [local(): low = lax.ppermute(both[:, :, 2:], 'gx', forward)]
    ppermute x1, starting transfers between devices: 11.5 us -> 14.4 us  [local(): high = lax.ppermute(both[:, :, :2], 'gx', backward)]
  transfers between devices with their start and end apart: 13 -> 9, of which waited for: 7 -> 7; matrix products, arithmetic and copies ran while one was open for 0% -> 0% of each run, Pallas kernels for 2% -> 2%
where the time goes in v5:
time: 126 us
  starting transfers between devices  45.9 us (36%)
  Pallas kernels  30.8 us (24%)
  waiting for transfers between devices  27.1 us (22%)
  blocking collectives  19.2 us (15%)
  local copies, waits for them, and re-layouts  2.36 us (2%)
    pallas_call x1, Pallas kernels, local(): pl.pallas_call(filter_kernel, out_shape=jax.ShapeDtypeStruct((OWN * 8, LA...  24.2 us
    all_to_all x1, blocking collectives, local(): lax.all_to_all(picked.reshape(GX, 1, SENT * LANES), 'gx', 0, 0, tiled=True)  19.2 us
    ppermute x3, waiting for transfers between devices, over_members(): lax.ppermute(x, 'ma', [(i, (i + s) % MA) for i in range(MA)])  17.9 us
    ppermute x1, starting transfers between devices, local(): high = lax.ppermute(both[:, :, :2], 'gx', backward)  14.4 us
    all_to_all x1, starting transfers between devices, local(): lax.all_to_all(owned.reshape(MA * GX, 1, CHUNK * LANES), ('ma', 'gx'), 0,...  12.4 us
    ppermute x3, starting transfers between devices, other_core(): return lax.ppermute(x, 'gy', [(0, 1), (1, 0)])  8.7 us
    ppermute x3, starting transfers between devices, over_members(): lax.ppermute(x, 'ma', [(i, (i + s) % MA) for i in range(MA)])  8.54 us
    ppermute x3, waiting for transfers between devices, other_core(): return lax.ppermute(x, 'gy', [(0, 1), (1, 0)])  4.62 us
  transfers between devices with their start and end apart: 9, of which 7 were waited for; matrix products, arithmetic and copies ran while one was open for 0% of the time, Pallas kernels for 2%

profile of v5, /device:TPU:1, one launch (start us, length us, event | category | flops | bytes accessed | tf_op | source)
XLA Modules:
  0.0 125.5 jit_solution(949858363502519047)
XLA Ops:
  0.0 0.9 constant_dynamic-update-slice_fusion.1
  0.9 0.7 constant_dynamic-update-slice_fusion
  1.6 14.4 %collective-permute-start.1 = (f32[22,2,2,128]{3,2,1,0:T(2,128)S(1)}, f32[22,2,2,128]{3,2,1,0:T(2,128)S(1)}, u32[]{:S(2)}, u32[]{:S(2)}) collective-permute-start(f32[22,2,2,128]{3,2,1,0:T(2,128)S(1)} %get-tuple-element.35), channel_id=1, source_target_pairs={{0,504},{8,0},{16,8},{24,16},{32,24},{40,32},{48,40},{56,48},{64,5... | collective-permute-start | bytes 135176 | tf_op jit(solution)/shard_map/ppermute | solution.py:333
  16.0 1.9 %collective-permute-start = (f32[22,2,2,128]{3,2,1,0:T(2,128)S(1)}, f32[22,2,2,128]{3,2,1,0:T(2,128)S(1)}, u32[]{:S(2)}, u32[]{:S(2)}) collective-permute-start(f32[22,2,2,128]{3,2,1,0:T(2,128)S(1)} %get-tuple-element.36), channel_id=1, source_target_pairs={{0,8},{8,16},{16,24},{24,32},{32,40},{40,48},{48,56},{56,64},{64,7... | collective-permute-start | bytes 135176 | tf_op jit(solution)/shard_map/ppermute | solution.py:332
  18.0 1.6 %prepare.1 = (f32[40,128]{1,0:T(8,128)}, f32[16,1024]{1,0:T(8,128)}) custom-call(s32[4]{0:T(128)} %refs_0_.1, s32[4,1024]{1,0:T(4,128)} %refs_1_.1, s32[4,1024]{1,0:T(4,128)} %refs_2_.1, f32[4,1024]{1,0:T(4,128)} %refs_3_.1, f32[4,1024]{1,0:T(4,128)} %refs_4_.1, f32[4,1024]{1,0:T(4,128)} %bitcast.14), custom_call_target="tpu_custom_call" | custom-call | flops 10000000 | bytes 2000000 | tf_op jit(solution)/shard_map/prepare/pallas_call | solution.py:334
  19.6 4.6 %collective-permute-done = f32[22,2,2,128]{3,2,1,0:T(2,128)S(1)} collective-permute-done((f32[22,2,2,128]{3,2,1,0:T(2,128)S(1)}, f32[22,2,2,128]{3,2,1,0:T(2,128)S(1)}, u32[]{:S(2)}, u32[]{:S(2)}) %collective-permute-start) | collective-permute-done | bytes 45088 | tf_op jit(solution)/shard_map/ppermute | solution.py:332
  24.2 4.0 %collective-permute-start.2 = (f32[352,128]{1,0:T(8,128)S(1)}, f32[352,128]{1,0:T(8,128)S(1)}, u32[]{:S(2)}, u32[]{:S(2)}) collective-permute-start(f32[352,128]{1,0:T(8,128)S(1)} %bitcast.9), channel_id=1, source_target_pairs={{0,4},{4,0},{1,5},{5,1},{2,6},{6,2},{3,7},{7,3},{8,12},{12,8},{9,1... | collective-permute-start | bytes 540680 | tf_op jit(solution)/shard_map/ppermute | solution.py:315
  28.2 1.0 collective-permute-done.2.other_ref
  29.3 0.7 copy-done.1
  30.0 3.6 %advect.1 = (f32[160,128]{1,0:T(8,128)S(1)}, f32[704,128]{1,0:T(8,128)S(1)}) custom-call(f32[352,128]{1,0:T(8,128)S(1)} %bitcast.10, f32[352,128]{1,0:T(8,128)S(1)} %collective-permute-done.2.other_ref, f32[40,128]{1,0:T(8,128)S(1)} %copy-done.1), custom_call_target="tpu_custom_call" | custom-call | flops 10000000 | bytes 1000000 | tf_op jit(solution)/shard_map/advect/pallas_call | solution.py:355
  33.6 19.2 %all_to_all.10 = f32[64,1,1408]{2,1,0:T(1,128)S(1)} all-to-all(f32[64,1,1408]{2,1,0:T(1,128)S(1)} %bitcast.13), channel_id=1, replica_groups=mesh['gx'=64,'gy'=2,'ma'=4] {'gx'}, dimensions={0} | all-to-all | bytes 720896 | tf_op jit(solution)/shard_map/all_to_all | solution.py:369
  52.8 0.9 owner.1
  53.7 12.4 %all-to-all-start.1 = ((f32[256,1,640]{2,1,0:T(1,128)}), f32[256,1,640]{2,1,0:T(1,128)S(1)}, u32[]{:S(2)}, u32[]{:S(2)}) async-start(f32[256,1,640]{2,1,0:T(1,128)} %bitcast.4), calls=%async_computation.1 | async-start | bytes 1310720 | tf_op jit(solution)/shard_map/all_to_all | solution.py:389
  66.1 4.0 %collective-permute-start.5 = (f32[544,128]{1,0:T(8,128)S(1)}, f32[544,128]{1,0:T(8,128)S(1)}, u32[]{:S(2)}, u32[]{:S(2)}) collective-permute-start(f32[544,128]{1,0:T(8,128)S(1)} %weights.1.refs_0_), channel_id=1, source_target_pairs={{0,3},{1,0},{2,1},{3,2},{4,7},{5,4},{6,5},{7,6},{8,11},{9,8},{10,9... | collective-permute-start | bytes 835592 | tf_op jit(solution)/shard_map/ppermute | solution.py:323
  70.1 1.9 %collective-permute-start.4 = (f32[544,128]{1,0:T(8,128)S(1)}, f32[544,128]{1,0:T(8,128)S(1)}, u32[]{:S(2)}, u32[]{:S(2)}) collective-permute-start(f32[544,128]{1,0:T(8,128)S(1)} %weights.1.refs_0_), channel_id=1, source_target_pairs={{0,2},{1,3},{2,0},{3,1},{4,6},{5,7},{6,4},{7,5},{8,10},{9,11},{10,... | collective-permute-start | bytes 835592 | tf_op jit(solution)/shard_map/ppermute | solution.py:323
  72.1 2.6 %collective-permute-start.3 = (f32[544,128]{1,0:T(8,128)S(1)}, f32[544,128]{1,0:T(8,128)S(1)}, u32[]{:S(2)}, u32[]{:S(2)}) collective-permute-start(f32[544,128]{1,0:T(8,128)S(1)} %weights.1.refs_0_), channel_id=1, source_target_pairs={{0,1},{1,2},{2,3},{3,0},{4,5},{5,6},{6,7},{7,4},{8,9},{9,10},{10,1... | collective-permute-start | bytes 835592 | tf_op jit(solution)/shard_map/ppermute | solution.py:323
  74.7 5.0 %collective-permute-done.5.refs_3_ = f32[544,128]{1,0:T(8,128)S(1)} collective-permute-done((f32[544,128]{1,0:T(8,128)S(1)}, f32[544,128]{1,0:T(8,128)S(1)}, u32[]{:S(2)}, u32[]{:S(2)}) %collective-permute-start.5) | collective-permute-done | bytes 278560 | tf_op jit(solution)/shard_map/ppermute | solution.py:323
  79.7 4.7 %collective-permute-done.4.refs_2_ = f32[544,128]{1,0:T(8,128)S(1)} collective-permute-done((f32[544,128]{1,0:T(8,128)S(1)}, f32[544,128]{1,0:T(8,128)S(1)}, u32[]{:S(2)}, u32[]{:S(2)}) %collective-permute-start.4) | collective-permute-done | bytes 278560 | tf_op jit(solution)/shard_map/ppermute | solution.py:323
  84.4 8.2 %collective-permute-done.3.refs_1_ = f32[544,128]{1,0:T(8,128)S(1)} collective-permute-done((f32[544,128]{1,0:T(8,128)S(1)}, f32[544,128]{1,0:T(8,128)S(1)}, u32[]{:S(2)}, u32[]{:S(2)}) %collective-permute-start.3) | collective-permute-done | bytes 278560 | tf_op jit(solution)/shard_map/ppermute | solution.py:323
  92.6 2.4 %collective-permute-start.6 = (f32[1536,128]{1,0:T(8,128)S(1)}, f32[1536,128]{1,0:T(8,128)S(1)}, u32[]{:S(2)}, u32[]{:S(2)}) collective-permute-start(f32[1536,128]{1,0:T(8,128)S(1)} %get-tuple-element.29.own_ref), channel_id=1, source_target_pairs={{0,4},{4,0},{1,5},{5,1},{2,6},{6,2},{3,7},{7,3},{8,12},{12,8},{9,1... | collective-permute-start | bytes 2359304 | tf_op jit(solution)/shard_map/ppermute | solution.py:315
  95.0 1.9 %collective-permute-done.6.other_ref = f32[1536,128]{1,0:T(8,128)S(1)} collective-permute-done((f32[1536,128]{1,0:T(8,128)S(1)}, f32[1536,128]{1,0:T(8,128)S(1)}, u32[]{:S(2)}, u32[]{:S(2)}) %collective-permute-start.6) | collective-permute-done | bytes 786464 | tf_op jit(solution)/shard_map/ppermute | solution.py:315
  97.4 2.3 %collective-permute-start.7 = (f32[1280,128]{1,0:T(8,128)S(1)}, f32[1280,128]{1,0:T(8,128)S(1)}, u32[]{:S(2)}, u32[]{:S(2)}) collective-permute-start(f32[1280,128]{1,0:T(8,128)S(1)} %bitcast.11), channel_id=1, source_target_pairs={{0,4},{4,0},{1,5},{5,1},{2,6},{6,2},{3,7},{7,3},{8,12},{12,8},{9,1... | collective-permute-start | bytes 1966088 | tf_op jit(solution)/shard_map/ppermute | solution.py:315
  99.7 1.7 %collective-permute-done.7.came_o_ref = f32[1280,128]{1,0:T(8,128)S(1)} collective-permute-done((f32[1280,128]{1,0:T(8,128)S(1)}, f32[1280,128]{1,0:T(8,128)S(1)}, u32[]{:S(2)}, u32[]{:S(2)}) %collective-permute-start.7) | collective-permute-done | bytes 655392 | tf_op jit(solution)/shard_map/ppermute | solution.py:315
  101.4 24.2 %filter.1 = f32[160,128]{1,0:T(8,128)} custom-call(f32[1280,128]{1,0:T(8,128)S(1)} %bitcast.12, f32[1280,128]{1,0:T(8,128)S(1)} %collective-permute-done.7.came_o_ref, bf16[9216,128]{1,0:T(8,128)(2,1)S(1)} %tapers.1, f32[16,1024]{1,0:T(8,128)S(1)} %copy-done, f32[640,128]{1,0:T(8,128)S(1)} %get-tuple-element.34.state_ref), custom_call_target="tpu_custom_call" | custom-call | flops 3000000000 | bytes 4000000 | tf_op jit(solution)/shard_map/filter/pallas_call | solution.py:417
  (10 shorter events, 0.6 us)
Async XLA Ops:
  1.6 17.9 %collective-permute-start.1 = (f32[22,2,2,128]{3,2,1,0:T(2,128)S(1)}, f32[22,2,2,128]{3,2,1,0:T(2,128)S(1)}, u32[]{:S(2)}, u32[]{:S(2)}) collective-permute-start(f32[22,2,2,128]{3,2,1,0:T(2,128)S(1)} %get-tuple-element.35), channel_id=1, source_target_pairs={{0,504},{8,0},{16,8},{24,16},{32,24},{40,32},{48,40},{56,48},{64,5... | collective-permute-start | bytes 135176 | tf_op jit(solution)/shard_map/ppermute | solution.py:333
  16.0 8.1 %collective-permute-start = (f32[22,2,2,128]{3,2,1,0:T(2,128)S(1)}, f32[22,2,2,128]{3,2,1,0:T(2,128)S(1)}, u32[]{:S(2)}, u32[]{:S(2)}) collective-permute-start(f32[22,2,2,128]{3,2,1,0:T(2,128)S(1)} %get-tuple-element.36), channel_id=1, source_target_pairs={{0,8},{8,16},{16,24},{24,32},{32,40},{40,48},{48,56},{56,64},{64,7... | collective-permute-start | bytes 135176 | tf_op jit(solution)/shard_map/ppermute | solution.py:332
  24.2 5.0 %collective-permute-start.2 = (f32[352,128]{1,0:T(8,128)S(1)}, f32[352,128]{1,0:T(8,128)S(1)}, u32[]{:S(2)}, u32[]{:S(2)}) collective-permute-start(f32[352,128]{1,0:T(8,128)S(1)} %bitcast.9), channel_id=1, source_target_pairs={{0,4},{4,0},{1,5},{5,1},{2,6},{6,2},{3,7},{7,3},{8,12},{12,8},{9,1... | collective-permute-start | bytes 540680 | tf_op jit(solution)/shard_map/ppermute | solution.py:315
  29.3 0.7 copy-start.1
  33.6 63.3 %copy-start = (f32[16,1024]{1,0:T(8,128)S(1)}, f32[16,1024]{1,0:T(8,128)}, u32[]{:S(2)}) copy-start(f32[16,1024]{1,0:T(8,128)} %get-tuple-element.30.obs_ref) | copy-start | bytes 196612
  53.7 43.6 %all-to-all-start.1 = ((f32[256,1,640]{2,1,0:T(1,128)}), f32[256,1,640]{2,1,0:T(1,128)S(1)}, u32[]{:S(2)}, u32[]{:S(2)}) async-start(f32[256,1,640]{2,1,0:T(1,128)} %bitcast.4), calls=%async_computation.1 | async-start | bytes 1310720 | tf_op jit(solution)/shard_map/all_to_all | solution.py:389
  66.1 13.5 %collective-permute-start.5 = (f32[544,128]{1,0:T(8,128)S(1)}, f32[544,128]{1,0:T(8,128)S(1)}, u32[]{:S(2)}, u32[]{:S(2)}) collective-permute-start(f32[544,128]{1,0:T(8,128)S(1)} %weights.1.refs_0_), channel_id=1, source_target_pairs={{0,3},{1,0},{2,1},{3,2},{4,7},{5,4},{6,5},{7,6},{8,11},{9,8},{10,9... | collective-permute-start | bytes 835592 | tf_op jit(solution)/shard_map/ppermute | solution.py:323
  70.1 14.2 %collective-permute-start.4 = (f32[544,128]{1,0:T(8,128)S(1)}, f32[544,128]{1,0:T(8,128)S(1)}, u32[]{:S(2)}, u32[]{:S(2)}) collective-permute-start(f32[544,128]{1,0:T(8,128)S(1)} %weights.1.refs_0_), channel_id=1, source_target_pairs={{0,2},{1,3},{2,0},{3,1},{4,6},{5,7},{6,4},{7,5},{8,10},{9,11},{10,... | collective-permute-start | bytes 835592 | tf_op jit(solution)/shard_map/ppermute | solution.py:323
  72.1 20.5 %collective-permute-start.3 = (f32[544,128]{1,0:T(8,128)S(1)}, f32[544,128]{1,0:T(8,128)S(1)}, u32[]{:S(2)}, u32[]{:S(2)}) collective-permute-start(f32[544,128]{1,0:T(8,128)S(1)} %weights.1.refs_0_), channel_id=1, source_target_pairs={{0,1},{1,2},{2,3},{3,0},{4,5},{5,6},{6,7},{7,4},{8,9},{9,10},{10,1... | collective-permute-start | bytes 835592 | tf_op jit(solution)/shard_map/ppermute | solution.py:323
  92.6 4.3 %collective-permute-start.6 = (f32[1536,128]{1,0:T(8,128)S(1)}, f32[1536,128]{1,0:T(8,128)S(1)}, u32[]{:S(2)}, u32[]{:S(2)}) collective-permute-start(f32[1536,128]{1,0:T(8,128)S(1)} %get-tuple-element.29.own_ref), channel_id=1, source_target_pairs={{0,4},{4,0},{1,5},{5,1},{2,6},{6,2},{3,7},{7,3},{8,12},{12,8},{9,1... | collective-permute-start | bytes 2359304 | tf_op jit(solution)/shard_map/ppermute | solution.py:315
  97.4 4.0 %collective-permute-start.7 = (f32[1280,128]{1,0:T(8,128)S(1)}, f32[1280,128]{1,0:T(8,128)S(1)}, u32[]{:S(2)}, u32[]{:S(2)}) collective-permute-start(f32[1280,128]{1,0:T(8,128)S(1)} %bitcast.11), channel_id=1, source_target_pairs={{0,4},{4,0},{1,5},{5,1},{2,6},{6,2},{3,7},{7,3},{8,12},{12,8},{9,1... | collective-permute-start | bytes 1966088 | tf_op jit(solution)/shard_map/ppermute | solution.py:315

commit v6 on v4

--- a/solution.py
+++ b/solution.py
@@ -20,7 +20,7 @@
 QUARTER = (BLOCKS - 1) * GROUPS // MA
 SENT = CHUNK + QUARTER
 TAPERS = (BLOCKS - 1) * GROUPS * 2 * LANES
-ROWS_O = 256
+ROWS_O = 1024
 F32 = jnp.float32
 BF16 = jnp.bfloat16
 VMEM = pl.BlockSpec(memory_space=pltpu.VMEM)
@@ -84,19 +84,25 @@
             work[0, at, :] = twice[2:6]
             work[1, at, :] = twice_o[2:6]
 
-    send = index_ref[pl.ds(32, QUARTER), :]
-    for g in range(2 * GROUPS):
-        y = jnp.broadcast_to(index_ref[pl.ds(g, 1), :].astype(jnp.int32), (24, LANES))
-        part = jnp.broadcast_to(index_ref[pl.ds(g + 16, 1), :].astype(jnp.int32), (24, LANES))
-        total = jnp.zeros((24, LANES), F32)
+    eight = jnp.concatenate(
+        [jnp.zeros((CHUNK, LANES), F32), index_ref[pl.ds(32, QUARTER), :]] * 8, axis=0
+    )
+    for i in range(GX // 8):
+        picked_ref[pl.ds(i * 8 * SENT, 8 * SENT), :] = eight
+    for half in range(2):
+        groups = range(half * GROUPS, (half + 1) * GROUPS)
+        ys = [jnp.broadcast_to(index_ref[pl.ds(g, 1), :].astype(jnp.int32), (24, LANES)) for g in groups]
+        parts = [jnp.broadcast_to(index_ref[pl.ds(g + 16, 1), :], (24, LANES)) for g in groups]
+        totals = [jnp.zeros((24, LANES), F32)] * GROUPS
         for c in range(16):
             source = work[c // 8, pl.ds(c % 8, 24, stride=8), :]
-            found = jnp.take_along_axis(source, y, axis=1, mode="promise_in_bounds")
-            total = jnp.where(part == c, found, total)
-        for i in range(MA):
-            at = (i * 2 * GROUPS + g) * SENT
-            picked_ref[pl.ds(at, CHUNK), :] = total[i * CHUNK : (i + 1) * CHUNK]
-            picked_ref[pl.ds(at + CHUNK, QUARTER), :] = send
+            for j in range(GROUPS):
+                found = jnp.take_along_axis(source, ys[j], axis=1, mode="promise_in_bounds")
+                totals[j] = jnp.where(parts[j] == c, found, totals[j])
+        for j, g in enumerate(groups):
+            for i in range(MA):
+                at = (i * 2 * GROUPS + g) * SENT
+                picked_ref[pl.ds(at, CHUNK), :] = totals[j][i * CHUNK : (i + 1) * CHUNK]
 
 
 def prepare_kernel(*refs):
@@ -190,6 +196,7 @@
     b_high,
     b_both,
     increments,
+    first_block,
 ):
     gy = lax.axis_index("gy")
     denom = MEMBERS - 1.0
@@ -203,7 +210,10 @@
             full = jnp.concatenate(
                 [block - mean, mean, jnp.zeros((LANES - MEMBERS - 1, LANES), F32)], axis=0
             )
-            xt[pl.ds((half * 16 + g) * LANES, LANES), :] = full.T
+            if half == 0 and g < GROUPS:
+                first_block[:, pl.ds(g * LANES, LANES)] = full
+            else:
+                xt[pl.ds((half * 16 + g) * LANES, LANES), :] = full.T
 
     @pl.when(gy == 0)
     def _():
@@ -219,9 +229,12 @@
     member_row = lax.broadcasted_iota(jnp.int32, (LANES, OBS), 0)
     increments[...] = jnp.zeros((LANES, LANES), F32)
     for k in range(BLOCKS):
-        now = jnp.concatenate(
-            [xt[pl.ds((k * GROUPS + g) * LANES, LANES), :].T for g in range(GROUPS)], axis=1
-        )
+        if k == 0:
+            now = first_block[...]
+        else:
+            now = jnp.concatenate(
+                [xt[pl.ds((k * GROUPS + g) * LANES, LANES), :].T for g in range(GROUPS)], axis=1
+            )
         anomaly = jnp.where(member_row < MEMBERS, now, 0.0)
         mean = now[MEMBERS : MEMBERS + 1]
         variance = jnp.sum(anomaly * anomaly, axis=0, keepdims=True) / denom
@@ -303,7 +316,9 @@
     centered = jnp.concatenate(
         [jnp.concatenate(tiles, axis=1), jnp.zeros((LANES - MEMBERS, CELLS), F32)], axis=0
     )
-    update = jnp.dot(transform, centered, precision=lax.Precision.HIGHEST, preferred_element_type=F32)
+    c_high, c_low = split(centered)
+    t_high, t_low = split(transform)
+    update = dot_nn(t_high, c_high) + dot_nn(t_low, c_high) + dot_nn(t_high, c_low)
     for c in range(8):
         at = pl.ds(c, OWN, stride=8)
         out_ref[at, :] = state_ref[at, :] + update[:OWN, c * LANES : (c + 1) * LANES]
@@ -388,15 +403,16 @@
         owned.reshape(MA * GX, 1, CHUNK * LANES), ("ma", "gx"), 0, 0, tiled=True
     ).reshape(-1, LANES)
     weights = jnp.concatenate([weights] + over_members(weights), axis=0)
+    came, weights = lax.optimization_barrier((came, weights))
     tapers = pl.pallas_call(
         tapers_kernel,
         out_shape=jax.ShapeDtypeStruct((TAPERS + (BLOCKS - 1) * OBS, LANES), BF16),
         in_specs=[VMEM] * 3,
         out_specs=VMEM,
         compiler_params=params(4),
+        cost_estimate=pl.CostEstimate(flops=1000, bytes_accessed=1000, transcendentals=0),
         name="tapers",
     )(weights, other_core(weights), observed)
-    came, tapers = lax.optimization_barrier((came, tapers))
     came_beside = other_core(came)
 
     out = pl.pallas_call(
@@ -409,6 +425,7 @@
             pltpu.VMEM((OBS, LANES), BF16),
             pltpu.VMEM((OBS, 2 * LANES), BF16),
             pltpu.VMEM((LANES, LANES), F32),
+            pltpu.VMEM((LANES, OBS), F32),
         ],
         compiler_params=params(32),
         cost_estimate=pl.CostEstimate(flops=3_000_000_000, bytes_accessed=4_000_000, transcendentals=0),

time: 124 us -> 120 us (0.968)
  Pallas kernels: 31.4 us -> 28.1 us
  waiting for transfers between devices: 17.3 us -> 15.3 us
  starting transfers between devices: 71.6 us -> 73.4 us
    pallas_call x1, Pallas kernels: 24.2 us -> 20.1 us  [local(): pl.pallas_call(filter_kernel, out_shape=jax.ShapeDtypeStruct((OWN * 8, LA...]
    ppermute x3, waiting for transfers between devices: 4.62 us -> 2.66 us  [other_core(): return lax.ppermute(x, 'gy', [(0, 1), (1, 0)])]
    ppermute x3, starting transfers between devices: 9.81 us -> 11.7 us  [other_core(): return lax.ppermute(x, 'gy', [(0, 1), (1, 0)])]
  transfers between devices with their start and end apart: 13 -> 13, of which waited for: 7 -> 6; matrix products, arithmetic and copies ran while one was open for 0% -> 0% of each run, Pallas kernels for 2% -> 2%
where the time goes in v6:
time: 120 us; the launch traced here: 119 us
  starting transfers between devices  73.4 us (61%)
  Pallas kernels  28.1 us (23%)
  waiting for transfers between devices  15.3 us (13%)
  local copies, waits for them, and re-layouts  2.36 us (2%)
    ppermute x6, starting transfers between devices, over_members(): lax.ppermute(x, 'ma', [(i, (i + s) % MA) for i in range(MA)])  20.4 us
    pallas_call x1, Pallas kernels, local(): pl.pallas_call(filter_kernel, out_shape=jax.ShapeDtypeStruct((OWN * 8, LA...  20.1 us
    all_to_all x1, starting transfers between devices, local(): lax.all_to_all(owned.reshape(MA * GX, 1, CHUNK * LANES), ('ma', 'gx'), 0,...  16.2 us
    ppermute x3, starting transfers between devices, other_core(): return lax.ppermute(x, 'gy', [(0, 1), (1, 0)])  11.7 us
    ppermute x1, starting transfers between devices, local(): high = lax.ppermute(both[:, :, :2], 'gx', backward)  11.5 us
    ppermute x6, waiting for transfers between devices, over_members(): lax.ppermute(x, 'ma', [(i, (i + s) % MA) for i in range(MA)])  11.3 us
    all_to_all x1, starting transfers between devices, local(): lax.all_to_all(picked.reshape(GX, 1, SENT * LANES), 'gx', 0, 0, tiled=True)  8.8 us
    pallas_call x1, Pallas kernels, local(): pl.pallas_call(advect_kernel, out_shape=(jax.ShapeDtypeStruct((OWN * 8, L...  5.02 us
  transfers between devices with their start and end apart: 13, of which 6 were waited for; matrix products, arithmetic and copies ran while one was open for 0% of the time, Pallas kernels for 2%

profile of v6, /device:TPU:1, one launch (start us, length us, event | category | flops | bytes accessed | tf_op | source)
XLA Modules:
  0.0 119.5 jit_solution(5413268437522476517)
XLA Ops:
  0.0 0.9 constant_dynamic-update-slice_fusion.1
  1.6 4.8 %collective-permute-start = (f32[22,2,2,128]{3,2,1,0:T(2,128)S(1)}, f32[22,2,2,128]{3,2,1,0:T(2,128)S(1)}, u32[]{:S(2)}, u32[]{:S(2)}) collective-permute-start(f32[22,2,2,128]{3,2,1,0:T(2,128)S(1)} %get-tuple-element.34), channel_id=1, source_target_pairs={{0,8},{8,16},{16,24},{24,32},{32,40},{40,48},{48,56},{56,64},{64,7... | collective-permute-start | bytes 135176 | tf_op jit(solution)/shard_map/ppermute | solution.py:345
  6.5 11.5 %collective-permute-start.1 = (f32[22,2,2,128]{3,2,1,0:T(2,128)S(1)}, f32[22,2,2,128]{3,2,1,0:T(2,128)S(1)}, u32[]{:S(2)}, u32[]{:S(2)}) collective-permute-start(f32[22,2,2,128]{3,2,1,0:T(2,128)S(1)} %get-tuple-element.33), channel_id=1, source_target_pairs={{0,504},{8,0},{16,8},{24,16},{32,24},{40,32},{48,40},{56,48},{64,5... | collective-permute-start | bytes 135176 | tf_op jit(solution)/shard_map/ppermute | solution.py:346
  18.0 1.6 %prepare.1 = (f32[40,128]{1,0:T(8,128)}, f32[16,1024]{1,0:T(8,128)}) custom-call(s32[4]{0:T(128)} %refs_0_.1, s32[4,1024]{1,0:T(4,128)} %refs_1_.1, s32[4,1024]{1,0:T(4,128)} %refs_2_.1, f32[4,1024]{1,0:T(4,128)} %refs_3_.1, f32[4,1024]{1,0:T(4,128)} %refs_4_.1, f32[4,1024]{1,0:T(4,128)} %bitcast.13), custom_call_target="tpu_custom_call" | custom-call | flops 10000000 | bytes 2000000 | tf_op jit(solution)/shard_map/prepare/pallas_call | solution.py:347
  19.7 2.9 %collective-permute-start.2 = (f32[352,128]{1,0:T(8,128)S(1)}, f32[352,128]{1,0:T(8,128)S(1)}, u32[]{:S(2)}, u32[]{:S(2)}) collective-permute-start(f32[352,128]{1,0:T(8,128)S(1)} %bitcast.9), channel_id=1, source_target_pairs={{0,4},{4,0},{1,5},{5,1},{2,6},{6,2},{3,7},{7,3},{8,12},{12,8},{9,1... | collective-permute-start | bytes 540680 | tf_op jit(solution)/shard_map/ppermute | solution.py:328
  22.6 1.0 collective-permute-done.2.other_ref
  24.4 5.0 %advect.1 = (f32[160,128]{1,0:T(8,128)S(1)}, f32[704,128]{1,0:T(8,128)}) custom-call(f32[352,128]{1,0:T(8,128)S(1)} %bitcast.10, f32[352,128]{1,0:T(8,128)S(1)} %collective-permute-done.2.other_ref, f32[40,128]{1,0:T(8,128)S(1)} %copy-done.1), custom_call_target="tpu_custom_call" | custom-call | flops 10000000 | bytes 1000000 | tf_op jit(solution)/shard_map/advect/pallas_call | solution.py:368
  29.4 8.8 %all-to-all-start = ((f32[64,1,1408]{2,1,0:T(1,128)}), f32[64,1,1408]{2,1,0:T(1,128)S(1)}, u32[]{:S(2)}, u32[]{:S(2)}) async-start(f32[64,1,1408]{2,1,0:T(1,128)} %bitcast.2), calls=%async_computation | async-start | bytes 720896 | tf_op jit(solution)/shard_map/all_to_all | solution.py:382
  38.2 3.3 %collective-permute-start.3 = (f32[160,128]{1,0:T(8,128)S(1)}, f32[160,128]{1,0:T(8,128)S(1)}, u32[]{:S(2)}, u32[]{:S(2)}) collective-permute-start(f32[160,128]{1,0:T(8,128)S(1)} %get-tuple-element.25.state_ref), channel_id=1, source_target_pairs={{0,1},{1,2},{2,3},{3,0},{4,5},{5,6},{6,7},{7,4},{8,9},{9,10},{10,1... | collective-permute-start | bytes 245768 | tf_op jit(solution)/shard_map/ppermute | solution.py:336
  41.5 4.4 %collective-permute-start.4 = (f32[160,128]{1,0:T(8,128)S(1)}, f32[160,128]{1,0:T(8,128)S(1)}, u32[]{:S(2)}, u32[]{:S(2)}) collective-permute-start(f32[160,128]{1,0:T(8,128)S(1)} %get-tuple-element.25.state_ref), channel_id=1, source_target_pairs={{0,2},{1,3},{2,0},{3,1},{4,6},{5,7},{6,4},{7,5},{8,10},{9,11},{10,... | collective-permute-start | bytes 245768 | tf_op jit(solution)/shard_map/ppermute | solution.py:336
  45.8 3.1 %collective-permute-start.5 = (f32[160,128]{1,0:T(8,128)S(1)}, f32[160,128]{1,0:T(8,128)S(1)}, u32[]{:S(2)}, u32[]{:S(2)}) collective-permute-start(f32[160,128]{1,0:T(8,128)S(1)} %get-tuple-element.25.state_ref), channel_id=1, source_target_pairs={{0,3},{1,0},{2,1},{3,2},{4,7},{5,4},{6,5},{7,6},{8,11},{9,8},{10,9... | collective-permute-start | bytes 245768 | tf_op jit(solution)/shard_map/ppermute | solution.py:336
  48.9 2.4 %collective-permute-done.5.gathered_3 = f32[160,128]{1,0:T(8,128)S(1)} collective-permute-done((f32[160,128]{1,0:T(8,128)S(1)}, f32[160,128]{1,0:T(8,128)S(1)}, u32[]{:S(2)}, u32[]{:S(2)}) %collective-permute-start.5) | collective-permute-done | bytes 81952 | tf_op jit(solution)/shard_map/ppermute | solution.py:336
  51.3 1.3 %all-to-all-done = f32[64,1,1408]{2,1,0:T(1,128)S(1)} async-done(((f32[64,1,1408]{2,1,0:T(1,128)}), f32[64,1,1408]{2,1,0:T(1,128)S(1)}, u32[]{:S(2)}, u32[]{:S(2)}) %all-to-all-start) | async-done | bytes 360480 | tf_op jit(solution)/shard_map/all_to_all | solution.py:382
  52.6 0.9 owner.1
  53.6 16.2 %all-to-all-start.1 = ((f32[256,1,640]{2,1,0:T(1,128)}), f32[256,1,640]{2,1,0:T(1,128)S(1)}, u32[]{:S(2)}, u32[]{:S(2)}) async-start(f32[256,1,640]{2,1,0:T(1,128)} %bitcast.4), calls=%async_computation.1 | async-start | bytes 1310720 | tf_op jit(solution)/shard_map/all_to_all | solution.py:402
  69.8 1.9 %collective-permute-start.6 = (f32[384,128]{1,0:T(8,128)S(1)}, f32[384,128]{1,0:T(8,128)S(1)}, u32[]{:S(2)}, u32[]{:S(2)}) collective-permute-start(f32[384,128]{1,0:T(8,128)S(1)} %weights.1), channel_id=1, source_target_pairs={{0,1},{1,2},{2,3},{3,0},{4,5},{5,6},{6,7},{7,4},{8,9},{9,10},{10,1... | collective-permute-start | bytes 589832 | tf_op jit(solution)/shard_map/ppermute | solution.py:336
  71.7 5.2 %collective-permute-start.7 = (f32[384,128]{1,0:T(8,128)S(1)}, f32[384,128]{1,0:T(8,128)S(1)}, u32[]{:S(2)}, u32[]{:S(2)}) collective-permute-start(f32[384,128]{1,0:T(8,128)S(1)} %weights.1), channel_id=1, source_target_pairs={{0,2},{1,3},{2,0},{3,1},{4,6},{5,7},{6,4},{7,5},{8,10},{9,11},{10,... | collective-permute-start | bytes 589832 | tf_op jit(solution)/shard_map/ppermute | solution.py:336
  76.9 2.7 %collective-permute-start.8 = (f32[384,128]{1,0:T(8,128)S(1)}, f32[384,128]{1,0:T(8,128)S(1)}, u32[]{:S(2)}, u32[]{:S(2)}) collective-permute-start(f32[384,128]{1,0:T(8,128)S(1)} %weights.1), channel_id=1, source_target_pairs={{0,3},{1,0},{2,1},{3,2},{4,7},{5,4},{6,5},{7,6},{8,11},{9,8},{10,9... | collective-permute-start | bytes 589832 | tf_op jit(solution)/shard_map/ppermute | solution.py:336
  79.6 8.1 %collective-permute-done.7 = f32[384,128]{1,0:T(8,128)S(1)} collective-permute-done((f32[384,128]{1,0:T(8,128)S(1)}, f32[384,128]{1,0:T(8,128)S(1)}, u32[]{:S(2)}, u32[]{:S(2)}) %collective-permute-start.7) | collective-permute-done | bytes 196640 | tf_op jit(solution)/shard_map/ppermute | solution.py:336
  87.7 0.8 collective-permute-done.8
  88.5 6.8 %collective-permute-start.10 = (f32[1536,128]{1,0:T(8,128)S(1)}, f32[1536,128]{1,0:T(8,128)S(1)}, u32[]{:S(2)}, u32[]{:S(2)}) collective-permute-start(f32[1536,128]{1,0:T(8,128)S(1)} %pad_maximum_fusion.own_ref), channel_id=1, source_target_pairs={{0,4},{4,0},{1,5},{5,1},{2,6},{6,2},{3,7},{7,3},{8,12},{12,8},{9,1... | collective-permute-start | bytes 2359304 | tf_op jit(solution)/shard_map/ppermute | solution.py:328
  95.4 1.9 %collective-permute-start.9 = (f32[1280,128]{1,0:T(8,128)S(1)}, f32[1280,128]{1,0:T(8,128)S(1)}, u32[]{:S(2)}, u32[]{:S(2)}) collective-permute-start(f32[1280,128]{1,0:T(8,128)S(1)} %bitcast.11), channel_id=1, source_target_pairs={{0,4},{4,0},{1,5},{5,1},{2,6},{6,2},{3,7},{7,3},{8,12},{12,8},{9,1... | collective-permute-start | bytes 1966088 | tf_op jit(solution)/shard_map/ppermute | solution.py:328
  97.7 1.6 %collective-permute-done.9.came_o_ref = f32[1280,128]{1,0:T(8,128)S(1)} collective-permute-done((f32[1280,128]{1,0:T(8,128)S(1)}, f32[1280,128]{1,0:T(8,128)S(1)}, u32[]{:S(2)}, u32[]{:S(2)}) %collective-permute-start.9) | collective-permute-done | bytes 655392 | tf_op jit(solution)/shard_map/ppermute | solution.py:328
  99.4 20.1 %filter.1 = f32[160,128]{1,0:T(8,128)} custom-call(f32[1280,128]{1,0:T(8,128)S(1)} %bitcast.12, f32[1280,128]{1,0:T(8,128)S(1)} %collective-permute-done.9.came_o_ref, bf16[9216,128]{1,0:T(8,128)(2,1)S(1)} %tapers.1, f32[16,1024]{1,0:T(8,128)S(1)} %copy-done, f32[160,128]{1,0:T(8,128)S(1)} %collective-permute-done.3.gathered_1, ...), custom_call_target="tpu_custom_call" | custom-call | flops 3000000000 | bytes 4000000 | tf_op jit(solution)/shard_map/filter/pallas_call | solution.py:418
  (17 shorter events, 2.0 us)
Async XLA Ops:
  1.6 17.9 %collective-permute-start = (f32[22,2,2,128]{3,2,1,0:T(2,128)S(1)}, f32[22,2,2,128]{3,2,1,0:T(2,128)S(1)}, u32[]{:S(2)}, u32[]{:S(2)}) collective-permute-start(f32[22,2,2,128]{3,2,1,0:T(2,128)S(1)} %get-tuple-element.34), channel_id=1, source_target_pairs={{0,8},{8,16},{16,24},{24,32},{32,40},{40,48},{48,56},{56,64},{64,7... | collective-permute-start | bytes 135176 | tf_op jit(solution)/shard_map/ppermute | solution.py:345
  6.5 13.1 %collective-permute-start.1 = (f32[22,2,2,128]{3,2,1,0:T(2,128)S(1)}, f32[22,2,2,128]{3,2,1,0:T(2,128)S(1)}, u32[]{:S(2)}, u32[]{:S(2)}) collective-permute-start(f32[22,2,2,128]{3,2,1,0:T(2,128)S(1)} %get-tuple-element.33), channel_id=1, source_target_pairs={{0,504},{8,0},{16,8},{24,16},{32,24},{40,32},{48,40},{56,48},{64,5... | collective-permute-start | bytes 135176 | tf_op jit(solution)/shard_map/ppermute | solution.py:346
  19.7 4.0 %collective-permute-start.2 = (f32[352,128]{1,0:T(8,128)S(1)}, f32[352,128]{1,0:T(8,128)S(1)}, u32[]{:S(2)}, u32[]{:S(2)}) collective-permute-start(f32[352,128]{1,0:T(8,128)S(1)} %bitcast.9), channel_id=1, source_target_pairs={{0,4},{4,0},{1,5},{5,1},{2,6},{6,2},{3,7},{7,3},{8,12},{12,8},{9,1... | collective-permute-start | bytes 540680 | tf_op jit(solution)/shard_map/ppermute | solution.py:328
  23.6 0.7 copy-start.1
  29.4 23.3 %all-to-all-start = ((f32[64,1,1408]{2,1,0:T(1,128)}), f32[64,1,1408]{2,1,0:T(1,128)S(1)}, u32[]{:S(2)}, u32[]{:S(2)}) async-start(f32[64,1,1408]{2,1,0:T(1,128)} %bitcast.2), calls=%async_computation | async-start | bytes 720896 | tf_op jit(solution)/shard_map/all_to_all | solution.py:382
  38.2 59.1 %copy-start = (f32[16,1024]{1,0:T(8,128)S(1)}, f32[16,1024]{1,0:T(8,128)}, u32[]{:S(2)}) copy-start(f32[16,1024]{1,0:T(8,128)} %get-tuple-element.29.obs_ref) | copy-start | bytes 196612
  38.2 10.7 %collective-permute-start.3 = (f32[160,128]{1,0:T(8,128)S(1)}, f32[160,128]{1,0:T(8,128)S(1)}, u32[]{:S(2)}, u32[]{:S(2)}) collective-permute-start(f32[160,128]{1,0:T(8,128)S(1)} %get-tuple-element.25.state_ref), channel_id=1, source_target_pairs={{0,1},{1,2},{2,3},{3,0},{4,5},{5,6},{6,7},{7,4},{8,9},{9,10},{10,1... | collective-permute-start | bytes 245768 | tf_op jit(solution)/shard_map/ppermute | solution.py:336
  41.5 7.4 %collective-permute-start.4 = (f32[160,128]{1,0:T(8,128)S(1)}, f32[160,128]{1,0:T(8,128)S(1)}, u32[]{:S(2)}, u32[]{:S(2)}) collective-permute-start(f32[160,128]{1,0:T(8,128)S(1)} %get-tuple-element.25.state_ref), channel_id=1, source_target_pairs={{0,2},{1,3},{2,0},{3,1},{4,6},{5,7},{6,4},{7,5},{8,10},{9,11},{10,... | collective-permute-start | bytes 245768 | tf_op jit(solution)/shard_map/ppermute | solution.py:336
  45.8 5.5 %collective-permute-start.5 = (f32[160,128]{1,0:T(8,128)S(1)}, f32[160,128]{1,0:T(8,128)S(1)}, u32[]{:S(2)}, u32[]{:S(2)}) collective-permute-start(f32[160,128]{1,0:T(8,128)S(1)} %get-tuple-element.25.state_ref), channel_id=1, source_target_pairs={{0,3},{1,0},{2,1},{3,2},{4,7},{5,4},{6,5},{7,6},{8,11},{9,8},{10,9... | collective-permute-start | bytes 245768 | tf_op jit(solution)/shard_map/ppermute | solution.py:336
  53.6 35.0 %all-to-all-start.1 = ((f32[256,1,640]{2,1,0:T(1,128)}), f32[256,1,640]{2,1,0:T(1,128)S(1)}, u32[]{:S(2)}, u32[]{:S(2)}) async-start(f32[256,1,640]{2,1,0:T(1,128)} %bitcast.4), calls=%async_computation.1 | async-start | bytes 1310720 | tf_op jit(solution)/shard_map/all_to_all | solution.py:402
  69.8 9.8 %collective-permute-start.6 = (f32[384,128]{1,0:T(8,128)S(1)}, f32[384,128]{1,0:T(8,128)S(1)}, u32[]{:S(2)}, u32[]{:S(2)}) collective-permute-start(f32[384,128]{1,0:T(8,128)S(1)} %weights.1), channel_id=1, source_target_pairs={{0,1},{1,2},{2,3},{3,0},{4,5},{5,6},{6,7},{7,4},{8,9},{9,10},{10,1... | collective-permute-start | bytes 589832 | tf_op jit(solution)/shard_map/ppermute | solution.py:336
  71.7 16.0 %collective-permute-start.7 = (f32[384,128]{1,0:T(8,128)S(1)}, f32[384,128]{1,0:T(8,128)S(1)}, u32[]{:S(2)}, u32[]{:S(2)}) collective-permute-start(f32[384,128]{1,0:T(8,128)S(1)} %weights.1), channel_id=1, source_target_pairs={{0,2},{1,3},{2,0},{3,1},{4,6},{5,7},{6,4},{7,5},{8,10},{9,11},{10,... | collective-permute-start | bytes 589832 | tf_op jit(solution)/shard_map/ppermute | solution.py:336
  76.9 11.6 %collective-permute-start.8 = (f32[384,128]{1,0:T(8,128)S(1)}, f32[384,128]{1,0:T(8,128)S(1)}, u32[]{:S(2)}, u32[]{:S(2)}) collective-permute-start(f32[384,128]{1,0:T(8,128)S(1)} %weights.1), channel_id=1, source_target_pairs={{0,3},{1,0},{2,1},{3,2},{4,7},{5,4},{6,5},{7,6},{8,11},{9,8},{10,9... | collective-permute-start | bytes 589832 | tf_op jit(solution)/shard_map/ppermute | solution.py:336
  88.5 8.8 %collective-permute-start.10 = (f32[1536,128]{1,0:T(8,128)S(1)}, f32[1536,128]{1,0:T(8,128)S(1)}, u32[]{:S(2)}, u32[]{:S(2)}) collective-permute-start(f32[1536,128]{1,0:T(8,128)S(1)} %pad_maximum_fusion.own_ref), channel_id=1, source_target_pairs={{0,4},{4,0},{1,5},{5,1},{2,6},{6,2},{3,7},{7,3},{8,12},{12,8},{9,1... | collective-permute-start | bytes 2359304 | tf_op jit(solution)/shard_map/ppermute | solution.py:328
  95.4 4.0 %collective-permute-start.9 = (f32[1280,128]{1,0:T(8,128)S(1)}, f32[1280,128]{1,0:T(8,128)S(1)}, u32[]{:S(2)}, u32[]{:S(2)}) collective-permute-start(f32[1280,128]{1,0:T(8,128)S(1)} %bitcast.11), channel_id=1, source_target_pairs={{0,4},{4,0},{1,5},{5,1},{2,6},{6,2},{3,7},{7,3},{8,12},{12,8},{9,1... | collective-permute-start | bytes 1966088 | tf_op jit(solution)/shard_map/ppermute | solution.py:328

commit v7 on v6

--- a/solution.py
+++ b/solution.py
@@ -89,20 +89,17 @@
     )
     for i in range(GX // 8):
         picked_ref[pl.ds(i * 8 * SENT, 8 * SENT), :] = eight
-    for half in range(2):
-        groups = range(half * GROUPS, (half + 1) * GROUPS)
-        ys = [jnp.broadcast_to(index_ref[pl.ds(g, 1), :].astype(jnp.int32), (24, LANES)) for g in groups]
-        parts = [jnp.broadcast_to(index_ref[pl.ds(g + 16, 1), :], (24, LANES)) for g in groups]
-        totals = [jnp.zeros((24, LANES), F32)] * GROUPS
+    for g in range(2 * GROUPS):
+        y = jnp.broadcast_to(index_ref[pl.ds(g, 1), :].astype(jnp.int32), (24, LANES))
+        part = jnp.broadcast_to(index_ref[pl.ds(g + 16, 1), :], (24, LANES))
+        total = jnp.zeros((24, LANES), F32)
         for c in range(16):
             source = work[c // 8, pl.ds(c % 8, 24, stride=8), :]
-            for j in range(GROUPS):
-                found = jnp.take_along_axis(source, ys[j], axis=1, mode="promise_in_bounds")
-                totals[j] = jnp.where(parts[j] == c, found, totals[j])
-        for j, g in enumerate(groups):
-            for i in range(MA):
-                at = (i * 2 * GROUPS + g) * SENT
-                picked_ref[pl.ds(at, CHUNK), :] = totals[j][i * CHUNK : (i + 1) * CHUNK]
+            found = jnp.take_along_axis(source, y, axis=1, mode="promise_in_bounds")
+            total = jnp.where(part == c, found, total)
+        for i in range(MA):
+            at = (i * 2 * GROUPS + g) * SENT
+            picked_ref[pl.ds(at, CHUNK), :] = total[i * CHUNK : (i + 1) * CHUNK]
 
 
 def prepare_kernel(*refs):
@@ -381,7 +378,6 @@
 
     parts = lax.all_to_all(picked.reshape(GX, 1, SENT * LANES), "gx", 0, 0, tiled=True)
     gathered = over_members(state)
-    parts, gathered = lax.optimization_barrier((parts, gathered))
     parts = parts.reshape(-1, LANES)
     owned = pl.pallas_call(
         owner_kernel,
@@ -402,7 +398,9 @@
     came = lax.all_to_all(
         owned.reshape(MA * GX, 1, CHUNK * LANES), ("ma", "gx"), 0, 0, tiled=True
     ).reshape(-1, LANES)
-    weights = jnp.concatenate([weights] + over_members(weights), axis=0)
+    weights = [weights] + over_members(weights)
+    weights, gathered = lax.optimization_barrier((weights, gathered))
+    weights = jnp.concatenate(weights, axis=0)
     came, weights = lax.optimization_barrier((came, weights))
     tapers = pl.pallas_call(
         tapers_kernel,

time: 120 us -> 121 us (level)
  blocking collectives: 0 us -> 23.1 us
  starting transfers between devices: 73.4 us -> 53.9 us
  Pallas kernels: 28.1 us -> 26.6 us
    all_to_all x0 -> x1, blocking collectives: none -> 23.1 us  [local(): lax.all_to_all(picked.reshape(GX, 1, SENT * LANES), 'gx', 0, 0, tiled=True)]
    all_to_all x1 -> x0, starting transfers between devices: 8.8 us -> none  [local(): lax.all_to_all(picked.reshape(GX, 1, SENT * LANES), 'gx', 0, 0, tiled=True)]
    all_to_all x1, starting transfers between devices: 16.2 us -> 12.4 us  [local(): lax.all_to_all(owned.reshape(MA * GX, 1, CHUNK * LANES), ('ma', 'gx'), 0,...]
    ppermute x6, starting transfers between devices: 20.4 us -> 16.7 us  [over_members(): lax.ppermute(x, 'ma', [(i, (i + s) % MA) for i in range(MA)])]
    ppermute x3, starting transfers between devices: 11.7 us -> 8.53 us  [other_core(): return lax.ppermute(x, 'gy', [(0, 1), (1, 0)])]
    pallas_call x1, Pallas kernels: 5.02 us -> 3.58 us  [local(): pl.pallas_call(advect_kernel, out_shape=(jax.ShapeDtypeStruct((OWN * 8, L...]
    all_to_all x1 -> x0, waiting for transfers between devices: 1.33 us -> none  [local(): lax.all_to_all(picked.reshape(GX, 1, SENT * LANES), 'gx', 0, 0, tiled=True)]
  transfers between devices with their start and end apart: 13 -> 12, of which waited for: 6 -> 4; matrix products, arithmetic and copies ran while one was open for 0% -> 0% of each run, Pallas kernels for 2% -> 2%
where the time goes in v7:
time: 121 us
  starting transfers between devices  53.9 us (45%)
  Pallas kernels  26.6 us (22%)
  blocking collectives  23.1 us (19%)
  waiting for transfers between devices  14.3 us (12%)
  local copies, waits for them, and re-layouts  2.36 us (2%)
    all_to_all x1, blocking collectives, local(): lax.all_to_all(picked.reshape(GX, 1, SENT * LANES), 'gx', 0, 0, tiled=True)  23.1 us
    pallas_call x1, Pallas kernels, local(): pl.pallas_call(filter_kernel, out_shape=jax.ShapeDtypeStruct((OWN * 8, LA...  20.1 us
    ppermute x6, starting transfers between devices, over_members(): lax.ppermute(x, 'ma', [(i, (i + s) % MA) for i in range(MA)])  16.7 us
    all_to_all x1, starting transfers between devices, local(): lax.all_to_all(owned.reshape(MA * GX, 1, CHUNK * LANES), ('ma', 'gx'), 0,...  12.4 us
    ppermute x6, waiting for transfers between devices, over_members(): lax.ppermute(x, 'ma', [(i, (i + s) % MA) for i in range(MA)])  11.7 us
    ppermute x1, starting transfers between devices, local(): high = lax.ppermute(both[:, :, :2], 'gx', backward)  11.5 us
    ppermute x3, starting transfers between devices, other_core(): return lax.ppermute(x, 'gy', [(0, 1), (1, 0)])  8.53 us
    ppermute x1, starting transfers between devices, local(): low = lax.ppermute(both[:, :, 2:], 'gx', forward)  4.83 us
  transfers between devices with their start and end apart: 12, of which 4 were waited for; matrix products, arithmetic and copies ran while one was open for 0% of the time, Pallas kernels for 2%

profile of v7, /device:TPU:1, one launch (start us, length us, event | category | flops | bytes accessed | tf_op | source)
XLA Modules:
  0.0 120.6 jit_solution(4325832616187293060)
XLA Ops:
  0.0 0.9 constant_dynamic-update-slice_fusion.1
  0.9 0.7 constant_dynamic-update-slice_fusion
  1.6 4.8 %collective-permute-start = (f32[22,2,2,128]{3,2,1,0:T(2,128)S(1)}, f32[22,2,2,128]{3,2,1,0:T(2,128)S(1)}, u32[]{:S(2)}, u32[]{:S(2)}) collective-permute-start(f32[22,2,2,128]{3,2,1,0:T(2,128)S(1)} %get-tuple-element.40), channel_id=1, source_target_pairs={{0,8},{8,16},{16,24},{24,32},{32,40},{40,48},{48,56},{56,64},{64,7... | collective-permute-start | bytes 135176 | tf_op jit(solution)/shard_map/ppermute | solution.py:342
  6.5 11.5 %collective-permute-start.1 = (f32[22,2,2,128]{3,2,1,0:T(2,128)S(1)}, f32[22,2,2,128]{3,2,1,0:T(2,128)S(1)}, u32[]{:S(2)}, u32[]{:S(2)}) collective-permute-start(f32[22,2,2,128]{3,2,1,0:T(2,128)S(1)} %get-tuple-element.39), channel_id=1, source_target_pairs={{0,504},{8,0},{16,8},{24,16},{32,24},{40,32},{48,40},{56,48},{64,5... | collective-permute-start | bytes 135176 | tf_op jit(solution)/shard_map/ppermute | solution.py:343
  18.0 1.6 %prepare.1 = (f32[40,128]{1,0:T(8,128)}, f32[16,1024]{1,0:T(8,128)}) custom-call(s32[4]{0:T(128)} %refs_0_.1, s32[4,1024]{1,0:T(4,128)} %refs_1_.1, s32[4,1024]{1,0:T(4,128)} %refs_2_.1, f32[4,1024]{1,0:T(4,128)} %refs_3_.1, f32[4,1024]{1,0:T(4,128)} %refs_4_.1, f32[4,1024]{1,0:T(4,128)} %bitcast.14), custom_call_target="tpu_custom_call" | custom-call | flops 10000000 | bytes 2000000 | tf_op jit(solution)/shard_map/prepare/pallas_call | solution.py:344
  19.7 2.9 %collective-permute-start.2 = (f32[352,128]{1,0:T(8,128)S(1)}, f32[352,128]{1,0:T(8,128)S(1)}, u32[]{:S(2)}, u32[]{:S(2)}) collective-permute-start(f32[352,128]{1,0:T(8,128)S(1)} %bitcast.9), channel_id=1, source_target_pairs={{0,4},{4,0},{1,5},{5,1},{2,6},{6,2},{3,7},{7,3},{8,12},{12,8},{9,1... | collective-permute-start | bytes 540680 | tf_op jit(solution)/shard_map/ppermute | solution.py:325
  22.6 1.0 collective-permute-done.2.other_ref
  23.6 0.7 copy-done.1
  24.4 3.6 %advect.1 = (f32[160,128]{1,0:T(8,128)S(1)}, f32[704,128]{1,0:T(8,128)S(1)}) custom-call(f32[352,128]{1,0:T(8,128)S(1)} %bitcast.10, f32[352,128]{1,0:T(8,128)S(1)} %collective-permute-done.2.other_ref, f32[40,128]{1,0:T(8,128)S(1)} %copy-done.1), custom_call_target="tpu_custom_call" | custom-call | flops 10000000 | bytes 1000000 | tf_op jit(solution)/shard_map/advect/pallas_call | solution.py:365
  27.9 23.1 %all_to_all.10 = f32[64,1,1408]{2,1,0:T(1,128)S(1)} all-to-all(f32[64,1,1408]{2,1,0:T(1,128)S(1)} %bitcast.13), channel_id=1, replica_groups=mesh['gx'=64,'gy'=2,'ma'=4] {'gx'}, dimensions={0} | all-to-all | bytes 720896 | tf_op jit(solution)/shard_map/all_to_all | solution.py:379
  51.0 0.9 owner.1
  51.9 12.4 %all-to-all-start.1 = ((f32[256,1,640]{2,1,0:T(1,128)}), f32[256,1,640]{2,1,0:T(1,128)S(1)}, u32[]{:S(2)}, u32[]{:S(2)}) async-start(f32[256,1,640]{2,1,0:T(1,128)} %bitcast.4), calls=%async_computation.1 | async-start | bytes 1310720 | tf_op jit(solution)/shard_map/all_to_all | solution.py:398
  64.3 1.9 %collective-permute-start.3 = (f32[384,128]{1,0:T(8,128)S(1)}, f32[384,128]{1,0:T(8,128)S(1)}, u32[]{:S(2)}, u32[]{:S(2)}) collective-permute-start(f32[384,128]{1,0:T(8,128)S(1)} %weights.1), channel_id=1, source_target_pairs={{0,1},{1,2},{2,3},{3,0},{4,5},{5,6},{6,7},{7,4},{8,9},{9,10},{10,1... | collective-permute-start | bytes 589832 | tf_op jit(solution)/shard_map/ppermute | solution.py:333
  66.3 5.2 %collective-permute-start.4 = (f32[384,128]{1,0:T(8,128)S(1)}, f32[384,128]{1,0:T(8,128)S(1)}, u32[]{:S(2)}, u32[]{:S(2)}) collective-permute-start(f32[384,128]{1,0:T(8,128)S(1)} %weights.1), channel_id=1, source_target_pairs={{0,2},{1,3},{2,0},{3,1},{4,6},{5,7},{6,4},{7,5},{8,10},{9,11},{10,... | collective-permute-start | bytes 589832 | tf_op jit(solution)/shard_map/ppermute | solution.py:333
  71.4 2.7 %collective-permute-start.5 = (f32[384,128]{1,0:T(8,128)S(1)}, f32[384,128]{1,0:T(8,128)S(1)}, u32[]{:S(2)}, u32[]{:S(2)}) collective-permute-start(f32[384,128]{1,0:T(8,128)S(1)} %weights.1), channel_id=1, source_target_pairs={{0,3},{1,0},{2,1},{3,2},{4,7},{5,4},{6,5},{7,6},{8,11},{9,8},{10,9... | collective-permute-start | bytes 589832 | tf_op jit(solution)/shard_map/ppermute | solution.py:333
  74.1 2.6 %collective-permute-start.6 = (f32[160,128]{1,0:T(8,128)S(1)}, f32[160,128]{1,0:T(8,128)S(1)}, u32[]{:S(2)}, u32[]{:S(2)}) collective-permute-start(f32[160,128]{1,0:T(8,128)S(1)} %get-tuple-element.28.state_ref), channel_id=1, source_target_pairs={{0,1},{1,2},{2,3},{3,0},{4,5},{5,6},{6,7},{7,4},{8,9},{9,10},{10,1... | collective-permute-start | bytes 245768 | tf_op jit(solution)/shard_map/ppermute | solution.py:333
  76.7 2.4 %collective-permute-start.7 = (f32[160,128]{1,0:T(8,128)S(1)}, f32[160,128]{1,0:T(8,128)S(1)}, u32[]{:S(2)}, u32[]{:S(2)}) collective-permute-start(f32[160,128]{1,0:T(8,128)S(1)} %get-tuple-element.28.state_ref), channel_id=1, source_target_pairs={{0,2},{1,3},{2,0},{3,1},{4,6},{5,7},{6,4},{7,5},{8,10},{9,11},{10,... | collective-permute-start | bytes 245768 | tf_op jit(solution)/shard_map/ppermute | solution.py:333
  79.1 8.4 %collective-permute-done.6.gathered_1 = f32[160,128]{1,0:T(8,128)S(1)} collective-permute-done((f32[160,128]{1,0:T(8,128)S(1)}, f32[160,128]{1,0:T(8,128)S(1)}, u32[]{:S(2)}, u32[]{:S(2)}) %collective-permute-start.6) | collective-permute-done | bytes 81952 | tf_op jit(solution)/shard_map/ppermute | solution.py:333
  87.5 1.9 %collective-permute-start.8 = (f32[160,128]{1,0:T(8,128)S(1)}, f32[160,128]{1,0:T(8,128)S(1)}, u32[]{:S(2)}, u32[]{:S(2)}) collective-permute-start(f32[160,128]{1,0:T(8,128)S(1)} %get-tuple-element.28.state_ref), channel_id=1, source_target_pairs={{0,3},{1,0},{2,1},{3,2},{4,7},{5,4},{6,5},{7,6},{8,11},{9,8},{10,9... | collective-permute-start | bytes 245768 | tf_op jit(solution)/shard_map/ppermute | solution.py:333
  89.5 3.2 %collective-permute-done.8.gathered_3 = f32[160,128]{1,0:T(8,128)S(1)} collective-permute-done((f32[160,128]{1,0:T(8,128)S(1)}, f32[160,128]{1,0:T(8,128)S(1)}, u32[]{:S(2)}, u32[]{:S(2)}) %collective-permute-start.8) | collective-permute-done | bytes 81952 | tf_op jit(solution)/shard_map/ppermute | solution.py:333
  92.8 3.7 %collective-permute-start.10 = (f32[1536,128]{1,0:T(8,128)S(1)}, f32[1536,128]{1,0:T(8,128)S(1)}, u32[]{:S(2)}, u32[]{:S(2)}) collective-permute-start(f32[1536,128]{1,0:T(8,128)S(1)} %pad_maximum_fusion.own_ref), channel_id=1, source_target_pairs={{0,4},{4,0},{1,5},{5,1},{2,6},{6,2},{3,7},{7,3},{8,12},{12,8},{9,1... | collective-permute-start | bytes 2359304 | tf_op jit(solution)/shard_map/ppermute | solution.py:325
  96.5 1.9 %collective-permute-start.9 = (f32[1280,128]{1,0:T(8,128)S(1)}, f32[1280,128]{1,0:T(8,128)S(1)}, u32[]{:S(2)}, u32[]{:S(2)}) collective-permute-start(f32[1280,128]{1,0:T(8,128)S(1)} %bitcast.11), channel_id=1, source_target_pairs={{0,4},{4,0},{1,5},{5,1},{2,6},{6,2},{3,7},{7,3},{8,12},{12,8},{9,1... | collective-permute-start | bytes 1966088 | tf_op jit(solution)/shard_map/ppermute | solution.py:325
  98.8 1.6 %collective-permute-done.9.came_o_ref = f32[1280,128]{1,0:T(8,128)S(1)} collective-permute-done((f32[1280,128]{1,0:T(8,128)S(1)}, f32[1280,128]{1,0:T(8,128)S(1)}, u32[]{:S(2)}, u32[]{:S(2)}) %collective-permute-start.9) | collective-permute-done | bytes 655392 | tf_op jit(solution)/shard_map/ppermute | solution.py:325
  100.5 20.1 %filter.1 = f32[160,128]{1,0:T(8,128)} custom-call(f32[1280,128]{1,0:T(8,128)S(1)} %bitcast.12, f32[1280,128]{1,0:T(8,128)S(1)} %collective-permute-done.9.came_o_ref, bf16[9216,128]{1,0:T(8,128)(2,1)S(1)} %tapers.1, f32[16,1024]{1,0:T(8,128)S(1)} %copy-done, f32[160,128]{1,0:T(8,128)S(1)} %collective-permute-done.6.gathered_1, ...), custom_call_target="tpu_custom_call" | custom-call | flops 3000000000 | bytes 4000000 | tf_op jit(solution)/shard_map/filter/pallas_call | solution.py:416
  (16 shorter events, 0.6 us)
Async XLA Ops:
  1.6 17.9 %collective-permute-start = (f32[22,2,2,128]{3,2,1,0:T(2,128)S(1)}, f32[22,2,2,128]{3,2,1,0:T(2,128)S(1)}, u32[]{:S(2)}, u32[]{:S(2)}) collective-permute-start(f32[22,2,2,128]{3,2,1,0:T(2,128)S(1)} %get-tuple-element.40), channel_id=1, source_target_pairs={{0,8},{8,16},{16,24},{24,32},{32,40},{40,48},{48,56},{56,64},{64,7... | collective-permute-start | bytes 135176 | tf_op jit(solution)/shard_map/ppermute | solution.py:342
  6.5 13.1 %collective-permute-start.1 = (f32[22,2,2,128]{3,2,1,0:T(2,128)S(1)}, f32[22,2,2,128]{3,2,1,0:T(2,128)S(1)}, u32[]{:S(2)}, u32[]{:S(2)}) collective-permute-start(f32[22,2,2,128]{3,2,1,0:T(2,128)S(1)} %get-tuple-element.39), channel_id=1, source_target_pairs={{0,504},{8,0},{16,8},{24,16},{32,24},{40,32},{48,40},{56,48},{64,5... | collective-permute-start | bytes 135176 | tf_op jit(solution)/shard_map/ppermute | solution.py:343
  19.7 4.0 %collective-permute-start.2 = (f32[352,128]{1,0:T(8,128)S(1)}, f32[352,128]{1,0:T(8,128)S(1)}, u32[]{:S(2)}, u32[]{:S(2)}) collective-permute-start(f32[352,128]{1,0:T(8,128)S(1)} %bitcast.9), channel_id=1, source_target_pairs={{0,4},{4,0},{1,5},{5,1},{2,6},{6,2},{3,7},{7,3},{8,12},{12,8},{9,1... | collective-permute-start | bytes 540680 | tf_op jit(solution)/shard_map/ppermute | solution.py:325
  23.6 0.7 copy-start.1
  51.0 47.4 %copy-start = (f32[16,1024]{1,0:T(8,128)S(1)}, f32[16,1024]{1,0:T(8,128)}, u32[]{:S(2)}) copy-start(f32[16,1024]{1,0:T(8,128)} %get-tuple-element.35.obs_ref) | copy-start | bytes 196612
  51.9 40.9 %all-to-all-start.1 = ((f32[256,1,640]{2,1,0:T(1,128)}), f32[256,1,640]{2,1,0:T(1,128)S(1)}, u32[]{:S(2)}, u32[]{:S(2)}) async-start(f32[256,1,640]{2,1,0:T(1,128)} %bitcast.4), calls=%async_computation.1 | async-start | bytes 1310720 | tf_op jit(solution)/shard_map/all_to_all | solution.py:398
  64.3 28.4 %collective-permute-start.3 = (f32[384,128]{1,0:T(8,128)S(1)}, f32[384,128]{1,0:T(8,128)S(1)}, u32[]{:S(2)}, u32[]{:S(2)}) collective-permute-start(f32[384,128]{1,0:T(8,128)S(1)} %weights.1), channel_id=1, source_target_pairs={{0,1},{1,2},{2,3},{3,0},{4,5},{5,6},{6,7},{7,4},{8,9},{9,10},{10,1... | collective-permute-start | bytes 589832 | tf_op jit(solution)/shard_map/ppermute | solution.py:333
  66.3 26.5 %collective-permute-start.4 = (f32[384,128]{1,0:T(8,128)S(1)}, f32[384,128]{1,0:T(8,128)S(1)}, u32[]{:S(2)}, u32[]{:S(2)}) collective-permute-start(f32[384,128]{1,0:T(8,128)S(1)} %weights.1), channel_id=1, source_target_pairs={{0,2},{1,3},{2,0},{3,1},{4,6},{5,7},{6,4},{7,5},{8,10},{9,11},{10,... | collective-permute-start | bytes 589832 | tf_op jit(solution)/shard_map/ppermute | solution.py:333
  71.4 21.3 %collective-permute-start.5 = (f32[384,128]{1,0:T(8,128)S(1)}, f32[384,128]{1,0:T(8,128)S(1)}, u32[]{:S(2)}, u32[]{:S(2)}) collective-permute-start(f32[384,128]{1,0:T(8,128)S(1)} %weights.1), channel_id=1, source_target_pairs={{0,3},{1,0},{2,1},{3,2},{4,7},{5,4},{6,5},{7,6},{8,11},{9,8},{10,9... | collective-permute-start | bytes 589832 | tf_op jit(solution)/shard_map/ppermute | solution.py:333
  74.1 13.4 %collective-permute-start.6 = (f32[160,128]{1,0:T(8,128)S(1)}, f32[160,128]{1,0:T(8,128)S(1)}, u32[]{:S(2)}, u32[]{:S(2)}) collective-permute-start(f32[160,128]{1,0:T(8,128)S(1)} %get-tuple-element.28.state_ref), channel_id=1, source_target_pairs={{0,1},{1,2},{2,3},{3,0},{4,5},{5,6},{6,7},{7,4},{8,9},{9,10},{10,1... | collective-permute-start | bytes 245768 | tf_op jit(solution)/shard_map/ppermute | solution.py:333
  76.7 12.7 %collective-permute-start.7 = (f32[160,128]{1,0:T(8,128)S(1)}, f32[160,128]{1,0:T(8,128)S(1)}, u32[]{:S(2)}, u32[]{:S(2)}) collective-permute-start(f32[160,128]{1,0:T(8,128)S(1)} %get-tuple-element.28.state_ref), channel_id=1, source_target_pairs={{0,2},{1,3},{2,0},{3,1},{4,6},{5,7},{6,4},{7,5},{8,10},{9,11},{10,... | collective-permute-start | bytes 245768 | tf_op jit(solution)/shard_map/ppermute | solution.py:333
  87.5 5.2 %collective-permute-start.8 = (f32[160,128]{1,0:T(8,128)S(1)}, f32[160,128]{1,0:T(8,128)S(1)}, u32[]{:S(2)}, u32[]{:S(2)}) collective-permute-start(f32[160,128]{1,0:T(8,128)S(1)} %get-tuple-element.28.state_ref), channel_id=1, source_target_pairs={{0,3},{1,0},{2,1},{3,2},{4,7},{5,4},{6,5},{7,6},{8,11},{9,8},{10,9... | collective-permute-start | bytes 245768 | tf_op jit(solution)/shard_map/ppermute | solution.py:333
  92.8 5.6 %collective-permute-start.10 = (f32[1536,128]{1,0:T(8,128)S(1)}, f32[1536,128]{1,0:T(8,128)S(1)}, u32[]{:S(2)}, u32[]{:S(2)}) collective-permute-start(f32[1536,128]{1,0:T(8,128)S(1)} %pad_maximum_fusion.own_ref), channel_id=1, source_target_pairs={{0,4},{4,0},{1,5},{5,1},{2,6},{6,2},{3,7},{7,3},{8,12},{12,8},{9,1... | collective-permute-start | bytes 2359304 | tf_op jit(solution)/shard_map/ppermute | solution.py:325
  96.5 4.0 %collective-permute-start.9 = (f32[1280,128]{1,0:T(8,128)S(1)}, f32[1280,128]{1,0:T(8,128)S(1)}, u32[]{:S(2)}, u32[]{:S(2)}) collective-permute-start(f32[1280,128]{1,0:T(8,128)S(1)} %bitcast.11), channel_id=1, source_target_pairs={{0,4},{4,0},{1,5},{5,1},{2,6},{6,2},{3,7},{7,3},{8,12},{12,8},{9,1... | collective-permute-start | bytes 1966088 | tf_op jit(solution)/shard_map/ppermute | solution.py:325

commit v8 on v7

--- a/solution.py
+++ b/solution.py
@@ -377,7 +377,6 @@
     )(own, beside, index)
 
     parts = lax.all_to_all(picked.reshape(GX, 1, SENT * LANES), "gx", 0, 0, tiled=True)
-    gathered = over_members(state)
     parts = parts.reshape(-1, LANES)
     owned = pl.pallas_call(
         owner_kernel,
@@ -399,9 +398,9 @@
         owned.reshape(MA * GX, 1, CHUNK * LANES), ("ma", "gx"), 0, 0, tiled=True
     ).reshape(-1, LANES)
     weights = [weights] + over_members(weights)
-    weights, gathered = lax.optimization_barrier((weights, gathered))
     weights = jnp.concatenate(weights, axis=0)
-    came, weights = lax.optimization_barrier((came, weights))
+    came, weights, late = lax.optimization_barrier((came, weights, state))
+    gathered = over_members(late)
     tapers = pl.pallas_call(
         tapers_kernel,
         out_shape=jax.ShapeDtypeStruct((TAPERS + (BLOCKS - 1) * OBS, LANES), BF16),
@@ -428,7 +427,7 @@
         compiler_params=params(32),
         cost_estimate=pl.CostEstimate(flops=3_000_000_000, bytes_accessed=4_000_000, transcendentals=0),
         name="filter",
-    )(came, came_beside, tapers, observed, *gathered, state)
+    )(came, came_beside, tapers, observed, *gathered, late)
     return out.reshape(ensemble.shape)
 
 

time: 121 us -> 126 us (1.041); the launches traced: 121 us -> 124 us
  starting transfers between devices: 53.9 us -> 56.8 us
    ppermute x3, waiting for transfers between devices: 2.66 us -> 1.03 us  [other_core(): return lax.ppermute(x, 'gy', [(0, 1), (1, 0)])]
    ppermute x3, starting transfers between devices: 8.53 us -> 10 us  [other_core(): return lax.ppermute(x, 'gy', [(0, 1), (1, 0)])]
    ppermute x6, waiting for transfers between devices: 11.7 us -> 13.1 us  [over_members(): lax.ppermute(x, 'ma', [(i, (i + s) % MA) for i in range(MA)])]
    ppermute x6, starting transfers between devices: 16.7 us -> 18 us  [over_members(): lax.ppermute(x, 'ma', [(i, (i + s) % MA) for i in range(MA)])]
  transfers between devices with their start and end apart: 12 -> 12, of which waited for: 4 -> 7; matrix products, arithmetic and copies ran while one was open for 0% -> 0% of each run, Pallas kernels for 2% -> 2%
where the time goes in v8:
time: 126 us; the launch traced here: 124 us
  starting transfers between devices  56.8 us (45%)
  Pallas kernels  26.6 us (21%)
  blocking collectives  23.1 us (18%)
  waiting for transfers between devices  14.9 us (12%)
  local copies, waits for them, and re-layouts  2.36 us (2%)
    all_to_all x1, blocking collectives, local(): lax.all_to_all(picked.reshape(GX, 1, SENT * LANES), 'gx', 0, 0, tiled=True)  23.1 us
    pallas_call x1, Pallas kernels, local(): pl.pallas_call(filter_kernel, out_shape=jax.ShapeDtypeStruct((OWN * 8, LA...  20.1 us
    ppermute x6, starting transfers between devices, over_members(): lax.ppermute(x, 'ma', [(i, (i + s) % MA) for i in range(MA)])  18 us
    ppermute x6, waiting for transfers between devices, over_members(): lax.ppermute(x, 'ma', [(i, (i + s) % MA) for i in range(MA)])  13.1 us
    all_to_all x1, starting transfers between devices, local(): lax.all_to_all(owned.reshape(MA * GX, 1, CHUNK * LANES), ('ma', 'gx'), 0,...  12.4 us
    ppermute x1, starting transfers between devices, local(): high = lax.ppermute(both[:, :, :2], 'gx', backward)  11.5 us
    ppermute x3, starting transfers between devices, other_core(): return lax.ppermute(x, 'gy', [(0, 1), (1, 0)])  10 us
    ppermute x1, starting transfers between devices, local(): low = lax.ppermute(both[:, :, 2:], 'gx', forward)  4.83 us
  transfers between devices with their start and end apart: 12, of which 7 were waited for; matrix products, arithmetic and copies ran while one was open for 0% of the time, Pallas kernels for 2%

profile of v8, /device:TPU:1, one launch (start us, length us, event | category | flops | bytes accessed | tf_op | source)
XLA Modules:
  0.0 123.9 jit_solution(11004227081969273641)
XLA Ops:
  0.0 0.9 constant_dynamic-update-slice_fusion.1
  1.6 4.8 %collective-permute-start = (f32[22,2,2,128]{3,2,1,0:T(2,128)S(1)}, f32[22,2,2,128]{3,2,1,0:T(2,128)S(1)}, u32[]{:S(2)}, u32[]{:S(2)}) collective-permute-start(f32[22,2,2,128]{3,2,1,0:T(2,128)S(1)} %get-tuple-element.28), channel_id=1, source_target_pairs={{0,8},{8,16},{16,24},{24,32},{32,40},{40,48},{48,56},{56,64},{64,7... | collective-permute-start | bytes 135176 | tf_op jit(solution)/shard_map/ppermute | solution.py:342
  6.5 11.5 %collective-permute-start.1 = (f32[22,2,2,128]{3,2,1,0:T(2,128)S(1)}, f32[22,2,2,128]{3,2,1,0:T(2,128)S(1)}, u32[]{:S(2)}, u32[]{:S(2)}) collective-permute-start(f32[22,2,2,128]{3,2,1,0:T(2,128)S(1)} %get-tuple-element.27), channel_id=1, source_target_pairs={{0,504},{8,0},{16,8},{24,16},{32,24},{40,32},{48,40},{56,48},{64,5... | collective-permute-start | bytes 135176 | tf_op jit(solution)/shard_map/ppermute | solution.py:343
  18.0 1.6 %prepare.1 = (f32[40,128]{1,0:T(8,128)}, f32[16,1024]{1,0:T(8,128)}) custom-call(s32[4]{0:T(128)} %refs_0_.1, s32[4,1024]{1,0:T(4,128)} %refs_1_.1, s32[4,1024]{1,0:T(4,128)} %refs_2_.1, f32[4,1024]{1,0:T(4,128)} %refs_3_.1, f32[4,1024]{1,0:T(4,128)} %refs_4_.1, f32[4,1024]{1,0:T(4,128)} %bitcast.14), custom_call_target="tpu_custom_call" | custom-call | flops 10000000 | bytes 2000000 | tf_op jit(solution)/shard_map/prepare/pallas_call | solution.py:344
  19.7 2.9 %collective-permute-start.2 = (f32[352,128]{1,0:T(8,128)S(1)}, f32[352,128]{1,0:T(8,128)S(1)}, u32[]{:S(2)}, u32[]{:S(2)}) collective-permute-start(f32[352,128]{1,0:T(8,128)S(1)} %bitcast.9), channel_id=1, source_target_pairs={{0,4},{4,0},{1,5},{5,1},{2,6},{6,2},{3,7},{7,3},{8,12},{12,8},{9,1... | collective-permute-start | bytes 540680 | tf_op jit(solution)/shard_map/ppermute | solution.py:325
  22.6 1.0 collective-permute-done.2.other_ref
  23.6 0.7 copy-done.1
  24.4 3.6 %advect.1 = (f32[160,128]{1,0:T(8,128)S(1)}, f32[704,128]{1,0:T(8,128)S(1)}) custom-call(f32[352,128]{1,0:T(8,128)S(1)} %bitcast.10, f32[352,128]{1,0:T(8,128)S(1)} %collective-permute-done.2.other_ref, f32[40,128]{1,0:T(8,128)S(1)} %copy-done.1), custom_call_target="tpu_custom_call" | custom-call | flops 10000000 | bytes 1000000 | tf_op jit(solution)/shard_map/advect/pallas_call | solution.py:365
  27.9 23.1 %all_to_all.10 = f32[64,1,1408]{2,1,0:T(1,128)S(1)} all-to-all(f32[64,1,1408]{2,1,0:T(1,128)S(1)} %bitcast.13), channel_id=1, replica_groups=mesh['gx'=64,'gy'=2,'ma'=4] {'gx'}, dimensions={0} | all-to-all | bytes 720896 | tf_op jit(solution)/shard_map/all_to_all | solution.py:379
  51.0 0.9 owner.1
  51.9 12.4 %all-to-all-start.1 = ((f32[256,1,640]{2,1,0:T(1,128)}), f32[256,1,640]{2,1,0:T(1,128)S(1)}, u32[]{:S(2)}, u32[]{:S(2)}) async-start(f32[256,1,640]{2,1,0:T(1,128)} %bitcast.4), calls=%async_computation.1 | async-start | bytes 1310720 | tf_op jit(solution)/shard_map/all_to_all | solution.py:397
  64.3 1.9 %collective-permute-start.3 = (f32[384,128]{1,0:T(8,128)S(1)}, f32[384,128]{1,0:T(8,128)S(1)}, u32[]{:S(2)}, u32[]{:S(2)}) collective-permute-start(f32[384,128]{1,0:T(8,128)S(1)} %weights.1), channel_id=1, source_target_pairs={{0,1},{1,2},{2,3},{3,0},{4,5},{5,6},{6,7},{7,4},{8,9},{9,10},{10,1... | collective-permute-start | bytes 589832 | tf_op jit(solution)/shard_map/ppermute | solution.py:333
  66.3 5.2 %collective-permute-start.4 = (f32[384,128]{1,0:T(8,128)S(1)}, f32[384,128]{1,0:T(8,128)S(1)}, u32[]{:S(2)}, u32[]{:S(2)}) collective-permute-start(f32[384,128]{1,0:T(8,128)S(1)} %weights.1), channel_id=1, source_target_pairs={{0,2},{1,3},{2,0},{3,1},{4,6},{5,7},{6,4},{7,5},{8,10},{9,11},{10,... | collective-permute-start | bytes 589832 | tf_op jit(solution)/shard_map/ppermute | solution.py:333
  71.4 2.7 %collective-permute-start.5 = (f32[384,128]{1,0:T(8,128)S(1)}, f32[384,128]{1,0:T(8,128)S(1)}, u32[]{:S(2)}, u32[]{:S(2)}) collective-permute-start(f32[384,128]{1,0:T(8,128)S(1)} %weights.1), channel_id=1, source_target_pairs={{0,3},{1,0},{2,1},{3,2},{4,7},{5,4},{6,5},{7,6},{8,11},{9,8},{10,9... | collective-permute-start | bytes 589832 | tf_op jit(solution)/shard_map/ppermute | solution.py:333
  74.1 1.5 %collective-permute-done.3 = f32[384,128]{1,0:T(8,128)S(1)} collective-permute-done((f32[384,128]{1,0:T(8,128)S(1)}, f32[384,128]{1,0:T(8,128)S(1)}, u32[]{:S(2)}, u32[]{:S(2)}) %collective-permute-start.3) | collective-permute-done | bytes 196640 | tf_op jit(solution)/shard_map/ppermute | solution.py:333
  75.6 7.9 %collective-permute-done.4 = f32[384,128]{1,0:T(8,128)S(1)} collective-permute-done((f32[384,128]{1,0:T(8,128)S(1)}, f32[384,128]{1,0:T(8,128)S(1)}, u32[]{:S(2)}, u32[]{:S(2)}) %collective-permute-start.4) | collective-permute-done | bytes 196640 | tf_op jit(solution)/shard_map/ppermute | solution.py:333
  84.7 5.2 %collective-permute-start.7 = (f32[1536,128]{1,0:T(8,128)S(1)}, f32[1536,128]{1,0:T(8,128)S(1)}, u32[]{:S(2)}, u32[]{:S(2)}) collective-permute-start(f32[1536,128]{1,0:T(8,128)S(1)} %pad_maximum_fusion.own_ref), channel_id=1, source_target_pairs={{0,4},{4,0},{1,5},{5,1},{2,6},{6,2},{3,7},{7,3},{8,12},{12,8},{9,1... | collective-permute-start | bytes 2359304 | tf_op jit(solution)/shard_map/ppermute | solution.py:325
  89.9 1.9 %collective-permute-start.6 = (f32[1280,128]{1,0:T(8,128)S(1)}, f32[1280,128]{1,0:T(8,128)S(1)}, u32[]{:S(2)}, u32[]{:S(2)}) collective-permute-start(f32[1280,128]{1,0:T(8,128)S(1)} %bitcast.11), channel_id=1, source_target_pairs={{0,4},{4,0},{1,5},{5,1},{2,6},{6,2},{3,7},{7,3},{8,12},{12,8},{9,1... | collective-permute-start | bytes 1966088 | tf_op jit(solution)/shard_map/ppermute | solution.py:325
  91.8 3.2 %collective-permute-start.10 = (f32[160,128]{1,0:T(8,128)S(1)}, f32[160,128]{1,0:T(8,128)S(1)}, u32[]{:S(2)}, u32[]{:S(2)}) collective-permute-start(f32[160,128]{1,0:T(8,128)S(1)} %get-tuple-element.26.state_ref), channel_id=1, source_target_pairs={{0,3},{1,0},{2,1},{3,2},{4,7},{5,4},{6,5},{7,6},{8,11},{9,8},{10,9... | collective-permute-start | bytes 245768 | tf_op jit(solution)/shard_map/ppermute | solution.py:333
  95.0 2.1 %collective-permute-start.8 = (f32[160,128]{1,0:T(8,128)S(1)}, f32[160,128]{1,0:T(8,128)S(1)}, u32[]{:S(2)}, u32[]{:S(2)}) collective-permute-start(f32[160,128]{1,0:T(8,128)S(1)} %get-tuple-element.26.state_ref), channel_id=1, source_target_pairs={{0,1},{1,2},{2,3},{3,0},{4,5},{5,6},{6,7},{7,4},{8,9},{9,10},{10,1... | collective-permute-start | bytes 245768 | tf_op jit(solution)/shard_map/ppermute | solution.py:333
  97.1 3.0 %collective-permute-start.9 = (f32[160,128]{1,0:T(8,128)S(1)}, f32[160,128]{1,0:T(8,128)S(1)}, u32[]{:S(2)}, u32[]{:S(2)}) collective-permute-start(f32[160,128]{1,0:T(8,128)S(1)} %get-tuple-element.26.state_ref), channel_id=1, source_target_pairs={{0,2},{1,3},{2,0},{3,1},{4,6},{5,7},{6,4},{7,5},{8,10},{9,11},{10,... | collective-permute-start | bytes 245768 | tf_op jit(solution)/shard_map/ppermute | solution.py:333
  100.6 0.8 collective-permute-done.8.gathered_1
  101.4 2.4 %collective-permute-done.9.gathered_2 = f32[160,128]{1,0:T(8,128)S(1)} collective-permute-done((f32[160,128]{1,0:T(8,128)S(1)}, f32[160,128]{1,0:T(8,128)S(1)}, u32[]{:S(2)}, u32[]{:S(2)}) %collective-permute-start.9) | collective-permute-done | bytes 81952 | tf_op jit(solution)/shard_map/ppermute | solution.py:333
  103.8 20.1 %filter.1 = f32[160,128]{1,0:T(8,128)} custom-call(f32[1280,128]{1,0:T(8,128)S(1)} %bitcast.12, f32[1280,128]{1,0:T(8,128)S(1)} %collective-permute-done.6.came_o_ref, bf16[9216,128]{1,0:T(8,128)(2,1)S(1)} %tapers.1, f32[16,1024]{1,0:T(8,128)S(1)} %copy-done, f32[160,128]{1,0:T(8,128)S(1)} %collective-permute-done.8.gathered_1, ...), custom_call_target="tpu_custom_call" | custom-call | flops 3000000000 | bytes 4000000 | tf_op jit(solution)/shard_map/filter/pallas_call | solution.py:415
  (16 shorter events, 2.5 us)
Async XLA Ops:
  1.6 17.9 %collective-permute-start = (f32[22,2,2,128]{3,2,1,0:T(2,128)S(1)}, f32[22,2,2,128]{3,2,1,0:T(2,128)S(1)}, u32[]{:S(2)}, u32[]{:S(2)}) collective-permute-start(f32[22,2,2,128]{3,2,1,0:T(2,128)S(1)} %get-tuple-element.28), channel_id=1, source_target_pairs={{0,8},{8,16},{16,24},{24,32},{32,40},{40,48},{48,56},{56,64},{64,7... | collective-permute-start | bytes 135176 | tf_op jit(solution)/shard_map/ppermute | solution.py:342
  6.5 13.1 %collective-permute-start.1 = (f32[22,2,2,128]{3,2,1,0:T(2,128)S(1)}, f32[22,2,2,128]{3,2,1,0:T(2,128)S(1)}, u32[]{:S(2)}, u32[]{:S(2)}) collective-permute-start(f32[22,2,2,128]{3,2,1,0:T(2,128)S(1)} %get-tuple-element.27), channel_id=1, source_target_pairs={{0,504},{8,0},{16,8},{24,16},{32,24},{40,32},{48,40},{56,48},{64,5... | collective-permute-start | bytes 135176 | tf_op jit(solution)/shard_map/ppermute | solution.py:343
  19.7 4.0 %collective-permute-start.2 = (f32[352,128]{1,0:T(8,128)S(1)}, f32[352,128]{1,0:T(8,128)S(1)}, u32[]{:S(2)}, u32[]{:S(2)}) collective-permute-start(f32[352,128]{1,0:T(8,128)S(1)} %bitcast.9), channel_id=1, source_target_pairs={{0,4},{4,0},{1,5},{5,1},{2,6},{6,2},{3,7},{7,3},{8,12},{12,8},{9,1... | collective-permute-start | bytes 540680 | tf_op jit(solution)/shard_map/ppermute | solution.py:325
  23.6 0.7 copy-start.1
  51.0 49.2 %copy-start = (f32[16,1024]{1,0:T(8,128)S(1)}, f32[16,1024]{1,0:T(8,128)}, u32[]{:S(2)}) copy-start(f32[16,1024]{1,0:T(8,128)} %get-tuple-element.25.obs_ref) | copy-start | bytes 196612
  51.9 32.8 %all-to-all-start.1 = ((f32[256,1,640]{2,1,0:T(1,128)}), f32[256,1,640]{2,1,0:T(1,128)S(1)}, u32[]{:S(2)}, u32[]{:S(2)}) async-start(f32[256,1,640]{2,1,0:T(1,128)} %bitcast.4), calls=%async_computation.1 | async-start | bytes 1310720 | tf_op jit(solution)/shard_map/all_to_all | solution.py:397
  64.3 11.3 %collective-permute-start.3 = (f32[384,128]{1,0:T(8,128)S(1)}, f32[384,128]{1,0:T(8,128)S(1)}, u32[]{:S(2)}, u32[]{:S(2)}) collective-permute-start(f32[384,128]{1,0:T(8,128)S(1)} %weights.1), channel_id=1, source_target_pairs={{0,1},{1,2},{2,3},{3,0},{4,5},{5,6},{6,7},{7,4},{8,9},{9,10},{10,1... | collective-permute-start | bytes 589832 | tf_op jit(solution)/shard_map/ppermute | solution.py:333
  66.3 17.3 %collective-permute-start.4 = (f32[384,128]{1,0:T(8,128)S(1)}, f32[384,128]{1,0:T(8,128)S(1)}, u32[]{:S(2)}, u32[]{:S(2)}) collective-permute-start(f32[384,128]{1,0:T(8,128)S(1)} %weights.1), channel_id=1, source_target_pairs={{0,2},{1,3},{2,0},{3,1},{4,6},{5,7},{6,4},{7,5},{8,10},{9,11},{10,... | collective-permute-start | bytes 589832 | tf_op jit(solution)/shard_map/ppermute | solution.py:333
  71.4 12.6 %collective-permute-start.5 = (f32[384,128]{1,0:T(8,128)S(1)}, f32[384,128]{1,0:T(8,128)S(1)}, u32[]{:S(2)}, u32[]{:S(2)}) collective-permute-start(f32[384,128]{1,0:T(8,128)S(1)} %weights.1), channel_id=1, source_target_pairs={{0,3},{1,0},{2,1},{3,2},{4,7},{5,4},{6,5},{7,6},{8,11},{9,8},{10,9... | collective-permute-start | bytes 589832 | tf_op jit(solution)/shard_map/ppermute | solution.py:333
  84.7 15.4 %collective-permute-start.7 = (f32[1536,128]{1,0:T(8,128)S(1)}, f32[1536,128]{1,0:T(8,128)S(1)}, u32[]{:S(2)}, u32[]{:S(2)}) collective-permute-start(f32[1536,128]{1,0:T(8,128)S(1)} %pad_maximum_fusion.own_ref), channel_id=1, source_target_pairs={{0,4},{4,0},{1,5},{5,1},{2,6},{6,2},{3,7},{7,3},{8,12},{12,8},{9,1... | collective-permute-start | bytes 2359304 | tf_op jit(solution)/shard_map/ppermute | solution.py:325
  89.9 13.9 %collective-permute-start.6 = (f32[1280,128]{1,0:T(8,128)S(1)}, f32[1280,128]{1,0:T(8,128)S(1)}, u32[]{:S(2)}, u32[]{:S(2)}) collective-permute-start(f32[1280,128]{1,0:T(8,128)S(1)} %bitcast.11), channel_id=1, source_target_pairs={{0,4},{4,0},{1,5},{5,1},{2,6},{6,2},{3,7},{7,3},{8,12},{12,8},{9,1... | collective-permute-start | bytes 1966088 | tf_op jit(solution)/shard_map/ppermute | solution.py:325
  91.8 8.8 %collective-permute-start.10 = (f32[160,128]{1,0:T(8,128)S(1)}, f32[160,128]{1,0:T(8,128)S(1)}, u32[]{:S(2)}, u32[]{:S(2)}) collective-permute-start(f32[160,128]{1,0:T(8,128)S(1)} %get-tuple-element.26.state_ref), channel_id=1, source_target_pairs={{0,3},{1,0},{2,1},{3,2},{4,7},{5,4},{6,5},{7,6},{8,11},{9,8},{10,9... | collective-permute-start | bytes 245768 | tf_op jit(solution)/shard_map/ppermute | solution.py:333
  95.0 6.4 %collective-permute-start.8 = (f32[160,128]{1,0:T(8,128)S(1)}, f32[160,128]{1,0:T(8,128)S(1)}, u32[]{:S(2)}, u32[]{:S(2)}) collective-permute-start(f32[160,128]{1,0:T(8,128)S(1)} %get-tuple-element.26.state_ref), channel_id=1, source_target_pairs={{0,1},{1,2},{2,3},{3,0},{4,5},{5,6},{6,7},{7,4},{8,9},{9,10},{10,1... | collective-permute-start | bytes 245768 | tf_op jit(solution)/shard_map/ppermute | solution.py:333
  97.1 6.7 %collective-permute-start.9 = (f32[160,128]{1,0:T(8,128)S(1)}, f32[160,128]{1,0:T(8,128)S(1)}, u32[]{:S(2)}, u32[]{:S(2)}) collective-permute-start(f32[160,128]{1,0:T(8,128)S(1)} %get-tuple-element.26.state_ref), channel_id=1, source_target_pairs={{0,2},{1,3},{2,0},{3,1},{4,6},{5,7},{6,4},{7,5},{8,10},{9,11},{10,... | collective-permute-start | bytes 245768 | tf_op jit(solution)/shard_map/ppermute | solution.py:333

commit v9 on v7

--- a/solution.py
+++ b/solution.py
@@ -378,6 +378,7 @@
 
     parts = lax.all_to_all(picked.reshape(GX, 1, SENT * LANES), "gx", 0, 0, tiled=True)
     gathered = over_members(state)
+    parts, gathered = lax.optimization_barrier((parts, gathered))
     parts = parts.reshape(-1, LANES)
     owned = pl.pallas_call(
         owner_kernel,
@@ -398,9 +399,7 @@
     came = lax.all_to_all(
         owned.reshape(MA * GX, 1, CHUNK * LANES), ("ma", "gx"), 0, 0, tiled=True
     ).reshape(-1, LANES)
-    weights = [weights] + over_members(weights)
-    weights, gathered = lax.optimization_barrier((weights, gathered))
-    weights = jnp.concatenate(weights, axis=0)
+    weights = jnp.concatenate([weights] + over_members(weights), axis=0)
     came, weights = lax.optimization_barrier((came, weights))
     tapers = pl.pallas_call(
         tapers_kernel,

time: 121 us -> 120 us (level)
  blocking collectives: 23.1 us -> 0 us
  starting transfers between devices: 53.9 us -> 73.4 us
    all_to_all x1 -> x0, blocking collectives: 23.1 us -> none  [local(): lax.all_to_all(picked.reshape(GX, 1, SENT * LANES), 'gx', 0, 0, tiled=True)]
    all_to_all x0 -> x1, starting transfers between devices: none -> 8.8 us  [local(): lax.all_to_all(picked.reshape(GX, 1, SENT * LANES), 'gx', 0, 0, tiled=True)]
    all_to_all x1, starting transfers between devices: 12.4 us -> 16.2 us  [local(): lax.all_to_all(owned.reshape(MA * GX, 1, CHUNK * LANES), ('ma', 'gx'), 0,...]
    ppermute x6, starting transfers between devices: 16.7 us -> 20.4 us  [over_members(): lax.ppermute(x, 'ma', [(i, (i + s) % MA) for i in range(MA)])]
    ppermute x3, starting transfers between devices: 8.53 us -> 11.7 us  [other_core(): return lax.ppermute(x, 'gy', [(0, 1), (1, 0)])]
    all_to_all x0 -> x1, waiting for transfers between devices: none -> 1.33 us  [local(): lax.all_to_all(picked.reshape(GX, 1, SENT * LANES), 'gx', 0, 0, tiled=True)]
  transfers between devices with their start and end apart: 12 -> 13, of which waited for: 4 -> 6; matrix products, arithmetic and copies ran while one was open for 0% -> 0% of each run, Pallas kernels for 2% -> 2%
where the time goes in v9:
time: 120 us; the launch traced here: 119 us
  starting transfers between devices  73.4 us (61%)
  Pallas kernels  27.4 us (23%)
  waiting for transfers between devices  15.3 us (13%)
  local copies, waits for them, and re-layouts  2.36 us (2%)
    ppermute x6, starting transfers between devices, over_members(): lax.ppermute(x, 'ma', [(i, (i + s) % MA) for i in range(MA)])  20.4 us
    pallas_call x1, Pallas kernels, local(): pl.pallas_call(filter_kernel, out_shape=jax.ShapeDtypeStruct((OWN * 8, LA...  20.1 us
    all_to_all x1, starting transfers between devices, local(): lax.all_to_all(owned.reshape(MA * GX, 1, CHUNK * LANES), ('ma', 'gx'), 0,...  16.2 us
    ppermute x3, starting transfers between devices, other_core(): return lax.ppermute(x, 'gy', [(0, 1), (1, 0)])  11.7 us
    ppermute x1, starting transfers between devices, local(): high = lax.ppermute(both[:, :, :2], 'gx', backward)  11.5 us
    ppermute x6, waiting for transfers between devices, over_members(): lax.ppermute(x, 'ma', [(i, (i + s) % MA) for i in range(MA)])  11.3 us
    all_to_all x1, starting transfers between devices, local(): lax.all_to_all(picked.reshape(GX, 1, SENT * LANES), 'gx', 0, 0, tiled=True)  8.8 us
    ppermute x1, starting transfers between devices, local(): low = lax.ppermute(both[:, :, 2:], 'gx', forward)  4.83 us
  transfers between devices with their start and end apart: 13, of which 6 were waited for; matrix products, arithmetic and copies ran while one was open for 0% of the time, Pallas kernels for 2%

profile of v9, /device:TPU:1, one launch (start us, length us, event | category | flops | bytes accessed | tf_op | source)
XLA Modules:
  0.0 118.8 jit_solution(13251108124881139017)
XLA Ops:
  0.0 0.9 constant_dynamic-update-slice_fusion.1
  1.6 4.8 %collective-permute-start = (f32[22,2,2,128]{3,2,1,0:T(2,128)S(1)}, f32[22,2,2,128]{3,2,1,0:T(2,128)S(1)}, u32[]{:S(2)}, u32[]{:S(2)}) collective-permute-start(f32[22,2,2,128]{3,2,1,0:T(2,128)S(1)} %get-tuple-element.34), channel_id=1, source_target_pairs={{0,8},{8,16},{16,24},{24,32},{32,40},{40,48},{48,56},{56,64},{64,7... | collective-permute-start | bytes 135176 | tf_op jit(solution)/shard_map/ppermute | solution.py:342
  6.5 11.5 %collective-permute-start.1 = (f32[22,2,2,128]{3,2,1,0:T(2,128)S(1)}, f32[22,2,2,128]{3,2,1,0:T(2,128)S(1)}, u32[]{:S(2)}, u32[]{:S(2)}) collective-permute-start(f32[22,2,2,128]{3,2,1,0:T(2,128)S(1)} %get-tuple-element.33), channel_id=1, source_target_pairs={{0,504},{8,0},{16,8},{24,16},{32,24},{40,32},{48,40},{56,48},{64,5... | collective-permute-start | bytes 135176 | tf_op jit(solution)/shard_map/ppermute | solution.py:343
  18.0 1.6 %prepare.1 = (f32[40,128]{1,0:T(8,128)}, f32[16,1024]{1,0:T(8,128)}) custom-call(s32[4]{0:T(128)} %refs_0_.1, s32[4,1024]{1,0:T(4,128)} %refs_1_.1, s32[4,1024]{1,0:T(4,128)} %refs_2_.1, f32[4,1024]{1,0:T(4,128)} %refs_3_.1, f32[4,1024]{1,0:T(4,128)} %refs_4_.1, f32[4,1024]{1,0:T(4,128)} %bitcast.13), custom_call_target="tpu_custom_call" | custom-call | flops 10000000 | bytes 2000000 | tf_op jit(solution)/shard_map/prepare/pallas_call | solution.py:344
  19.7 2.9 %collective-permute-start.2 = (f32[352,128]{1,0:T(8,128)S(1)}, f32[352,128]{1,0:T(8,128)S(1)}, u32[]{:S(2)}, u32[]{:S(2)}) collective-permute-start(f32[352,128]{1,0:T(8,128)S(1)} %bitcast.9), channel_id=1, source_target_pairs={{0,4},{4,0},{1,5},{5,1},{2,6},{6,2},{3,7},{7,3},{8,12},{12,8},{9,1... | collective-permute-start | bytes 540680 | tf_op jit(solution)/shard_map/ppermute | solution.py:325
  22.6 1.0 collective-permute-done.2.other_ref
  24.4 4.3 %advect.1 = (f32[160,128]{1,0:T(8,128)S(1)}, f32[704,128]{1,0:T(8,128)}) custom-call(f32[352,128]{1,0:T(8,128)S(1)} %bitcast.10, f32[352,128]{1,0:T(8,128)S(1)} %collective-permute-done.2.other_ref, f32[40,128]{1,0:T(8,128)S(1)} %copy-done.1), custom_call_target="tpu_custom_call" | custom-call | flops 10000000 | bytes 1000000 | tf_op jit(solution)/shard_map/advect/pallas_call | solution.py:365
  28.7 8.8 %all-to-all-start = ((f32[64,1,1408]{2,1,0:T(1,128)}), f32[64,1,1408]{2,1,0:T(1,128)S(1)}, u32[]{:S(2)}, u32[]{:S(2)}) async-start(f32[64,1,1408]{2,1,0:T(1,128)} %bitcast.2), calls=%async_computation | async-start | bytes 720896 | tf_op jit(solution)/shard_map/all_to_all | solution.py:379
  37.5 3.3 %collective-permute-start.3 = (f32[160,128]{1,0:T(8,128)S(1)}, f32[160,128]{1,0:T(8,128)S(1)}, u32[]{:S(2)}, u32[]{:S(2)}) collective-permute-start(f32[160,128]{1,0:T(8,128)S(1)} %get-tuple-element.25.state_ref), channel_id=1, source_target_pairs={{0,1},{1,2},{2,3},{3,0},{4,5},{5,6},{6,7},{7,4},{8,9},{9,10},{10,1... | collective-permute-start | bytes 245768 | tf_op jit(solution)/shard_map/ppermute | solution.py:333
  40.8 4.4 %collective-permute-start.4 = (f32[160,128]{1,0:T(8,128)S(1)}, f32[160,128]{1,0:T(8,128)S(1)}, u32[]{:S(2)}, u32[]{:S(2)}) collective-permute-start(f32[160,128]{1,0:T(8,128)S(1)} %get-tuple-element.25.state_ref), channel_id=1, source_target_pairs={{0,2},{1,3},{2,0},{3,1},{4,6},{5,7},{6,4},{7,5},{8,10},{9,11},{10,... | collective-permute-start | bytes 245768 | tf_op jit(solution)/shard_map/ppermute | solution.py:333
  45.1 3.1 %collective-permute-start.5 = (f32[160,128]{1,0:T(8,128)S(1)}, f32[160,128]{1,0:T(8,128)S(1)}, u32[]{:S(2)}, u32[]{:S(2)}) collective-permute-start(f32[160,128]{1,0:T(8,128)S(1)} %get-tuple-element.25.state_ref), channel_id=1, source_target_pairs={{0,3},{1,0},{2,1},{3,2},{4,7},{5,4},{6,5},{7,6},{8,11},{9,8},{10,9... | collective-permute-start | bytes 245768 | tf_op jit(solution)/shard_map/ppermute | solution.py:333
  48.2 2.4 %collective-permute-done.5.gathered_3 = f32[160,128]{1,0:T(8,128)S(1)} collective-permute-done((f32[160,128]{1,0:T(8,128)S(1)}, f32[160,128]{1,0:T(8,128)S(1)}, u32[]{:S(2)}, u32[]{:S(2)}) %collective-permute-start.5) | collective-permute-done | bytes 81952 | tf_op jit(solution)/shard_map/ppermute | solution.py:333
  50.6 1.3 %all-to-all-done = f32[64,1,1408]{2,1,0:T(1,128)S(1)} async-done(((f32[64,1,1408]{2,1,0:T(1,128)}), f32[64,1,1408]{2,1,0:T(1,128)S(1)}, u32[]{:S(2)}, u32[]{:S(2)}) %all-to-all-start) | async-done | bytes 360480 | tf_op jit(solution)/shard_map/all_to_all | solution.py:379
  52.0 0.9 owner.1
  52.9 16.2 %all-to-all-start.1 = ((f32[256,1,640]{2,1,0:T(1,128)}), f32[256,1,640]{2,1,0:T(1,128)S(1)}, u32[]{:S(2)}, u32[]{:S(2)}) async-start(f32[256,1,640]{2,1,0:T(1,128)} %bitcast.4), calls=%async_computation.1 | async-start | bytes 1310720 | tf_op jit(solution)/shard_map/all_to_all | solution.py:399
  69.1 1.9 %collective-permute-start.6 = (f32[384,128]{1,0:T(8,128)S(1)}, f32[384,128]{1,0:T(8,128)S(1)}, u32[]{:S(2)}, u32[]{:S(2)}) collective-permute-start(f32[384,128]{1,0:T(8,128)S(1)} %weights.1), channel_id=1, source_target_pairs={{0,1},{1,2},{2,3},{3,0},{4,5},{5,6},{6,7},{7,4},{8,9},{9,10},{10,1... | collective-permute-start | bytes 589832 | tf_op jit(solution)/shard_map/ppermute | solution.py:333
  71.0 5.2 %collective-permute-start.7 = (f32[384,128]{1,0:T(8,128)S(1)}, f32[384,128]{1,0:T(8,128)S(1)}, u32[]{:S(2)}, u32[]{:S(2)}) collective-permute-start(f32[384,128]{1,0:T(8,128)S(1)} %weights.1), channel_id=1, source_target_pairs={{0,2},{1,3},{2,0},{3,1},{4,6},{5,7},{6,4},{7,5},{8,10},{9,11},{10,... | collective-permute-start | bytes 589832 | tf_op jit(solution)/shard_map/ppermute | solution.py:333
  76.2 2.7 %collective-permute-start.8 = (f32[384,128]{1,0:T(8,128)S(1)}, f32[384,128]{1,0:T(8,128)S(1)}, u32[]{:S(2)}, u32[]{:S(2)}) collective-permute-start(f32[384,128]{1,0:T(8,128)S(1)} %weights.1), channel_id=1, source_target_pairs={{0,3},{1,0},{2,1},{3,2},{4,7},{5,4},{6,5},{7,6},{8,11},{9,8},{10,9... | collective-permute-start | bytes 589832 | tf_op jit(solution)/shard_map/ppermute | solution.py:333
  78.9 8.1 %collective-permute-done.7 = f32[384,128]{1,0:T(8,128)S(1)} collective-permute-done((f32[384,128]{1,0:T(8,128)S(1)}, f32[384,128]{1,0:T(8,128)S(1)}, u32[]{:S(2)}, u32[]{:S(2)}) %collective-permute-start.7) | collective-permute-done | bytes 196640 | tf_op jit(solution)/shard_map/ppermute | solution.py:333
  87.0 0.8 collective-permute-done.8
  87.9 6.8 %collective-permute-start.10 = (f32[1536,128]{1,0:T(8,128)S(1)}, f32[1536,128]{1,0:T(8,128)S(1)}, u32[]{:S(2)}, u32[]{:S(2)}) collective-permute-start(f32[1536,128]{1,0:T(8,128)S(1)} %pad_maximum_fusion.own_ref), channel_id=1, source_target_pairs={{0,4},{4,0},{1,5},{5,1},{2,6},{6,2},{3,7},{7,3},{8,12},{12,8},{9,1... | collective-permute-start | bytes 2359304 | tf_op jit(solution)/shard_map/ppermute | solution.py:325
  94.7 1.9 %collective-permute-start.9 = (f32[1280,128]{1,0:T(8,128)S(1)}, f32[1280,128]{1,0:T(8,128)S(1)}, u32[]{:S(2)}, u32[]{:S(2)}) collective-permute-start(f32[1280,128]{1,0:T(8,128)S(1)} %bitcast.11), channel_id=1, source_target_pairs={{0,4},{4,0},{1,5},{5,1},{2,6},{6,2},{3,7},{7,3},{8,12},{12,8},{9,1... | collective-permute-start | bytes 1966088 | tf_op jit(solution)/shard_map/ppermute | solution.py:325
  97.0 1.6 %collective-permute-done.9.came_o_ref = f32[1280,128]{1,0:T(8,128)S(1)} collective-permute-done((f32[1280,128]{1,0:T(8,128)S(1)}, f32[1280,128]{1,0:T(8,128)S(1)}, u32[]{:S(2)}, u32[]{:S(2)}) %collective-permute-start.9) | collective-permute-done | bytes 655392 | tf_op jit(solution)/shard_map/ppermute | solution.py:325
  98.7 20.1 %filter.1 = f32[160,128]{1,0:T(8,128)} custom-call(f32[1280,128]{1,0:T(8,128)S(1)} %bitcast.12, f32[1280,128]{1,0:T(8,128)S(1)} %collective-permute-done.9.came_o_ref, bf16[9216,128]{1,0:T(8,128)(2,1)S(1)} %tapers.1, f32[16,1024]{1,0:T(8,128)S(1)} %copy-done, f32[160,128]{1,0:T(8,128)S(1)} %collective-permute-done.3.gathered_1, ...), custom_call_target="tpu_custom_call" | custom-call | flops 3000000000 | bytes 4000000 | tf_op jit(solution)/shard_map/filter/pallas_call | solution.py:415
  (17 shorter events, 2.0 us)
Async XLA Ops:
  1.6 17.9 %collective-permute-start = (f32[22,2,2,128]{3,2,1,0:T(2,128)S(1)}, f32[22,2,2,128]{3,2,1,0:T(2,128)S(1)}, u32[]{:S(2)}, u32[]{:S(2)}) collective-permute-start(f32[22,2,2,128]{3,2,1,0:T(2,128)S(1)} %get-tuple-element.34), channel_id=1, source_target_pairs={{0,8},{8,16},{16,24},{24,32},{32,40},{40,48},{48,56},{56,64},{64,7... | collective-permute-start | bytes 135176 | tf_op jit(solution)/shard_map/ppermute | solution.py:342
  6.5 13.1 %collective-permute-start.1 = (f32[22,2,2,128]{3,2,1,0:T(2,128)S(1)}, f32[22,2,2,128]{3,2,1,0:T(2,128)S(1)}, u32[]{:S(2)}, u32[]{:S(2)}) collective-permute-start(f32[22,2,2,128]{3,2,1,0:T(2,128)S(1)} %get-tuple-element.33), channel_id=1, source_target_pairs={{0,504},{8,0},{16,8},{24,16},{32,24},{40,32},{48,40},{56,48},{64,5... | collective-permute-start | bytes 135176 | tf_op jit(solution)/shard_map/ppermute | solution.py:343
  19.7 4.0 %collective-permute-start.2 = (f32[352,128]{1,0:T(8,128)S(1)}, f32[352,128]{1,0:T(8,128)S(1)}, u32[]{:S(2)}, u32[]{:S(2)}) collective-permute-start(f32[352,128]{1,0:T(8,128)S(1)} %bitcast.9), channel_id=1, source_target_pairs={{0,4},{4,0},{1,5},{5,1},{2,6},{6,2},{3,7},{7,3},{8,12},{12,8},{9,1... | collective-permute-start | bytes 540680 | tf_op jit(solution)/shard_map/ppermute | solution.py:325
  23.6 0.7 copy-start.1
  28.7 23.3 %all-to-all-start = ((f32[64,1,1408]{2,1,0:T(1,128)}), f32[64,1,1408]{2,1,0:T(1,128)S(1)}, u32[]{:S(2)}, u32[]{:S(2)}) async-start(f32[64,1,1408]{2,1,0:T(1,128)} %bitcast.2), calls=%async_computation | async-start | bytes 720896 | tf_op jit(solution)/shard_map/all_to_all | solution.py:379
  37.5 59.1 %copy-start = (f32[16,1024]{1,0:T(8,128)S(1)}, f32[16,1024]{1,0:T(8,128)}, u32[]{:S(2)}) copy-start(f32[16,1024]{1,0:T(8,128)} %get-tuple-element.29.obs_ref) | copy-start | bytes 196612
  37.5 10.7 %collective-permute-start.3 = (f32[160,128]{1,0:T(8,128)S(1)}, f32[160,128]{1,0:T(8,128)S(1)}, u32[]{:S(2)}, u32[]{:S(2)}) collective-permute-start(f32[160,128]{1,0:T(8,128)S(1)} %get-tuple-element.25.state_ref), channel_id=1, source_target_pairs={{0,1},{1,2},{2,3},{3,0},{4,5},{5,6},{6,7},{7,4},{8,9},{9,10},{10,1... | collective-permute-start | bytes 245768 | tf_op jit(solution)/shard_map/ppermute | solution.py:333
  40.8 7.4 %collective-permute-start.4 = (f32[160,128]{1,0:T(8,128)S(1)}, f32[160,128]{1,0:T(8,128)S(1)}, u32[]{:S(2)}, u32[]{:S(2)}) collective-permute-start(f32[160,128]{1,0:T(8,128)S(1)} %get-tuple-element.25.state_ref), channel_id=1, source_target_pairs={{0,2},{1,3},{2,0},{3,1},{4,6},{5,7},{6,4},{7,5},{8,10},{9,11},{10,... | collective-permute-start | bytes 245768 | tf_op jit(solution)/shard_map/ppermute | solution.py:333
  45.1 5.5 %collective-permute-start.5 = (f32[160,128]{1,0:T(8,128)S(1)}, f32[160,128]{1,0:T(8,128)S(1)}, u32[]{:S(2)}, u32[]{:S(2)}) collective-permute-start(f32[160,128]{1,0:T(8,128)S(1)} %get-tuple-element.25.state_ref), channel_id=1, source_target_pairs={{0,3},{1,0},{2,1},{3,2},{4,7},{5,4},{6,5},{7,6},{8,11},{9,8},{10,9... | collective-permute-start | bytes 245768 | tf_op jit(solution)/shard_map/ppermute | solution.py:333
  52.9 35.0 %all-to-all-start.1 = ((f32[256,1,640]{2,1,0:T(1,128)}), f32[256,1,640]{2,1,0:T(1,128)S(1)}, u32[]{:S(2)}, u32[]{:S(2)}) async-start(f32[256,1,640]{2,1,0:T(1,128)} %bitcast.4), calls=%async_computation.1 | async-start | bytes 1310720 | tf_op jit(solution)/shard_map/all_to_all | solution.py:399
  69.1 9.8 %collective-permute-start.6 = (f32[384,128]{1,0:T(8,128)S(1)}, f32[384,128]{1,0:T(8,128)S(1)}, u32[]{:S(2)}, u32[]{:S(2)}) collective-permute-start(f32[384,128]{1,0:T(8,128)S(1)} %weights.1), channel_id=1, source_target_pairs={{0,1},{1,2},{2,3},{3,0},{4,5},{5,6},{6,7},{7,4},{8,9},{9,10},{10,1... | collective-permute-start | bytes 589832 | tf_op jit(solution)/shard_map/ppermute | solution.py:333
  71.0 16.0 %collective-permute-start.7 = (f32[384,128]{1,0:T(8,128)S(1)}, f32[384,128]{1,0:T(8,128)S(1)}, u32[]{:S(2)}, u32[]{:S(2)}) collective-permute-start(f32[384,128]{1,0:T(8,128)S(1)} %weights.1), channel_id=1, source_target_pairs={{0,2},{1,3},{2,0},{3,1},{4,6},{5,7},{6,4},{7,5},{8,10},{9,11},{10,... | collective-permute-start | bytes 589832 | tf_op jit(solution)/shard_map/ppermute | solution.py:333
  76.2 11.6 %collective-permute-start.8 = (f32[384,128]{1,0:T(8,128)S(1)}, f32[384,128]{1,0:T(8,128)S(1)}, u32[]{:S(2)}, u32[]{:S(2)}) collective-permute-start(f32[384,128]{1,0:T(8,128)S(1)} %weights.1), channel_id=1, source_target_pairs={{0,3},{1,0},{2,1},{3,2},{4,7},{5,4},{6,5},{7,6},{8,11},{9,8},{10,9... | collective-permute-start | bytes 589832 | tf_op jit(solution)/shard_map/ppermute | solution.py:333
  87.9 8.8 %collective-permute-start.10 = (f32[1536,128]{1,0:T(8,128)S(1)}, f32[1536,128]{1,0:T(8,128)S(1)}, u32[]{:S(2)}, u32[]{:S(2)}) collective-permute-start(f32[1536,128]{1,0:T(8,128)S(1)} %pad_maximum_fusion.own_ref), channel_id=1, source_target_pairs={{0,4},{4,0},{1,5},{5,1},{2,6},{6,2},{3,7},{7,3},{8,12},{12,8},{9,1... | collective-permute-start | bytes 2359304 | tf_op jit(solution)/shard_map/ppermute | solution.py:325
  94.7 4.0 %collective-permute-start.9 = (f32[1280,128]{1,0:T(8,128)S(1)}, f32[1280,128]{1,0:T(8,128)S(1)}, u32[]{:S(2)}, u32[]{:S(2)}) collective-permute-start(f32[1280,128]{1,0:T(8,128)S(1)} %bitcast.11), channel_id=1, source_target_pairs={{0,4},{4,0},{1,5},{5,1},{2,6},{6,2},{3,7},{7,3},{8,12},{12,8},{9,1... | collective-permute-start | bytes 1966088 | tf_op jit(solution)/shard_map/ppermute | solution.py:325

commit v10 on v9

--- a/solution.py
+++ b/solution.py
@@ -224,7 +224,6 @@
 
     lane = lax.broadcasted_iota(jnp.int32, (ROWS_O, LANES), 1)
     member_row = lax.broadcasted_iota(jnp.int32, (LANES, OBS), 0)
-    increments[...] = jnp.zeros((LANES, LANES), F32)
     for k in range(BLOCKS):
         if k == 0:
             now = first_block[...]
@@ -249,10 +248,12 @@
             + dot_nt(gain_low, tapered_high)
             + dot_nt(gain_high, tapered_low)
         )
-        e = increments[...]
-        increments[...] = e + mixing + jnp.dot(
-            mixing, e, precision=lax.Precision.HIGHEST, preferred_element_type=F32
-        )
+        if k > 0:
+            e = increments[...]
+            e_high, e_low = split(e)
+            m_high, m_low = split(mixing)
+            mixing = mixing + e + dot_nn(m_high, e_high) + dot_nn(m_low, e_high) + dot_nn(m_high, e_low)
+        increments[...] = mixing
 
         if k == BLOCKS - 1:
             continue
@@ -294,7 +295,7 @@
     fifth = sum(jnp.where(row >= i * CHUNK, 1, 0) for i in range(1, MA))
     member = (row - fifth * CHUNK) * 16 + q * MA + fifth
     chosen = jnp.where((col == member) & (row < OWN), 1.0, 0.0)
-    transform = jnp.dot(chosen, total, precision=lax.Precision.HIGHEST, preferred_element_type=F32)
+    chosen = chosen.astype(BF16)
     row = lax.broadcasted_iota(jnp.int32, (LANES, LANES), 0)
     col = lax.broadcasted_iota(jnp.int32, (LANES, LANES), 1)
     back = sum(jnp.where(col >= i * OWN, 1, 0) for i in range(1, MA))
@@ -302,7 +303,10 @@
     fifth = sum(jnp.where(place >= i * CHUNK, 1, 0) for i in range(1, MA))
     member = (place - fifth * CHUNK) * 16 + jnp.bitwise_and(q - back, MA - 1) * MA + fifth
     shuffle = jnp.where((row == member) & (col < MEMBERS), 1.0, 0.0)
-    transform = jnp.dot(transform, shuffle, precision=lax.Precision.HIGHEST, preferred_element_type=F32)
+    shuffle = shuffle.astype(BF16)
+    t_high, t_low = [
+        dot_nn(dot_nn(chosen, piece).astype(BF16), shuffle).astype(BF16) for piece in split(total)
+    ]
     tiles = []
     for c in range(8):
         at = pl.ds(c, OWN, stride=8)
@@ -314,7 +318,6 @@
         [jnp.concatenate(tiles, axis=1), jnp.zeros((LANES - MEMBERS, CELLS), F32)], axis=0
     )
     c_high, c_low = split(centered)
-    t_high, t_low = split(transform)
     update = dot_nn(t_high, c_high) + dot_nn(t_low, c_high) + dot_nn(t_high, c_low)
     for c in range(8):
         at = pl.ds(c, OWN, stride=8)

time: 120 us -> 119 us (level)
  no operation moved by 1% of the time
where the time goes in v10:
time: 119 us; the launch traced here: 118 us
  starting transfers between devices  73.4 us (62%)
  Pallas kernels  26.9 us (23%)
  waiting for transfers between devices  15.3 us (13%)
  local copies, waits for them, and re-layouts  2.36 us (2%)
    ppermute x6, starting transfers between devices, over_members(): lax.ppermute(x, 'ma', [(i, (i + s) % MA) for i in range(MA)])  20.4 us
    pallas_call x1, Pallas kernels, local(): pl.pallas_call(filter_kernel, out_shape=jax.ShapeDtypeStruct((OWN * 8, LA...  19.7 us
    all_to_all x1, starting transfers between devices, local(): lax.all_to_all(owned.reshape(MA * GX, 1, CHUNK * LANES), ('ma', 'gx'), 0,...  16.2 us
    ppermute x3, starting transfers between devices, other_core(): return lax.ppermute(x, 'gy', [(0, 1), (1, 0)])  11.7 us
    ppermute x1, starting transfers between devices, local(): high = lax.ppermute(both[:, :, :2], 'gx', backward)  11.5 us
    ppermute x6, waiting for transfers between devices, over_members(): lax.ppermute(x, 'ma', [(i, (i + s) % MA) for i in range(MA)])  11.3 us
    all_to_all x1, starting transfers between devices, local(): lax.all_to_all(picked.reshape(GX, 1, SENT * LANES), 'gx', 0, 0, tiled=True)  8.8 us
    ppermute x1, starting transfers between devices, local(): low = lax.ppermute(both[:, :, 2:], 'gx', forward)  4.83 us
  transfers between devices with their start and end apart: 13, of which 6 were waited for; matrix products, arithmetic and copies ran while one was open for 0% of the time, Pallas kernels for 2%

profile of v10, /device:TPU:1, one launch (start us, length us, event | category | flops | bytes accessed | tf_op | source)
XLA Modules:
  0.0 118.3 jit_solution(2857288289021177357)
XLA Ops:
  0.0 0.9 constant_dynamic-update-slice_fusion.1
  1.6 4.8 %collective-permute-start = (f32[22,2,2,128]{3,2,1,0:T(2,128)S(1)}, f32[22,2,2,128]{3,2,1,0:T(2,128)S(1)}, u32[]{:S(2)}, u32[]{:S(2)}) collective-permute-start(f32[22,2,2,128]{3,2,1,0:T(2,128)S(1)} %get-tuple-element.34), channel_id=1, source_target_pairs={{0,8},{8,16},{16,24},{24,32},{32,40},{40,48},{48,56},{56,64},{64,7... | collective-permute-start | bytes 135176 | tf_op jit(solution)/shard_map/ppermute | solution.py:345
  6.5 11.5 %collective-permute-start.1 = (f32[22,2,2,128]{3,2,1,0:T(2,128)S(1)}, f32[22,2,2,128]{3,2,1,0:T(2,128)S(1)}, u32[]{:S(2)}, u32[]{:S(2)}) collective-permute-start(f32[22,2,2,128]{3,2,1,0:T(2,128)S(1)} %get-tuple-element.33), channel_id=1, source_target_pairs={{0,504},{8,0},{16,8},{24,16},{32,24},{40,32},{48,40},{56,48},{64,5... | collective-permute-start | bytes 135176 | tf_op jit(solution)/shard_map/ppermute | solution.py:346
  18.0 1.6 %prepare.1 = (f32[40,128]{1,0:T(8,128)}, f32[16,1024]{1,0:T(8,128)}) custom-call(s32[4]{0:T(128)} %refs_0_.1, s32[4,1024]{1,0:T(4,128)} %refs_1_.1, s32[4,1024]{1,0:T(4,128)} %refs_2_.1, f32[4,1024]{1,0:T(4,128)} %refs_3_.1, f32[4,1024]{1,0:T(4,128)} %refs_4_.1, f32[4,1024]{1,0:T(4,128)} %bitcast.13), custom_call_target="tpu_custom_call" | custom-call | flops 10000000 | bytes 2000000 | tf_op jit(solution)/shard_map/prepare/pallas_call | solution.py:347
  19.7 2.9 %collective-permute-start.2 = (f32[352,128]{1,0:T(8,128)S(1)}, f32[352,128]{1,0:T(8,128)S(1)}, u32[]{:S(2)}, u32[]{:S(2)}) collective-permute-start(f32[352,128]{1,0:T(8,128)S(1)} %bitcast.9), channel_id=1, source_target_pairs={{0,4},{4,0},{1,5},{5,1},{2,6},{6,2},{3,7},{7,3},{8,12},{12,8},{9,1... | collective-permute-start | bytes 540680 | tf_op jit(solution)/shard_map/ppermute | solution.py:328
  22.6 1.0 collective-permute-done.2.other_ref
  24.4 4.3 %advect.1 = (f32[160,128]{1,0:T(8,128)S(1)}, f32[704,128]{1,0:T(8,128)}) custom-call(f32[352,128]{1,0:T(8,128)S(1)} %bitcast.10, f32[352,128]{1,0:T(8,128)S(1)} %collective-permute-done.2.other_ref, f32[40,128]{1,0:T(8,128)S(1)} %copy-done.1), custom_call_target="tpu_custom_call" | custom-call | flops 10000000 | bytes 1000000 | tf_op jit(solution)/shard_map/advect/pallas_call | solution.py:368
  28.7 8.8 %all-to-all-start = ((f32[64,1,1408]{2,1,0:T(1,128)}), f32[64,1,1408]{2,1,0:T(1,128)S(1)}, u32[]{:S(2)}, u32[]{:S(2)}) async-start(f32[64,1,1408]{2,1,0:T(1,128)} %bitcast.2), calls=%async_computation | async-start | bytes 720896 | tf_op jit(solution)/shard_map/all_to_all | solution.py:382
  37.5 3.3 %collective-permute-start.3 = (f32[160,128]{1,0:T(8,128)S(1)}, f32[160,128]{1,0:T(8,128)S(1)}, u32[]{:S(2)}, u32[]{:S(2)}) collective-permute-start(f32[160,128]{1,0:T(8,128)S(1)} %get-tuple-element.25.state_ref), channel_id=1, source_target_pairs={{0,1},{1,2},{2,3},{3,0},{4,5},{5,6},{6,7},{7,4},{8,9},{9,10},{10,1... | collective-permute-start | bytes 245768 | tf_op jit(solution)/shard_map/ppermute | solution.py:336
  40.8 4.4 %collective-permute-start.4 = (f32[160,128]{1,0:T(8,128)S(1)}, f32[160,128]{1,0:T(8,128)S(1)}, u32[]{:S(2)}, u32[]{:S(2)}) collective-permute-start(f32[160,128]{1,0:T(8,128)S(1)} %get-tuple-element.25.state_ref), channel_id=1, source_target_pairs={{0,2},{1,3},{2,0},{3,1},{4,6},{5,7},{6,4},{7,5},{8,10},{9,11},{10,... | collective-permute-start | bytes 245768 | tf_op jit(solution)/shard_map/ppermute | solution.py:336
  45.1 3.1 %collective-permute-start.5 = (f32[160,128]{1,0:T(8,128)S(1)}, f32[160,128]{1,0:T(8,128)S(1)}, u32[]{:S(2)}, u32[]{:S(2)}) collective-permute-start(f32[160,128]{1,0:T(8,128)S(1)} %get-tuple-element.25.state_ref), channel_id=1, source_target_pairs={{0,3},{1,0},{2,1},{3,2},{4,7},{5,4},{6,5},{7,6},{8,11},{9,8},{10,9... | collective-permute-start | bytes 245768 | tf_op jit(solution)/shard_map/ppermute | solution.py:336
  48.2 2.4 %collective-permute-done.5.gathered_3 = f32[160,128]{1,0:T(8,128)S(1)} collective-permute-done((f32[160,128]{1,0:T(8,128)S(1)}, f32[160,128]{1,0:T(8,128)S(1)}, u32[]{:S(2)}, u32[]{:S(2)}) %collective-permute-start.5) | collective-permute-done | bytes 81952 | tf_op jit(solution)/shard_map/ppermute | solution.py:336
  50.6 1.3 %all-to-all-done = f32[64,1,1408]{2,1,0:T(1,128)S(1)} async-done(((f32[64,1,1408]{2,1,0:T(1,128)}), f32[64,1,1408]{2,1,0:T(1,128)S(1)}, u32[]{:S(2)}, u32[]{:S(2)}) %all-to-all-start) | async-done | bytes 360480 | tf_op jit(solution)/shard_map/all_to_all | solution.py:382
  52.0 0.9 owner.1
  52.9 16.2 %all-to-all-start.1 = ((f32[256,1,640]{2,1,0:T(1,128)}), f32[256,1,640]{2,1,0:T(1,128)S(1)}, u32[]{:S(2)}, u32[]{:S(2)}) async-start(f32[256,1,640]{2,1,0:T(1,128)} %bitcast.4), calls=%async_computation.1 | async-start | bytes 1310720 | tf_op jit(solution)/shard_map/all_to_all | solution.py:402
  69.1 1.9 %collective-permute-start.6 = (f32[384,128]{1,0:T(8,128)S(1)}, f32[384,128]{1,0:T(8,128)S(1)}, u32[]{:S(2)}, u32[]{:S(2)}) collective-permute-start(f32[384,128]{1,0:T(8,128)S(1)} %weights.1), channel_id=1, source_target_pairs={{0,1},{1,2},{2,3},{3,0},{4,5},{5,6},{6,7},{7,4},{8,9},{9,10},{10,1... | collective-permute-start | bytes 589832 | tf_op jit(solution)/shard_map/ppermute | solution.py:336
  71.0 5.2 %collective-permute-start.7 = (f32[384,128]{1,0:T(8,128)S(1)}, f32[384,128]{1,0:T(8,128)S(1)}, u32[]{:S(2)}, u32[]{:S(2)}) collective-permute-start(f32[384,128]{1,0:T(8,128)S(1)} %weights.1), channel_id=1, source_target_pairs={{0,2},{1,3},{2,0},{3,1},{4,6},{5,7},{6,4},{7,5},{8,10},{9,11},{10,... | collective-permute-start | bytes 589832 | tf_op jit(solution)/shard_map/ppermute | solution.py:336
  76.2 2.7 %collective-permute-start.8 = (f32[384,128]{1,0:T(8,128)S(1)}, f32[384,128]{1,0:T(8,128)S(1)}, u32[]{:S(2)}, u32[]{:S(2)}) collective-permute-start(f32[384,128]{1,0:T(8,128)S(1)} %weights.1), channel_id=1, source_target_pairs={{0,3},{1,0},{2,1},{3,2},{4,7},{5,4},{6,5},{7,6},{8,11},{9,8},{10,9... | collective-permute-start | bytes 589832 | tf_op jit(solution)/shard_map/ppermute | solution.py:336
  78.9 8.1 %collective-permute-done.7 = f32[384,128]{1,0:T(8,128)S(1)} collective-permute-done((f32[384,128]{1,0:T(8,128)S(1)}, f32[384,128]{1,0:T(8,128)S(1)}, u32[]{:S(2)}, u32[]{:S(2)}) %collective-permute-start.7) | collective-permute-done | bytes 196640 | tf_op jit(solution)/shard_map/ppermute | solution.py:336
  87.0 0.8 collective-permute-done.8
  87.9 6.8 %collective-permute-start.10 = (f32[1536,128]{1,0:T(8,128)S(1)}, f32[1536,128]{1,0:T(8,128)S(1)}, u32[]{:S(2)}, u32[]{:S(2)}) collective-permute-start(f32[1536,128]{1,0:T(8,128)S(1)} %pad_maximum_fusion.own_ref), channel_id=1, source_target_pairs={{0,4},{4,0},{1,5},{5,1},{2,6},{6,2},{3,7},{7,3},{8,12},{12,8},{9,1... | collective-permute-start | bytes 2359304 | tf_op jit(solution)/shard_map/ppermute | solution.py:328
  94.7 1.9 %collective-permute-start.9 = (f32[1280,128]{1,0:T(8,128)S(1)}, f32[1280,128]{1,0:T(8,128)S(1)}, u32[]{:S(2)}, u32[]{:S(2)}) collective-permute-start(f32[1280,128]{1,0:T(8,128)S(1)} %bitcast.11), channel_id=1, source_target_pairs={{0,4},{4,0},{1,5},{5,1},{2,6},{6,2},{3,7},{7,3},{8,12},{12,8},{9,1... | collective-permute-start | bytes 1966088 | tf_op jit(solution)/shard_map/ppermute | solution.py:328
  97.0 1.6 %collective-permute-done.9.came_o_ref = f32[1280,128]{1,0:T(8,128)S(1)} collective-permute-done((f32[1280,128]{1,0:T(8,128)S(1)}, f32[1280,128]{1,0:T(8,128)S(1)}, u32[]{:S(2)}, u32[]{:S(2)}) %collective-permute-start.9) | collective-permute-done | bytes 655392 | tf_op jit(solution)/shard_map/ppermute | solution.py:328
  98.7 19.7 %filter.1 = f32[160,128]{1,0:T(8,128)} custom-call(f32[1280,128]{1,0:T(8,128)S(1)} %bitcast.12, f32[1280,128]{1,0:T(8,128)S(1)} %collective-permute-done.9.came_o_ref, bf16[9216,128]{1,0:T(8,128)(2,1)S(1)} %tapers.1, f32[16,1024]{1,0:T(8,128)S(1)} %copy-done, f32[160,128]{1,0:T(8,128)S(1)} %collective-permute-done.3.gathered_1, ...), custom_call_target="tpu_custom_call" | custom-call | flops 3000000000 | bytes 4000000 | tf_op jit(solution)/shard_map/filter/pallas_call | solution.py:418
  (17 shorter events, 2.0 us)
Async XLA Ops:
  1.6 17.9 %collective-permute-start = (f32[22,2,2,128]{3,2,1,0:T(2,128)S(1)}, f32[22,2,2,128]{3,2,1,0:T(2,128)S(1)}, u32[]{:S(2)}, u32[]{:S(2)}) collective-permute-start(f32[22,2,2,128]{3,2,1,0:T(2,128)S(1)} %get-tuple-element.34), channel_id=1, source_target_pairs={{0,8},{8,16},{16,24},{24,32},{32,40},{40,48},{48,56},{56,64},{64,7... | collective-permute-start | bytes 135176 | tf_op jit(solution)/shard_map/ppermute | solution.py:345
  6.5 13.1 %collective-permute-start.1 = (f32[22,2,2,128]{3,2,1,0:T(2,128)S(1)}, f32[22,2,2,128]{3,2,1,0:T(2,128)S(1)}, u32[]{:S(2)}, u32[]{:S(2)}) collective-permute-start(f32[22,2,2,128]{3,2,1,0:T(2,128)S(1)} %get-tuple-element.33), channel_id=1, source_target_pairs={{0,504},{8,0},{16,8},{24,16},{32,24},{40,32},{48,40},{56,48},{64,5... | collective-permute-start | bytes 135176 | tf_op jit(solution)/shard_map/ppermute | solution.py:346
  19.7 4.0 %collective-permute-start.2 = (f32[352,128]{1,0:T(8,128)S(1)}, f32[352,128]{1,0:T(8,128)S(1)}, u32[]{:S(2)}, u32[]{:S(2)}) collective-permute-start(f32[352,128]{1,0:T(8,128)S(1)} %bitcast.9), channel_id=1, source_target_pairs={{0,4},{4,0},{1,5},{5,1},{2,6},{6,2},{3,7},{7,3},{8,12},{12,8},{9,1... | collective-permute-start | bytes 540680 | tf_op jit(solution)/shard_map/ppermute | solution.py:328
  23.6 0.7 copy-start.1
  28.7 23.3 %all-to-all-start = ((f32[64,1,1408]{2,1,0:T(1,128)}), f32[64,1,1408]{2,1,0:T(1,128)S(1)}, u32[]{:S(2)}, u32[]{:S(2)}) async-start(f32[64,1,1408]{2,1,0:T(1,128)} %bitcast.2), calls=%async_computation | async-start | bytes 720896 | tf_op jit(solution)/shard_map/all_to_all | solution.py:382
  37.5 59.1 %copy-start = (f32[16,1024]{1,0:T(8,128)S(1)}, f32[16,1024]{1,0:T(8,128)}, u32[]{:S(2)}) copy-start(f32[16,1024]{1,0:T(8,128)} %get-tuple-element.29.obs_ref) | copy-start | bytes 196612
  37.5 10.7 %collective-permute-start.3 = (f32[160,128]{1,0:T(8,128)S(1)}, f32[160,128]{1,0:T(8,128)S(1)}, u32[]{:S(2)}, u32[]{:S(2)}) collective-permute-start(f32[160,128]{1,0:T(8,128)S(1)} %get-tuple-element.25.state_ref), channel_id=1, source_target_pairs={{0,1},{1,2},{2,3},{3,0},{4,5},{5,6},{6,7},{7,4},{8,9},{9,10},{10,1... | collective-permute-start | bytes 245768 | tf_op jit(solution)/shard_map/ppermute | solution.py:336
  40.8 7.4 %collective-permute-start.4 = (f32[160,128]{1,0:T(8,128)S(1)}, f32[160,128]{1,0:T(8,128)S(1)}, u32[]{:S(2)}, u32[]{:S(2)}) collective-permute-start(f32[160,128]{1,0:T(8,128)S(1)} %get-tuple-element.25.state_ref), channel_id=1, source_target_pairs={{0,2},{1,3},{2,0},{3,1},{4,6},{5,7},{6,4},{7,5},{8,10},{9,11},{10,... | collective-permute-start | bytes 245768 | tf_op jit(solution)/shard_map/ppermute | solution.py:336
  45.1 5.5 %collective-permute-start.5 = (f32[160,128]{1,0:T(8,128)S(1)}, f32[160,128]{1,0:T(8,128)S(1)}, u32[]{:S(2)}, u32[]{:S(2)}) collective-permute-start(f32[160,128]{1,0:T(8,128)S(1)} %get-tuple-element.25.state_ref), channel_id=1, source_target_pairs={{0,3},{1,0},{2,1},{3,2},{4,7},{5,4},{6,5},{7,6},{8,11},{9,8},{10,9... | collective-permute-start | bytes 245768 | tf_op jit(solution)/shard_map/ppermute | solution.py:336
  52.9 35.0 %all-to-all-start.1 = ((f32[256,1,640]{2,1,0:T(1,128)}), f32[256,1,640]{2,1,0:T(1,128)S(1)}, u32[]{:S(2)}, u32[]{:S(2)}) async-start(f32[256,1,640]{2,1,0:T(1,128)} %bitcast.4), calls=%async_computation.1 | async-start | bytes 1310720 | tf_op jit(solution)/shard_map/all_to_all | solution.py:402
  69.1 9.8 %collective-permute-start.6 = (f32[384,128]{1,0:T(8,128)S(1)}, f32[384,128]{1,0:T(8,128)S(1)}, u32[]{:S(2)}, u32[]{:S(2)}) collective-permute-start(f32[384,128]{1,0:T(8,128)S(1)} %weights.1), channel_id=1, source_target_pairs={{0,1},{1,2},{2,3},{3,0},{4,5},{5,6},{6,7},{7,4},{8,9},{9,10},{10,1... | collective-permute-start | bytes 589832 | tf_op jit(solution)/shard_map/ppermute | solution.py:336
  71.0 16.0 %collective-permute-start.7 = (f32[384,128]{1,0:T(8,128)S(1)}, f32[384,128]{1,0:T(8,128)S(1)}, u32[]{:S(2)}, u32[]{:S(2)}) collective-permute-start(f32[384,128]{1,0:T(8,128)S(1)} %weights.1), channel_id=1, source_target_pairs={{0,2},{1,3},{2,0},{3,1},{4,6},{5,7},{6,4},{7,5},{8,10},{9,11},{10,... | collective-permute-start | bytes 589832 | tf_op jit(solution)/shard_map/ppermute | solution.py:336
  76.2 11.6 %collective-permute-start.8 = (f32[384,128]{1,0:T(8,128)S(1)}, f32[384,128]{1,0:T(8,128)S(1)}, u32[]{:S(2)}, u32[]{:S(2)}) collective-permute-start(f32[384,128]{1,0:T(8,128)S(1)} %weights.1), channel_id=1, source_target_pairs={{0,3},{1,0},{2,1},{3,2},{4,7},{5,4},{6,5},{7,6},{8,11},{9,8},{10,9... | collective-permute-start | bytes 589832 | tf_op jit(solution)/shard_map/ppermute | solution.py:336
  87.9 8.8 %collective-permute-start.10 = (f32[1536,128]{1,0:T(8,128)S(1)}, f32[1536,128]{1,0:T(8,128)S(1)}, u32[]{:S(2)}, u32[]{:S(2)}) collective-permute-start(f32[1536,128]{1,0:T(8,128)S(1)} %pad_maximum_fusion.own_ref), channel_id=1, source_target_pairs={{0,4},{4,0},{1,5},{5,1},{2,6},{6,2},{3,7},{7,3},{8,12},{12,8},{9,1... | collective-permute-start | bytes 2359304 | tf_op jit(solution)/shard_map/ppermute | solution.py:328
  94.7 4.0 %collective-permute-start.9 = (f32[1280,128]{1,0:T(8,128)S(1)}, f32[1280,128]{1,0:T(8,128)S(1)}, u32[]{:S(2)}, u32[]{:S(2)}) collective-permute-start(f32[1280,128]{1,0:T(8,128)S(1)} %bitcast.11), channel_id=1, source_target_pairs={{0,4},{4,0},{1,5},{5,1},{2,6},{6,2},{3,7},{7,3},{8,12},{12,8},{9,1... | collective-permute-start | bytes 1966088 | tf_op jit(solution)/shard_map/ppermute | solution.py:328
